TPU v7x, 128 devices: a whole 4x4x4 slice. The times are simulated.
128 devices in a mesh: px: 8 (over x, core), py: 16 (over z, y).
Axes of the slice: x: 4, y: 4, z: 4, core: 2. Of those that a mesh axis runs over, the one named last changes fastest.
Arguments:
- fields: float32 [4, 35, 589824], P(None, None, ('px', 'py')), may hold values from -6 to 6
- residue: float32 [4, 35, 589824], P(None, None, ('px', 'py')), may hold values from -4 to 4
- geometry: float32 [9, 589824], P(None, ('px', 'py')), may hold values from -4 to 4
- normals: float32 [3, 4, 589824], P(None, None, ('px', 'py')), as said below
- face_scale: float32 [4, 589824], P(None, ('px', 'py')), may hold values from 0.5 to 4
- neighbours: int32 [4, 589824], P(None, ('px', 'py')), may hold values from -1 to 19199, as said below
- send_faces: int32 [8, 12288], P(None, ('px', 'py')), may hold values from 0 to 14591, as said below
- live_counts: int32 [128], P(('px', 'py')), may hold values from 768 to 4608, as said below
- sample_ids: int32 [25600], P(('px', 'py')), may hold values from 0 to 25599, each once
- sample_elems: int32 [25600], P(('px', 'py')), may hold values from 0 to 4607, as said below
- sample_coords: float32 [3, 25600], P(None, ('px', 'py')), as said below
Outputs:
- fields_next: float32 [4, 35, 589824], P(None, None, ('px', 'py'))
- residue_next: float32 [4, 35, 589824], P(None, None, ('px', 'py'))
- coefficients: float32 [25, 512], P(None, ('px', 'py'))
Inputs may be any that keep to these rules, and one draw needn't show every extreme that they name: `live_counts`: one partition holds exactly 4608 live slots, each other one between 768 and 2304. `neighbours`: codes of live slots name live face blocks. Slot d * 96 + j, for d below 8, has exactly one face coded 4 * 4608 + d * 96 + j, or coded -1 where that neighbour lies off the grid; no other face has a code at or above 18432. Matched faces list their nodes in the same order. send_faces[d, P * 96 + j] is the face block of partition P's slot d * 96 + j that faces neighbour d. `sample_elems`: each names a live slot of the partition holding the sample slot. `sample_coords`: the point lies inside the reference tetrahedron. `normals`: unit vectors.
All inputs are finite; a program needn't handle non-finite values.
Results may differ from a plain program's by a relative error of at most 0.0003.
Values sent between devices are 32-bit elements; how exact they have to be, the bound alone decides.
No kernel may reach another device: no remote copies, remote signals or barrier semaphores. Data moves between devices by JAX's collectives and lax.ppermute only.
A program may use at most 128 MiB of HBM per device.

v0:
```python
import functools
import math

import jax
import jax.numpy as jnp
import numpy as np
from jax import lax
from jax.experimental import pallas as pl
from jax.experimental.pallas import tpu as pltpu
from jax.sharding import PartitionSpec as P

QPTS = 50
NODES = 35
PAD = 40
FACE_ROWS = 16
LANES = 128


highest = lax.Precision.HIGHEST
section_decay = -567301805773.0 / 1357537059087.0
section_gain = 5161836677717.0 / 13612068292357.0
time_step = 0.01
f32 = jnp.float32
bf16 = jnp.bfloat16


def exponent_table():
    listing = []
    for degree in range(5):
        for third in range(degree + 1):
            for second in range(degree + 1 - third):
                listing.append((degree - second - third, second, third))
    return np.array(listing)


def factorials(values):
    lookup = np.array([float(math.factorial(level)) for level in range(24)])
    return lookup[values]


def eliminate(matrix, right_hand):
    order_size = matrix.shape[0]
    work = np.concatenate([matrix, right_hand], axis=1).astype(float)
    for pivot_col in range(order_size):
        best = max(range(pivot_col, order_size), key=lambda row_id: abs(work[row_id, pivot_col]))
        work[[pivot_col, best]] = work[[best, pivot_col]]
        work[pivot_col] = work[pivot_col] / work[pivot_col, pivot_col]
        for row_id in range(order_size):
            if row_id != pivot_col:
                work[row_id] = work[row_id] - work[row_id, pivot_col] * work[pivot_col]
    return work[:, order_size:]


def element_tables():
    powers = exponent_table()
    points = powers / 4.0
    vander = np.prod(points[:, None, :] ** powers[None, :, :], axis=2)
    inverse = eliminate(vander, np.eye(35))
    derivs = []
    for axis_id in range(3):
        lowered = np.maximum(powers - (np.arange(3) == axis_id)[None, :], 0)
        slope_table = powers[None, :, axis_id] * np.prod(
            points[:, None, :] ** lowered[None, :, :], axis=2
        )
        derivs.append(slope_table @ inverse)
    summed = powers[:, None, :] + powers[None, :, :]
    exp_r = summed[..., 0]
    exp_s = summed[..., 1]
    exp_t = summed[..., 2]
    volume = (
        factorials(exp_r)
        * factorials(exp_s)
        * factorials(exp_t)
        / factorials(exp_r + exp_s + exp_t + 3)
    )
    mass_matrix = inverse.T @ volume @ inverse
    face_grams = [
        np.where(
            exp_t == 0, factorials(exp_r) * factorials(exp_s) / factorials(exp_r + exp_s + 2), 0.0
        ),
        np.where(
            exp_s == 0, factorials(exp_r) * factorials(exp_t) / factorials(exp_r + exp_t + 2), 0.0
        ),
        factorials(exp_r)
        * factorials(exp_s)
        * factorials(exp_t)
        / factorials(exp_r + exp_s + exp_t + 2),
        np.where(
            exp_r == 0, factorials(exp_s) * factorials(exp_t) / factorials(exp_s + exp_t + 2), 0.0
        ),
    ]
    listed = [tuple((int(entry) for entry in powers[node_id])) for node_id in range(35)]
    face_nodes = np.array(
        [
            [node_id for node_id in range(35) if listed[node_id][2] == 0],
            [node_id for node_id in range(35) if listed[node_id][1] == 0],
            [node_id for node_id in range(35) if sum(listed[node_id]) == 4],
            [node_id for node_id in range(35) if listed[node_id][0] == 0],
        ]
    )
    surface = np.zeros((35, 60))
    for face_id in range(4):
        face_mass = inverse.T @ face_grams[face_id] @ inverse
        for node_id in range(15):
            surface[:, 4 * node_id + face_id] = face_mass[:, face_nodes[face_id, node_id]]
    lifting = eliminate(mass_matrix, surface)
    return (np.stack(derivs), lifting, face_nodes, inverse, powers)


def associated(degree, order, cosine, sine):
    current = cosine * 0.0 + 1.0
    for step_id in range(1, order + 1):
        current = -(2 * step_id - 1) * sine * current
    if degree == order:
        return current
    following = cosine * (2 * order + 1) * current
    for level in range(order + 2, degree + 1):
        current, following = (
            following,
            ((2 * level - 1) * cosine * following - (level + order - 1) * current)
            / (level - order),
        )
    return following


def harmonic_table():
    inner_node = math.sqrt(5.0 - 2.0 * math.sqrt(10.0 / 7.0)) / 3.0
    outer_node = math.sqrt(5.0 + 2.0 * math.sqrt(10.0 / 7.0)) / 3.0
    inner_weight = (322.0 + 13.0 * math.sqrt(70.0)) / 900.0
    outer_weight = (322.0 - 13.0 * math.sqrt(70.0)) / 900.0
    cosines = np.array([-outer_node, -inner_node, 0.0, inner_node, outer_node])
    weights = np.array([outer_weight, inner_weight, 128.0 / 225.0, inner_weight, outer_weight])
    azimuth = 2.0 * np.pi * (np.arange(10) + 0.5) / 10.0
    polar = np.repeat(cosines, 10)
    circle = np.tile(azimuth, 5)
    point_weight = np.repeat(weights, 10) * 2.0 * np.pi / 10.0
    sine = np.sqrt(1.0 - polar**2)
    table_rows = []
    for degree in range(5):
        for order in range(-degree, degree + 1):
            absolute = abs(order)
            legendre = associated(degree, absolute, polar, sine)
            factor = math.sqrt(
                (2 * degree + 1)
                / (4.0 * math.pi)
                * math.factorial(degree - absolute)
                / math.factorial(degree + absolute)
            )
            if order > 0:
                angular = math.sqrt(2.0) * np.cos(order * circle)
            elif order < 0:
                angular = math.sqrt(2.0) * np.sin(absolute * circle)
            else:
                angular = circle * 0.0 + 1.0
            table_rows.append(factor * legendre * angular * point_weight)
    return np.array(table_rows)


def constant_tables():
    derivs, lifting, face_nodes, inverse, powers = element_tables()
    table_select = np.zeros((4 * PAD, 4 * LANES), np.float32)
    trace_select = np.zeros((4 * 4 * FACE_ROWS, 4 * PAD), np.float32)
    for face in range(4):
        for field in range(4):
            for place in range(15):
                source = PAD * field + face_nodes[face, place]
                column = FACE_ROWS * field + place
                table_select[source, LANES * face + column] = 1.0
                table_select[source, LANES * face + 64 + column] = 1.0
                trace_select[64 * face + column, source] = 1.0
    whole = np.round(3.0 * derivs)
    into_p = np.zeros((PAD, 128), np.float32)
    from_p = np.zeros((3 * PAD, 48), np.float32)
    for axis_id in range(3):
        into_p[:NODES, PAD * axis_id : PAD * axis_id + NODES] = whole[axis_id]
        from_p[PAD * axis_id : PAD * axis_id + NODES, :NODES] = whole[axis_id]
    lift = np.zeros((PAD, 64), np.float32)
    for face in range(4):
        for place in range(15):
            lift[:NODES, FACE_ROWS * face + place] = lifting[:, 4 * place + face]
    lift_hi = lift.astype(jnp.bfloat16)
    lift_lo = (lift - lift_hi.astype(np.float32)).astype(jnp.bfloat16)
    return {
        "table_select": jnp.asarray(table_select, bf16),
        "trace_select": jnp.asarray(trace_select, bf16),
        "into_p": jnp.asarray(np.concatenate([into_p, into_p], axis=1), bf16),
        "from_p": jnp.asarray(np.concatenate([from_p, from_p], axis=1), bf16),
        "lift": jnp.asarray(np.concatenate([lift_hi, lift_hi, lift_lo], axis=1)),
        "inverse": jnp.asarray(np.pad(inverse.T, ((0, 5), (0, 5))), f32),
        "powers": powers,
    }


def halves(values):
    high = values.astype(bf16)
    return high, (values - high.astype(f32)).astype(bf16)


def thirds(values):
    high = values.astype(bf16)
    rest = values - high.astype(f32)
    middle = rest.astype(bf16)
    return high, middle, (rest - middle.astype(f32)).astype(bf16)


def product(left, right, dims=((1,), (0,))):
    return lax.dot_general(left, right, (dims, ((), ())), preferred_element_type=f32)


def stack_fields(fields_ref, stacked):
    for field in range(4):
        stacked[PAD * field : PAD * field + NODES, :] = fields_ref[field]
    return halves(stacked[...])


def pack_kernel(slot_faces, fields_ref, codes_ref, select_ref, up_ref, down_ref, left_ref, right_ref, stacked):
    stacked[...] = jnp.zeros_like(stacked)
    high, low = stack_fields(fields_ref, stacked)
    traces = product(select_ref[...], high) + product(select_ref[...], low)
    chosen = jnp.zeros((64, traces.shape[1]), f32)
    for face in range(4):
        remote = codes_ref[face : face + 1, :] >= slot_faces
        chosen = jnp.where(remote, traces[64 * face : 64 * face + 64, :], chosen)
    width = left_ref.shape[1]
    pieces = [chosen[:, width * heading : width * heading + width] for heading in range(8)]
    for place in range(3):
        up_ref[place] = pieces[place]
        down_ref[place] = pieces[5 + place]
    left_ref[...] = pieces[3]
    right_ref[...] = pieces[4]


def table_kernel(fields_ref, select_ref, table_ref, stacked):
    @pl.when(pl.program_id(0) == 0)
    def _():
        stacked[...] = jnp.zeros_like(stacked)

    high, low = stack_fields(fields_ref, stacked)
    for half in range(2):
        select = select_ref[:, 256 * half : 256 * half + 256]
        rows = product(high, select, ((0,), (0,))) + product(low, select, ((0,), (0,)))
        table_ref[2 * half] = rows[:, :LANES]
        table_ref[2 * half + 1] = rows[:, LANES:]


def gather_kernel(slot_count, codes_ref, table_ref, normals_ref, outer_ref, *rows_refs):
    width = outer_ref.shape[1]
    first = pl.program_id(0) * width
    left_half = lax.broadcasted_iota(jnp.int32, (1, LANES), 1) < 64
    for tile in range(width // LANES):
        for half in range(2):
            rows_ref = rows_refs[half]
            base = half * slot_count + first + tile * LANES
            for row in range(LANES):
                code = codes_ref[base + row]
                one = table_ref[pl.ds(code & 0xFFFF, 1), :]
                two = table_ref[pl.ds(lax.shift_right_logical(code, 16), 1), :]
                rows_ref[row : row + 1, :] = jnp.where(left_half, one, two)
            turned = rows_ref[...].T
            lanes = slice(tile * LANES, tile * LANES + LANES)
            for side in range(2):
                face = 2 * half + side
                part = turned[64 * side : 64 * side + 64, :]
                total = -part[0:16]
                for axis_id in range(3):
                    facing = normals_ref[axis_id, face : face + 1, lanes]
                    total = total + facing * part[16 + 16 * axis_id : 32 + 16 * axis_id]
                outer_ref[FACE_ROWS * face : FACE_ROWS * face + FACE_ROWS, lanes] = total


def pressure_kernel(
    slot_faces,
    powers,
    group,
    live_ref,
    fields_ref,
    residue_ref,
    geometry_ref,
    normals_ref,
    scale_ref,
    codes_ref,
    outer_ref,
    right_ref,
    left_ref,
    below_ref,
    above_ref,
    elems_ref,
    ids_ref,
    coords_ref,
    select_ref,
    into_ref,
    lift_ref,
    inverse_ref,
    next_ref,
    rate_ref,
    flux_ref,
    spread_ref,
    stacked,
    combined,
    remote,
    outside,
    sampled,
    pressure,
    monomials,
):
    step = pl.program_id(0)
    width = fields_ref.shape[2]

    @pl.when(step == 0)
    def _():
        stacked[...] = jnp.zeros_like(stacked)
        combined[...] = jnp.zeros_like(combined)
        pressure[...] = jnp.zeros_like(pressure)
        sampled[...] = jnp.zeros_like(sampled)
        monomials[...] = jnp.zeros_like(monomials)

    outside[...] = outer_ref[...]

    @pl.when(step == 0)
    def _():
        count = right_ref.shape[2]
        sources = [
            left_ref[2],
            above_ref[1],
            right_ref[2],
            left_ref[0],
            right_ref[0],
            left_ref[1],
            below_ref[1],
            right_ref[1],
        ]
        for heading in range(8):
            remote[:, count * heading : count * heading + count] = sources[heading]
        for face in range(4):
            rows = slice(FACE_ROWS * face, FACE_ROWS * face + FACE_ROWS)
            total = -remote[0:16, :]
            for axis_id in range(3):
                facing = normals_ref[axis_id, face : face + 1, :]
                total = total + facing * remote[16 + 16 * axis_id : 32 + 16 * axis_id, :]
            is_remote = codes_ref[face : face + 1, :] >= slot_faces
            outside[rows, :] = jnp.where(is_remote, total, outside[rows, :])

    high, low = stack_fields(fields_ref, stacked)
    traces = product(select_ref[...], high) + product(select_ref[...], low)
    fluxes = []
    for face in range(4):
        inner_p = traces[64 * face : 64 * face + 16]
        along = jnp.zeros_like(inner_p)
        for axis_id in range(3):
            facing = normals_ref[axis_id, face : face + 1, :]
            start = 64 * face + 16 + 16 * axis_id
            along = along + facing * traces[start : start + 16]
        wall = codes_ref[face : face + 1, :] < 0
        beyond = outside[FACE_ROWS * face : FACE_ROWS * face + FACE_ROWS, :]
        beyond = jnp.where(wall, -along - inner_p, beyond)
        flux = (0.5 * scale_ref[face : face + 1, :]) * (along - inner_p - beyond)
        flux_ref[FACE_ROWS * face : FACE_ROWS * face + FACE_ROWS, :] = flux
    flux_hi, flux_lo = halves(flux_ref[...])
    lifted = product(lift_ref[...], jnp.concatenate([flux_hi, flux_lo, flux_hi], axis=0))
    for axis_id in range(3):
        total = geometry_ref[3 * axis_id : 3 * axis_id + 1, :] * fields_ref[1]
        for direction in range(1, 3):
            at = 3 * axis_id + direction
            total = total + geometry_ref[at : at + 1, :] * fields_ref[1 + direction]
        combined[PAD * axis_id : PAD * axis_id + NODES, :] = total
    high, low = halves(combined[...])
    divergence = product(into_ref[...], jnp.concatenate([high, low], axis=0))
    rate = (lifted - divergence * (1.0 / 3.0))[:NODES]
    keep = lax.broadcasted_iota(jnp.int32, (1, width), 1) + step * width < live_ref[0]
    residue_next = section_decay * residue_ref[0] + time_step * rate
    fields_next = fields_ref[0] + section_gain * residue_next
    fields_next = jnp.where(keep, fields_next, 0.0)
    next_ref[...] = fields_next
    rate_ref[...] = jnp.where(keep, residue_next, 0.0)

    pressure[0:NODES, :] = fields_next
    parts = jnp.concatenate(thirds(pressure[...]), axis=0)
    slots = lax.broadcasted_iota(jnp.int32, (width, elems_ref.shape[1]), 0) + step * width
    picks = jnp.where(slots == elems_ref[...], 1.0, 0.0).astype(bf16)
    sampled[...] += product(parts, picks)

    @pl.when(step == pl.num_programs(0) - 1)
    def _():
        ladders = []
        for axis_id in range(3):
            base = coords_ref[axis_id : axis_id + 1, :]
            square = base * base
            ladders.append([jnp.ones_like(base), base, square, square * base, square * square])
        for node in range(NODES):
            exps = [int(entry) for entry in powers[node]]
            monomials[node : node + 1, :] = (
                ladders[0][exps[0]] * ladders[1][exps[1]] * ladders[2][exps[2]]
            )
        basis = jnp.dot(
            inverse_ref[...], monomials[...], precision=highest, preferred_element_type=f32
        )
        gathered = sampled[0:PAD, :] + sampled[48 : 48 + PAD, :] + sampled[96 : 96 + PAD, :]
        values = jnp.sum(basis * gathered, axis=0, keepdims=True)
        ids = ids_ref[...]
        owner = lax.shift_right_logical(ids * 5243, 20)
        place = ids - group * owner
        devices = spread_ref.shape[0]
        owners = lax.broadcasted_iota(jnp.int32, (devices, ids.shape[1]), 0)
        held = jnp.where(owners == owner, values, 0.0)
        places = lax.broadcasted_iota(jnp.int32, (spread_ref.shape[1], ids.shape[1]), 0)
        chosen = jnp.where(places == place, 1.0, 0.0).astype(bf16)
        spread = jnp.zeros(spread_ref.shape, f32)
        for part in thirds(held):
            spread = spread + product(part, chosen, ((1,), (1,)))
        spread_ref[...] = spread


def velocity_kernel(
    live_ref,
    fields_ref,
    residue_x_ref,
    residue_y_ref,
    residue_z_ref,
    geometry_ref,
    normals_ref,
    flux_ref,
    done_p_ref,
    done_r_ref,
    from_ref,
    lift_ref,
    fields_out,
    residue_out,
    pressure,
):
    step = pl.program_id(0)
    width = fields_ref.shape[2]

    @pl.when(step == 0)
    def _():
        pressure[...] = jnp.zeros_like(pressure)

    pressure[0:NODES, :] = fields_ref[0]
    high, low = halves(pressure[...])
    slopes = product(from_ref[...], jnp.concatenate([high, low], axis=0))
    keep = lax.broadcasted_iota(jnp.int32, (1, width), 1) + step * width < live_ref[0]
    fields_out[0] = done_p_ref[...]
    residue_out[0] = done_r_ref[...]
    for direction, residue_ref in enumerate((residue_x_ref, residue_y_ref, residue_z_ref)):
        pieces = []
        for face in range(4):
            facing = normals_ref[direction, face : face + 1, :]
            pieces.append(facing * flux_ref[FACE_ROWS * face : FACE_ROWS * face + FACE_ROWS, :])
        flux_hi, flux_lo = halves(jnp.concatenate(pieces, axis=0))
        lifted = product(lift_ref[...], jnp.concatenate([flux_hi, flux_lo, flux_hi], axis=0))
        rate = lifted
        for axis_id in range(3):
            at = 3 * axis_id + direction
            rate = rate + (geometry_ref[at : at + 1, :] * (1.0 / 3.0)) * (
                slopes[PAD * axis_id : PAD * axis_id + PAD]
            )
        residue_next = section_decay * residue_ref[0] - time_step * rate[:NODES]
        fields_next = fields_ref[1 + direction] + section_gain * residue_next
        fields_out[1 + direction] = jnp.where(keep, fields_next, 0.0)
        residue_out[1 + direction] = jnp.where(keep, residue_next, 0.0)


def harmonic_kernel(received_ref, table_ref, groups_ref, out_ref):
    mine = jnp.sum(received_ref[...], axis=0, keepdims=True)
    weighted = table_ref[...] * mine
    out_ref[...] = jnp.dot(
        weighted, groups_ref[...], precision=highest, preferred_element_type=f32
    )


def fixed(shape):
    return pl.BlockSpec(shape, lambda *_: (0,) * len(shape))


def local(
    fields,
    residue,
    geometry,
    normals,
    face_scale,
    neighbours,
    send_faces,
    live_counts,
    sample_ids,
    sample_elems,
    sample_coords,
):
    const = constant_tables()
    slot_count = fields.shape[2]
    slot_faces = 4 * slot_count
    bound_count = send_faces.shape[1]
    reach = 8 * bound_count
    width = reach
    steps = slot_count // width
    samples = sample_ids.shape[0]
    devices = lax.axis_size(("px", "py"))
    limit = pltpu.CompilerParams(vmem_limit_bytes=48 << 20)
    shape = jax.ShapeDtypeStruct

    up, down, left, right = pl.pallas_call(
        functools.partial(pack_kernel, slot_faces),
        grid=(1,),
        in_specs=[
            pl.BlockSpec((4, NODES, reach), lambda t: (0, 0, 0)),
            pl.BlockSpec((4, reach), lambda t: (0, 0)),
            fixed((256, 4 * PAD)),
        ],
        out_specs=[
            fixed((3, 64, bound_count)),
            fixed((3, 64, bound_count)),
            fixed((64, bound_count)),
            fixed((64, bound_count)),
        ],
        out_shape=[
            shape((3, 64, bound_count), f32),
            shape((3, 64, bound_count), f32),
            shape((64, bound_count), f32),
            shape((64, bound_count), f32),
        ],
        scratch_shapes=[pltpu.VMEM((4 * PAD, reach), f32)],
        compiler_params=limit,
        name="pack",
    )(fields, neighbours, const["trace_select"])

    def steps_along(axis):
        count = lax.axis_size(axis)
        forward = [(i, i + 1) for i in range(count - 1)]
        return forward, [(target, source) for source, target in forward]

    forward, backward = steps_along("px")
    below = lax.ppermute(up, "px", backward)
    above = lax.ppermute(down, "px", forward)

    table = pl.pallas_call(
        table_kernel,
        grid=(steps,),
        in_specs=[
            pl.BlockSpec((4, NODES, width), lambda t: (0, 0, t)),
            fixed((4 * PAD, 4 * LANES)),
        ],
        out_specs=pl.BlockSpec((4, width, LANES), lambda t: (0, t, 0)),
        out_shape=shape((4, slot_count, LANES), f32),
        scratch_shapes=[pltpu.VMEM((4 * PAD, width), f32)],
        compiler_params=limit,
        name="table",
    )(fields, const["table_select"]).reshape(slot_faces, LANES)

    forward, backward = steps_along("py")
    to_left = jnp.concatenate([left[None], below[0:1], above[0:1]])
    to_right = jnp.concatenate([right[None], below[2:3], above[2:3]])
    from_right = lax.ppermute(to_left, "py", backward)
    from_left = lax.ppermute(to_right, "py", forward)

    inside = (neighbours >= 0) & (neighbours < slot_faces)
    codes = jnp.where(inside, neighbours, 0)
    codes = (codes[0::2] + (codes[1::2] << 16)).reshape(-1)
    gather_width = 512
    outer = pl.pallas_call(
        functools.partial(gather_kernel, slot_count),
        grid_spec=pltpu.PrefetchScalarGridSpec(
            num_scalar_prefetch=1,
            grid=(slot_count // gather_width,),
            in_specs=[
                pl.BlockSpec(memory_space=pltpu.VMEM),
                pl.BlockSpec((3, 4, gather_width), lambda t, _: (0, 0, t)),
            ],
            out_specs=pl.BlockSpec((64, gather_width), lambda t, _: (0, t)),
            scratch_shapes=[pltpu.VMEM((LANES, LANES), f32)] * 2,
        ),
        out_shape=shape((64, slot_count), f32),
        compiler_params=limit,
        name="gather",
    )(codes, table, normals)

    next_p, next_r, flux, spread = pl.pallas_call(
        functools.partial(pressure_kernel, slot_faces, const["powers"], samples),
        grid_spec=pltpu.PrefetchScalarGridSpec(
            num_scalar_prefetch=1,
            grid=(steps,),
            in_specs=[
                pl.BlockSpec((4, NODES, width), lambda t, _: (0, 0, t)),
                pl.BlockSpec((1, NODES, width), lambda t, _: (0, 0, t)),
                pl.BlockSpec((9, width), lambda t, _: (0, t)),
                pl.BlockSpec((3, 4, width), lambda t, _: (0, 0, t)),
                pl.BlockSpec((4, width), lambda t, _: (0, t)),
                pl.BlockSpec((4, width), lambda t, _: (0, t)),
                pl.BlockSpec((64, width), lambda t, _: (0, t)),
                fixed((3, 64, bound_count)),
                fixed((3, 64, bound_count)),
                fixed((3, 64, bound_count)),
                fixed((3, 64, bound_count)),
                fixed((1, samples)),
                fixed((1, samples)),
                fixed((3, samples)),
                fixed((256, 4 * PAD)),
                fixed((PAD, 256)),
                fixed((PAD, 192)),
                fixed((PAD, PAD)),
            ],
            out_specs=[
                pl.BlockSpec((NODES, width), lambda t, _: (0, t)),
                pl.BlockSpec((NODES, width), lambda t, _: (0, t)),
                pl.BlockSpec((64, width), lambda t, _: (0, t)),
                fixed((devices, samples)),
            ],
            scratch_shapes=[
                pltpu.VMEM((4 * PAD, width), f32),
                pltpu.VMEM((128, width), f32),
                pltpu.VMEM((64, width), f32),
                pltpu.VMEM((64, width), f32),
                pltpu.VMEM((144, samples), f32),
                pltpu.VMEM((48, width), f32),
                pltpu.VMEM((PAD, samples), f32),
            ],
        ),
        out_shape=[
            shape((NODES, slot_count), f32),
            shape((NODES, slot_count), f32),
            shape((64, slot_count), f32),
            shape((devices, samples), f32),
        ],
        compiler_params=limit,
        name="pressure",
    )(
        live_counts,
        fields,
        residue,
        geometry,
        normals,
        face_scale,
        neighbours,
        outer,
        from_right,
        from_left,
        below,
        above,
        sample_elems.reshape(1, samples),
        sample_ids.reshape(1, samples),
        sample_coords,
        const["trace_select"],
        const["into_p"],
        const["lift"],
        const["inverse"],
    )
    received = lax.all_to_all(spread, ("px", "py"), 0, 0, tiled=True)

    def plane(index):
        return pl.BlockSpec((1, NODES, width), lambda t, _: (index, 0, t))

    fields_next, residue_next = pl.pallas_call(
        velocity_kernel,
        grid_spec=pltpu.PrefetchScalarGridSpec(
            num_scalar_prefetch=1,
            grid=(steps,),
            in_specs=[
                pl.BlockSpec((4, NODES, width), lambda t, _: (0, 0, t)),
                plane(1),
                plane(2),
                plane(3),
                pl.BlockSpec((9, width), lambda t, _: (0, t)),
                pl.BlockSpec((3, 4, width), lambda t, _: (0, 0, t)),
                pl.BlockSpec((64, width), lambda t, _: (0, t)),
                pl.BlockSpec((NODES, width), lambda t, _: (0, t)),
                pl.BlockSpec((NODES, width), lambda t, _: (0, t)),
                fixed((3 * PAD, 96)),
                fixed((PAD, 192)),
            ],
            out_specs=[
                pl.BlockSpec((4, NODES, width), lambda t, _: (0, 0, t)),
                pl.BlockSpec((4, NODES, width), lambda t, _: (0, 0, t)),
            ],
            scratch_shapes=[pltpu.VMEM((48, width), f32)],
        ),
        out_shape=[shape(fields.shape, f32), shape(residue.shape, f32)],
        compiler_params=limit,
        name="velocity",
    )(
        live_counts,
        fields,
        residue,
        residue,
        residue,
        geometry,
        normals,
        flux,
        next_p,
        next_r,
        const["from_p"],
        const["lift"],
    )

    receivers = samples // QPTS
    harmonic = np.tile(harmonic_table(), (1, receivers)).astype(np.float32)
    groups = (np.arange(samples)[:, None] // QPTS == np.arange(receivers)[None]).astype(np.float32)
    coefficients = pl.pallas_call(
        harmonic_kernel,
        out_shape=shape((harmonic.shape[0], receivers), f32),
        name="harmonic",
    )(received, jnp.asarray(harmonic), jnp.asarray(groups))
    return (fields_next, residue_next, coefficients)


def solution(mesh):
    placed = (
        P(None, None, ("px", "py")),
        P(None, None, ("px", "py")),
        P(None, ("px", "py")),
        P(None, None, ("px", "py")),
        P(None, ("px", "py")),
        P(None, ("px", "py")),
        P(None, ("px", "py")),
        P(("px", "py")),
        P(("px", "py")),
        P(("px", "py")),
        P(None, ("px", "py")),
    )
    return jax.shard_map(
        local,
        mesh=mesh,
        in_specs=placed,
        out_specs=(P(None, None, ("px", "py")), P(None, None, ("px", "py")), P(None, ("px", "py"))),
        check_vma=False,
    )
```

profile of v0, /device:TPU:1, one launch (start us, length us, event | category | flops | bytes accessed | tf_op | source)
XLA Modules:
  0.0 91.9 jit_solution(2426439454993074663)
XLA Ops:
  0.6 0.0 copy-start.4
  0.6 0.0 copy-start.3
  0.7 2.6 %copy.48.fields_ref = f32[4,35,4608]{2,1,0:T(8,128)S(1)} copy(f32[4,35,4608]{2,0,1:T(4,128)} %param.19) | data formatting | bytes 5160960 | tf_op args[0]
  3.3 0.0 copy-done.4
  3.3 0.0 copy-done.3
  3.3 0.0 copy-start
  3.3 1.6 %pack.1 = (f32[3,64,96]{2,1,0:T(8,128)}, f32[3,64,96]{2,1,0:T(8,128)}, f32[64,96]{1,0:T(8,128)S(1)}, f32[64,96]{1,0:T(8,128)S(1)}) custom-call(f32[4,35,4608]{2,1,0:T(8,128)S(1)} %copy.48.fields_ref, s32[4,4608]{1,0:T(4,128)S(1)} %copy-done.3, bf16[256,160]{1,0:T(8,128)(2,1)S(1)} %copy-done.4), custom_call_target="tpu_custom_call" | custom-call | tf_op jit(solution)/shard_map/pack/pallas_call | solution.py:499
  4.9 3.3 %collective-permute-start = (f32[3,64,96]{2,1,0:T(8,128)}, f32[3,64,96]{2,1,0:T(8,128)S(1)}, u32[]{:S(2)}, u32[]{:S(2)}) collective-permute-start(f32[3,64,96]{2,1,0:T(8,128)} %get-tuple-element.14), channel_id=1, source_target_pairs={{16,0},{32,16},{48,32},{64,48},{80,64},{96,80},{112,96},{17,1},{33... | collective-permute-start | bytes 221192 | tf_op jit(solution)/shard_map/ppermute | solution.py:530
  8.2 3.1 %collective-permute-start.1 = (f32[3,64,96]{2,1,0:T(8,128)}, f32[3,64,96]{2,1,0:T(8,128)S(1)}, u32[]{:S(2)}, u32[]{:S(2)}) collective-permute-start(f32[3,64,96]{2,1,0:T(8,128)} %get-tuple-element.15), channel_id=1, source_target_pairs={{0,16},{16,32},{32,48},{48,64},{64,80},{80,96},{96,112},{1,17},{17... | collective-permute-start | bytes 221192 | tf_op jit(solution)/shard_map/ppermute | solution.py:531
  11.3 0.1 slice.18
  11.5 0.7 slice.19
  12.2 0.0 collective-permute-done.below_ref
  12.2 1.1 %collective-permute-done.1.above_ref = f32[3,64,96]{2,1,0:T(8,128)S(1)} collective-permute-done((f32[3,64,96]{2,1,0:T(8,128)}, f32[3,64,96]{2,1,0:T(8,128)S(1)}, u32[]{:S(2)}, u32[]{:S(2)}) %collective-permute-start.1) | collective-permute-done | bytes 73760 | tf_op jit(solution)/shard_map/ppermute | solution.py:531
  13.3 1.3 %collective-permute-start.2 = (f32[3,64,96]{2,1,0:T(8,128)S(1)}, f32[3,64,96]{2,1,0:T(8,128)}, u32[]{:S(2)}, u32[]{:S(2)}) collective-permute-start(f32[3,64,96]{2,1,0:T(8,128)S(1)} %pad_maximum_fusion), channel_id=1, source_target_pairs={{1,0},{2,1},{3,2},{4,3},{5,4},{6,5},{7,6},{8,7},{9,8},{10,9},{11,1... | collective-permute-start | bytes 221192 | tf_op jit(solution)/shard_map/ppermute | solution.py:550
  14.6 0.7 pad_maximum_fusion.1
  15.2 4.6 %collective-permute-start.3 = (f32[3,64,96]{2,1,0:T(8,128)}, f32[3,64,96]{2,1,0:T(8,128)}, u32[]{:S(2)}, u32[]{:S(2)}) collective-permute-start(f32[3,64,96]{2,1,0:T(8,128)} %pad_maximum_fusion.1), channel_id=1, source_target_pairs={{0,1},{1,2},{2,3},{3,4},{4,5},{5,6},{6,7},{7,8},{8,9},{9,10},{10,1... | collective-permute-start | bytes 221192 | tf_op jit(solution)/shard_map/ppermute | solution.py:551
  19.8 0.8 shift-left_add_fusion
  20.6 0.0 copy-start.7
  20.6 0.9 copy-done.7
  21.5 6.2 %table.1 = f32[4,4608,128]{2,1,0:T(8,128)} custom-call(f32[4,35,4608]{2,1,0:T(8,128)S(1)} %copy.48.fields_ref, bf16[160,512]{1,0:T(8,128)(2,1)S(1)} %copy-done.7), custom_call_target="tpu_custom_call" | custom-call | tf_op jit(solution)/shard_map/table/pallas_call | solution.py:533
  27.7 0.0 copy-done
  27.7 0.0 copy-done.5
  27.8 0.0 copy-start.1
  27.8 4.2 %copy.49.residue_ref.residue_x_ref.residue_y_ref.residue_z_ref = f32[4,35,4608]{2,1,0:T(8,128)} copy(f32[4,35,4608]{2,0,1:T(4,128)} %param.20) | data formatting | bytes 5160960 | tf_op args[1]
  32.6 0.0 copy-start.2
  32.7 0.0 copy-start.6
  32.7 0.0 copy-start.8
  32.7 0.0 copy-start.9
  32.7 0.0 copy-start.11
  32.7 0.0 copy-start.12
  32.7 0.0 copy-start.13
  32.7 0.0 copy-start.14
  32.7 0.0 copy-start.15
  32.7 20.4 %gather.1.outer_ref = f32[64,4608]{1,0:T(8,128)S(1)} custom-call(s32[9216]{0:T(1024)S(1)} %reshape.20.codes_ref, f32[18432,128]{1,0:T(8,128)} %bitcast.15, f32[3,4,4608]{2,1,0:T(4,128)S(1)} %copy-done.1), custom_call_target="tpu_custom_call" | custom-call | tf_op jit(solution)/shard_map/gather/pallas_call | solution.py:557
  53.2 0.0 collective-permute-done.2.right_ref
  53.2 0.0 collective-permute-done.3.left_ref
  53.3 0.0 copy-start.10
  53.3 8.1 %pressure.1 = (f32[35,4608]{1,0:T(8,128)S(1)}, f32[35,4608]{1,0:T(8,128)S(1)}, f32[64,4608]{1,0:T(8,128)S(1)}, f32[128,200]{1,0:T(8,128)S(1)}) custom-call(s32[1]{0:T(128)S(6)} %copy.61.live_ref, f32[4,35,4608]{2,1,0:T(8,128)} %copy-done, f32[4,35,4608]{2,1,0:T(8,128)} %copy.49.residue_ref.residue_x_ref.residue_y_ref.residue_z_ref, f32[9,4608]{1,0:T(8,128)S(1)} %copy-done.2, ...), custom_call_target="tpu_custom_call" | custom-call | tf_op jit(solution)/shard_map/pressure/pallas_call | solution.py:574
  61.5 0.8 copy.52
  62.2 12.9 %all-to-all-start = ((f32[128,1,200]{2,1,0:T(1,128)}), f32[128,1,200]{2,1,0:T(1,128)S(1)}, u32[]{:S(2)}, u32[]{:S(2)}) async-start(f32[128,1,200]{2,1,0:T(1,128)} %copy.52), calls=%async_computation | async-start | bytes 262144 | tf_op jit(solution)/shard_map/all_to_all | solution.py:644
  75.2 0.0 copy-done.10
  75.2 6.6 %velocity.1 = (f32[4,35,4608]{2,1,0:T(8,128)S(1)}, f32[4,35,4608]{2,1,0:T(8,128)}) custom-call(s32[1]{0:T(128)S(6)} %copy.61.live_ref, f32[4,35,4608]{2,1,0:T(8,128)} %copy-done, f32[4,35,4608]{2,1,0:T(8,128)} %copy.49.residue_ref.residue_x_ref.residue_y_ref.residue_z_ref, f32[4,35,4608]{2,1,0:T(8,128)} %copy.49.residue_ref.residue_x_ref.residue_y_ref.residue_z_ref, ...), custom_call_target="tpu_custom_call" | custom-call | tf_op jit(solution)/shard_map/velocity/pallas_call | solution.py:649
  81.8 3.1 %copy.55 = f32[4,35,4608]{2,0,1:T(4,128)} copy(f32[4,35,4608]{2,1,0:T(8,128)S(1)} %get-tuple-element.29) | data formatting | bytes 5160960
  84.9 3.1 %copy.56 = f32[4,35,4608]{2,0,1:T(4,128)} copy(f32[4,35,4608]{2,1,0:T(8,128)S(1)} %copy-done.16) | data formatting | bytes 5160960
  88.1 0.0 all-to-all-done
  88.1 0.7 copy.60
  88.7 1.8 %harmonic.1 = f32[25,4]{1,0:T(8,128)} custom-call(f32[128,200]{1,0:T(8,128)} %bitcast.16, f32[25,200]{1,0:T(8,128)} %constant.29.clone.table_ref, f32[200,4]{1,0:T(8,128)} %constant.30.clone.groups_ref), custom_call_target="tpu_custom_call" | custom-call | tf_op jit(solution)/shard_map/harmonic/pallas_call | solution.py:694
  90.5 1.4 %copy.57 = f32[25,4]{0,1:T(4,128)} copy(f32[25,4]{1,0:T(8,128)} %harmonic.1) | data formatting | bytes 800
  (18 shorter events, 0.1 us)
Async XLA Ops:
  0.6 2.6 %copy-start.4 = (bf16[256,160]{1,0:T(8,128)(2,1)S(1)}, bf16[256,160]{1,0:T(8,128)(2,1)}, u32[]{:S(2)}) copy-start(bf16[256,160]{1,0:T(8,128)(2,1)} %constant.24.clone.select_ref) | copy-start | bytes 245764
  0.6 2.6 %copy-start.3 = (s32[4,4608]{1,0:T(4,128)S(1)}, s32[4,4608]{1,0:T(4,128)}, u32[]{:S(2)}) copy-start(s32[4,4608]{1,0:T(4,128)} %codes_ref.3) | copy-start | bytes 221188
  3.3 24.4 %copy-start = (f32[4,35,4608]{2,1,0:T(8,128)}, f32[4,35,4608]{2,1,0:T(8,128)S(1)}, u32[]{:S(2)}) copy-start(f32[4,35,4608]{2,1,0:T(8,128)S(1)} %copy.48.fields_ref) | copy-start | bytes 7741444
  4.9 7.3 %collective-permute-start = (f32[3,64,96]{2,1,0:T(8,128)}, f32[3,64,96]{2,1,0:T(8,128)S(1)}, u32[]{:S(2)}, u32[]{:S(2)}) collective-permute-start(f32[3,64,96]{2,1,0:T(8,128)} %get-tuple-element.14), channel_id=1, source_target_pairs={{16,0},{32,16},{48,32},{64,48},{80,64},{96,80},{112,96},{17,1},{33... | collective-permute-start | bytes 221192 | tf_op jit(solution)/shard_map/ppermute | solution.py:530
  8.2 5.0 %collective-permute-start.1 = (f32[3,64,96]{2,1,0:T(8,128)}, f32[3,64,96]{2,1,0:T(8,128)S(1)}, u32[]{:S(2)}, u32[]{:S(2)}) collective-permute-start(f32[3,64,96]{2,1,0:T(8,128)} %get-tuple-element.15), channel_id=1, source_target_pairs={{0,16},{16,32},{32,48},{48,64},{64,80},{80,96},{96,112},{1,17},{17... | collective-permute-start | bytes 221192 | tf_op jit(solution)/shard_map/ppermute | solution.py:531
  13.2 14.5 %copy-start.5 = (f32[3,64,96]{2,1,0:T(8,128)}, f32[3,64,96]{2,1,0:T(8,128)S(1)}, u32[]{:S(2)}) copy-start(f32[3,64,96]{2,1,0:T(8,128)S(1)} %collective-permute-done.1.above_ref) | copy-start | bytes 221188
  13.3 39.9 %collective-permute-start.2 = (f32[3,64,96]{2,1,0:T(8,128)S(1)}, f32[3,64,96]{2,1,0:T(8,128)}, u32[]{:S(2)}, u32[]{:S(2)}) collective-permute-start(f32[3,64,96]{2,1,0:T(8,128)S(1)} %pad_maximum_fusion), channel_id=1, source_target_pairs={{1,0},{2,1},{3,2},{4,3},{5,4},{6,5},{7,6},{8,7},{9,8},{10,9},{11,1... | collective-permute-start | bytes 221192 | tf_op jit(solution)/shard_map/ppermute | solution.py:550
  15.2 38.0 %collective-permute-start.3 = (f32[3,64,96]{2,1,0:T(8,128)}, f32[3,64,96]{2,1,0:T(8,128)}, u32[]{:S(2)}, u32[]{:S(2)}) collective-permute-start(f32[3,64,96]{2,1,0:T(8,128)} %pad_maximum_fusion.1), channel_id=1, source_target_pairs={{0,1},{1,2},{2,3},{3,4},{4,5},{5,6},{6,7},{7,8},{8,9},{9,10},{10,1... | collective-permute-start | bytes 221192 | tf_op jit(solution)/shard_map/ppermute | solution.py:551
  20.6 0.9 %copy-start.7 = (bf16[160,512]{1,0:T(8,128)(2,1)S(1)}, bf16[160,512]{1,0:T(8,128)(2,1)}, u32[]{:S(2)}) copy-start(bf16[160,512]{1,0:T(8,128)(2,1)} %constant.10.clone.select_ref) | copy-start | bytes 491524
  27.8 4.9 %copy-start.1 = (f32[3,4,4608]{2,1,0:T(4,128)S(1)}, f32[3,4,4608]{2,1,0:T(4,128)}, u32[]{:S(2)}) copy-start(f32[3,4,4608]{2,1,0:T(4,128)} %normals_ref.5) | copy-start | bytes 663556
  32.6 20.6 %copy-start.2 = (f32[9,4608]{1,0:T(8,128)S(1)}, f32[9,4608]{1,0:T(8,128)}, u32[]{:S(2)}) copy-start(f32[9,4608]{1,0:T(8,128)} %geometry_ref.3) | copy-start | bytes 497668
  32.7 20.6 %copy-start.6 = (f32[3,64,96]{2,1,0:T(8,128)S(1)}, f32[3,64,96]{2,1,0:T(8,128)}, u32[]{:S(2)}) copy-start(f32[3,64,96]{2,1,0:T(8,128)} %copy-done.5) | copy-start | bytes 221188
  32.7 20.6 %copy-start.8 = (bf16[40,192]{1,0:T(8,128)(2,1)S(1)}, bf16[40,192]{1,0:T(8,128)(2,1)}, u32[]{:S(2)}) copy-start(bf16[40,192]{1,0:T(8,128)(2,1)} %constant.27.clone.lift_ref) | copy-start | bytes 46084
  32.7 20.5 %copy-start.9 = (f32[4,4608]{1,0:T(4,128)S(1)}, f32[4,4608]{1,0:T(4,128)}, u32[]{:S(2)}) copy-start(f32[4,4608]{1,0:T(4,128)} %scale_ref.1) | copy-start | bytes 221188
  32.7 20.5 %copy-start.11 = (bf16[40,256]{1,0:T(8,128)(2,1)S(1)}, bf16[40,256]{1,0:T(8,128)(2,1)}, u32[]{:S(2)}) copy-start(bf16[40,256]{1,0:T(8,128)(2,1)} %constant.25.clone.into_ref) | copy-start | bytes 61444
  32.7 20.5 %copy-start.12 = (f32[40,40]{1,0:T(8,128)S(1)}, f32[40,40]{1,0:T(8,128)}, u32[]{:S(2)}) copy-start(f32[40,40]{1,0:T(8,128)} %constant.28.clone.inverse_ref) | copy-start | bytes 19204
  32.7 20.5 %copy-start.13 = (f32[3,200]{1,0:T(4,128)S(1)}, f32[3,200]{1,0:T(4,128)}, u32[]{:S(2)}) copy-start(f32[3,200]{1,0:T(4,128)} %coords_ref.1) | copy-start | bytes 7204
  32.7 20.5 %copy-start.14 = (s32[200]{0:T(256)S(1)}, s32[200]{0:T(256)}, u32[]{:S(2)}) copy-start(s32[200]{0:T(256)} %param.27) | copy-start | bytes 2404
  32.7 20.5 %copy-start.15 = (s32[200]{0:T(256)S(1)}, s32[200]{0:T(256)}, u32[]{:S(2)}) copy-start(s32[200]{0:T(256)} %param.26) | copy-start | bytes 2404
  53.3 21.9 %copy-start.10 = (bf16[120,96]{1,0:T(8,128)(2,1)S(1)}, bf16[120,96]{1,0:T(8,128)(2,1)}, u32[]{:S(2)}) copy-start(bf16[120,96]{1,0:T(8,128)(2,1)} %constant.26.clone.from_ref) | copy-start | bytes 69124
  62.2 25.8 %all-to-all-start = ((f32[128,1,200]{2,1,0:T(1,128)}), f32[128,1,200]{2,1,0:T(1,128)S(1)}, u32[]{:S(2)}, u32[]{:S(2)}) async-start(f32[128,1,200]{2,1,0:T(1,128)} %copy.52), calls=%async_computation | async-start | bytes 262144 | tf_op jit(solution)/shard_map/all_to_all | solution.py:644
  81.8 3.1 %copy-start.16 = (f32[4,35,4608]{2,1,0:T(8,128)S(1)}, f32[4,35,4608]{2,1,0:T(8,128)}, u32[]{:S(2)}) copy-start(f32[4,35,4608]{2,1,0:T(8,128)} %get-tuple-element.30) | copy-start | bytes 7741444
where the time goes:
time: 92.6 us; the launch traced here: 91.9 us
  Pallas kernels  44.8 us (48%)
  starting transfers between devices  25.2 us (27%)
  local copies, waits for them, and re-layouts  17.8 us (19%)
  between operations  1.61 us (2%)
  other arithmetic  1.48 us (2%)
  waiting for transfers between devices  1.06 us (1%)
    pallas_call x1, Pallas kernels, local(): pl.pallas_call(functools.partial(gather_kernel, slot_count), grid_spec=pl...  20.4 us
    unnamed x39, local copies, waits for them, and re-layouts  15.5 us
    all_to_all x1, starting transfers between devices, local(): received = lax.all_to_all(spread, ('px', 'py'), 0, 0, tiled=True)  12.9 us
    pallas_call x1, Pallas kernels, local(): pl.pallas_call(functools.partial(pressure_kernel, slot_faces, const['powe...  8.15 us
    pallas_call x1, Pallas kernels, local(): pl.pallas_call(velocity_kernel, grid_spec=pltpu.PrefetchScalarGridSpec(nu...  6.63 us
    pallas_call x1, Pallas kernels, local(): pl.pallas_call(table_kernel, grid=(steps,), in_specs=[pl.BlockSpec((4, NO...  6.18 us
    ppermute x1, starting transfers between devices, local(): from_left = lax.ppermute(to_right, 'py', forward)  4.61 us
    ppermute x1, starting transfers between devices, local(): below = lax.ppermute(up, 'px', backward)  3.32 us
  transfers between devices with their start and end apart: 5, of which 1 were waited for; matrix products, arithmetic and copies ran while one was open for 14% of the time, Pallas kernels for 36%

commit v1 on v0

v1 whole, which is shorter than its diff:
```python
import functools
import math

import jax
import jax.numpy as jnp
import numpy as np
from jax import lax
from jax.experimental import pallas as pl
from jax.experimental.pallas import tpu as pltpu
from jax.sharding import PartitionSpec as P

QPTS = 50
NODES = 35
PAD = 40
FACE_ROWS = 16
ROWS = 144
LANES = 128


highest = lax.Precision.HIGHEST
section_decay = -567301805773.0 / 1357537059087.0
section_gain = 5161836677717.0 / 13612068292357.0
time_step = 0.01
f32 = jnp.float32
bf16 = jnp.bfloat16


def exponent_table():
    listing = []
    for degree in range(5):
        for third in range(degree + 1):
            for second in range(degree + 1 - third):
                listing.append((degree - second - third, second, third))
    return np.array(listing)


def factorials(values):
    lookup = np.array([float(math.factorial(level)) for level in range(24)])
    return lookup[values]


def eliminate(matrix, right_hand):
    order_size = matrix.shape[0]
    work = np.concatenate([matrix, right_hand], axis=1).astype(float)
    for pivot_col in range(order_size):
        best = max(range(pivot_col, order_size), key=lambda row_id: abs(work[row_id, pivot_col]))
        work[[pivot_col, best]] = work[[best, pivot_col]]
        work[pivot_col] = work[pivot_col] / work[pivot_col, pivot_col]
        for row_id in range(order_size):
            if row_id != pivot_col:
                work[row_id] = work[row_id] - work[row_id, pivot_col] * work[pivot_col]
    return work[:, order_size:]


def element_tables():
    powers = exponent_table()
    points = powers / 4.0
    vander = np.prod(points[:, None, :] ** powers[None, :, :], axis=2)
    inverse = eliminate(vander, np.eye(35))
    derivs = []
    for axis_id in range(3):
        lowered = np.maximum(powers - (np.arange(3) == axis_id)[None, :], 0)
        slope_table = powers[None, :, axis_id] * np.prod(
            points[:, None, :] ** lowered[None, :, :], axis=2
        )
        derivs.append(slope_table @ inverse)
    summed = powers[:, None, :] + powers[None, :, :]
    exp_r = summed[..., 0]
    exp_s = summed[..., 1]
    exp_t = summed[..., 2]
    volume = (
        factorials(exp_r)
        * factorials(exp_s)
        * factorials(exp_t)
        / factorials(exp_r + exp_s + exp_t + 3)
    )
    mass_matrix = inverse.T @ volume @ inverse
    face_grams = [
        np.where(
            exp_t == 0, factorials(exp_r) * factorials(exp_s) / factorials(exp_r + exp_s + 2), 0.0
        ),
        np.where(
            exp_s == 0, factorials(exp_r) * factorials(exp_t) / factorials(exp_r + exp_t + 2), 0.0
        ),
        factorials(exp_r)
        * factorials(exp_s)
        * factorials(exp_t)
        / factorials(exp_r + exp_s + exp_t + 2),
        np.where(
            exp_r == 0, factorials(exp_s) * factorials(exp_t) / factorials(exp_s + exp_t + 2), 0.0
        ),
    ]
    listed = [tuple((int(entry) for entry in powers[node_id])) for node_id in range(35)]
    face_nodes = np.array(
        [
            [node_id for node_id in range(35) if listed[node_id][2] == 0],
            [node_id for node_id in range(35) if listed[node_id][1] == 0],
            [node_id for node_id in range(35) if sum(listed[node_id]) == 4],
            [node_id for node_id in range(35) if listed[node_id][0] == 0],
        ]
    )
    surface = np.zeros((35, 60))
    for face_id in range(4):
        face_mass = inverse.T @ face_grams[face_id] @ inverse
        for node_id in range(15):
            surface[:, 4 * node_id + face_id] = face_mass[:, face_nodes[face_id, node_id]]
    lifting = eliminate(mass_matrix, surface)
    return (np.stack(derivs), lifting, face_nodes, inverse, powers)


def associated(degree, order, cosine, sine):
    current = cosine * 0.0 + 1.0
    for step_id in range(1, order + 1):
        current = -(2 * step_id - 1) * sine * current
    if degree == order:
        return current
    following = cosine * (2 * order + 1) * current
    for level in range(order + 2, degree + 1):
        current, following = (
            following,
            ((2 * level - 1) * cosine * following - (level + order - 1) * current)
            / (level - order),
        )
    return following


def harmonic_table():
    inner_node = math.sqrt(5.0 - 2.0 * math.sqrt(10.0 / 7.0)) / 3.0
    outer_node = math.sqrt(5.0 + 2.0 * math.sqrt(10.0 / 7.0)) / 3.0
    inner_weight = (322.0 + 13.0 * math.sqrt(70.0)) / 900.0
    outer_weight = (322.0 - 13.0 * math.sqrt(70.0)) / 900.0
    cosines = np.array([-outer_node, -inner_node, 0.0, inner_node, outer_node])
    weights = np.array([outer_weight, inner_weight, 128.0 / 225.0, inner_weight, outer_weight])
    azimuth = 2.0 * np.pi * (np.arange(10) + 0.5) / 10.0
    polar = np.repeat(cosines, 10)
    circle = np.tile(azimuth, 5)
    point_weight = np.repeat(weights, 10) * 2.0 * np.pi / 10.0
    sine = np.sqrt(1.0 - polar**2)
    table_rows = []
    for degree in range(5):
        for order in range(-degree, degree + 1):
            absolute = abs(order)
            legendre = associated(degree, absolute, polar, sine)
            factor = math.sqrt(
                (2 * degree + 1)
                / (4.0 * math.pi)
                * math.factorial(degree - absolute)
                / math.factorial(degree + absolute)
            )
            if order > 0:
                angular = math.sqrt(2.0) * np.cos(order * circle)
            elif order < 0:
                angular = math.sqrt(2.0) * np.sin(absolute * circle)
            else:
                angular = circle * 0.0 + 1.0
            table_rows.append(factor * legendre * angular * point_weight)
    return np.array(table_rows)


def constant_tables():
    derivs, lifting, face_nodes, inverse, powers = element_tables()
    table_select = np.zeros((ROWS, 4 * LANES), np.float32)
    trace_select = np.zeros((4 * 4 * FACE_ROWS, ROWS), np.float32)
    for face in range(4):
        for field in range(4):
            for place in range(15):
                source = 4 * face_nodes[face, place] + field
                column = FACE_ROWS * field + place
                table_select[source, LANES * face + column] = 1.0
                table_select[source, LANES * face + 64 + column] = 1.0
                trace_select[64 * face + column, source] = 1.0
    whole = np.round(3.0 * derivs)
    into_p = np.zeros((ROWS, 128), np.float32)
    from_p = np.zeros((3 * ROWS, 48), np.float32)
    lift = np.zeros((ROWS, 256), np.float32)
    for node in range(NODES):
        for axis_id in range(3):
            into_p[4 * node, PAD * axis_id : PAD * axis_id + NODES] = -whole[axis_id, node]
            for field in range(1, 4):
                from_p[ROWS * axis_id + 4 * node + field, :NODES] = whole[axis_id, node]
        for face in range(4):
            for place in range(15):
                entry = lifting[node, 4 * place + face]
                column = FACE_ROWS * face + place
                lift[4 * node, column] = entry
                for field in range(1, 4):
                    lift[4 * node + field, 64 * field + column] = -entry
    lift_hi = lift.astype(jnp.bfloat16)
    lift_lo = (lift - lift_hi.astype(np.float32)).astype(jnp.bfloat16)
    return {
        "table_select": jnp.asarray(table_select, bf16),
        "trace_select": jnp.asarray(trace_select, bf16),
        "into_p": jnp.asarray(np.concatenate([into_p, into_p], axis=1), bf16),
        "from_p": jnp.asarray(np.concatenate([from_p, from_p], axis=1), bf16),
        "lift": jnp.asarray(np.concatenate([lift_hi, lift_lo], axis=0)),
        "inverse": jnp.asarray(np.pad(inverse.T, ((0, 5), (0, 5))), f32),
        "powers": powers,
    }


def halves(values):
    high = values.astype(bf16)
    return high, (values - high.astype(f32)).astype(bf16)


def thirds(values):
    high = values.astype(bf16)
    rest = values - high.astype(f32)
    middle = rest.astype(bf16)
    return high, middle, (rest - middle.astype(f32)).astype(bf16)


def product(left, right, dims=((1,), (0,))):
    return lax.dot_general(left, right, (dims, ((), ())), preferred_element_type=f32)


def stack_nodes(fields_ref, stacked):
    tiles = range(stacked.shape[0])
    for tile in tiles:
        for node in range(NODES):
            stacked[tile, 4 * node : 4 * node + 4, :] = fields_ref[
                node, :, LANES * tile : LANES * tile + LANES
            ]
    return halves(jnp.concatenate([stacked[tile] for tile in tiles], axis=1))


def one_field(stacked, field):
    tiles = range(stacked.shape[0])
    rows = pl.ds(field, NODES, stride=4)
    return jnp.concatenate([stacked[tile, rows, :] for tile in tiles], axis=1)


def pack_kernel(slot_faces, fields_ref, codes_ref, select_ref, up_ref, down_ref, left_ref, right_ref, stacked):
    stacked[...] = jnp.zeros_like(stacked)
    high, low = stack_nodes(fields_ref, stacked)
    traces = product(select_ref[...], high) + product(select_ref[...], low)
    chosen = jnp.zeros((64, traces.shape[1]), f32)
    for face in range(4):
        remote = codes_ref[face : face + 1, :] >= slot_faces
        chosen = jnp.where(remote, traces[64 * face : 64 * face + 64, :], chosen)
    width = left_ref.shape[1]
    pieces = [chosen[:, width * heading : width * heading + width] for heading in range(8)]
    for place in range(3):
        up_ref[place] = pieces[place]
        down_ref[place] = pieces[5 + place]
    left_ref[...] = pieces[3]
    right_ref[...] = pieces[4]


def table_kernel(slot_faces, fields_ref, codes_ref, select_ref, table_ref, packed_ref, stacked):
    @pl.when(pl.program_id(0) == 0)
    def _():
        stacked[...] = jnp.zeros_like(stacked)

    high, low = stack_nodes(fields_ref, stacked)
    for half in range(2):
        select = select_ref[:, 256 * half : 256 * half + 256]
        rows = product(high, select, ((0,), (0,))) + product(low, select, ((0,), (0,)))
        table_ref[2 * half] = rows[:, :LANES]
        table_ref[2 * half + 1] = rows[:, LANES:]
        codes = codes_ref[2 * half : 2 * half + 2, :]
        codes = jnp.where((codes >= 0) & (codes < slot_faces), codes, 0)
        packed_ref[half : half + 1, :] = codes[0:1] + (codes[1:2] << 16)


def gather_rows(slot_count, first, codes_ref, table_ref, normals_ref, outer_ref, rows_refs):
    width = outer_ref.shape[1]
    left_half = lax.broadcasted_iota(jnp.int32, (1, LANES), 1) < 64
    for tile in range(width // LANES):
        for half in range(2):
            rows_ref = rows_refs[half]
            base = half * slot_count + first + tile * LANES
            for row in range(LANES):
                code = codes_ref[base + row]
                one = table_ref[pl.ds(code & 0xFFFF, 1), :]
                two = table_ref[pl.ds(lax.shift_right_logical(code, 16), 1), :]
                rows_ref[row : row + 1, :] = jnp.where(left_half, one, two)
            turned = rows_ref[...].T
            lanes = slice(tile * LANES, tile * LANES + LANES)
            for side in range(2):
                face = 2 * half + side
                part = turned[64 * side : 64 * side + 64, :]
                total = -part[0:16]
                for axis_id in range(3):
                    facing = normals_ref[axis_id, face : face + 1, lanes]
                    total = total + facing * part[16 + 16 * axis_id : 32 + 16 * axis_id]
                outer_ref[FACE_ROWS * face : FACE_ROWS * face + FACE_ROWS, lanes] = total


def outer_flux(traces, normals_ref, scale_ref, codes_ref, outer_ref):
    fluxes = []
    for face in range(4):
        inner_p = traces[64 * face : 64 * face + 16]
        along = jnp.zeros_like(inner_p)
        for axis_id in range(3):
            facing = normals_ref[axis_id, face : face + 1, :]
            start = 64 * face + 16 + 16 * axis_id
            along = along + facing * traces[start : start + 16]
        wall = codes_ref[face : face + 1, :] < 0
        beyond = outer_ref[FACE_ROWS * face : FACE_ROWS * face + FACE_ROWS, :]
        beyond = jnp.where(wall, -along - inner_p, beyond)
        fluxes.append((0.5 * scale_ref[face : face + 1, :]) * (along - inner_p - beyond))
    columns = list(fluxes)
    for axis_id in range(3):
        for face in range(4):
            columns.append(normals_ref[axis_id, face : face + 1, :] * fluxes[face])
    return jnp.concatenate(columns, axis=0)


def section_kernel(
    slot_count,
    powers,
    group,
    packed_ref,
    live_ref,
    table_ref,
    next_normals_ref,
    fields_ref,
    residue_ref,
    geometry_ref,
    normals_ref,
    scale_ref,
    codes_ref,
    right_ref,
    left_ref,
    below_ref,
    above_ref,
    elems_ref,
    ids_ref,
    coords_ref,
    select_ref,
    into_ref,
    from_ref,
    lift_ref,
    inverse_ref,
    fields_out,
    residue_out,
    spread_ref,
    stacked,
    combined,
    slow,
    rates,
    remote,
    outer,
    sampled,
    pressure,
    monomials,
    *rows_refs,
):
    step = pl.program_id(0)
    last = pl.num_programs(0) - 1
    width = fields_ref.shape[2]
    slot_faces = 4 * slot_count

    def gather():
        first = step * width
        gather_rows(slot_count, first, packed_ref, table_ref, next_normals_ref, outer, rows_refs)

    def update(beside):
        first = (step - 1) * width
        high, low = stack_nodes(fields_ref, stacked)
        traces = product(select_ref[...], high) + product(select_ref[...], low)
        flux = outer_flux(traces, normals_ref, scale_ref, codes_ref, outer)
        beside()
        flux_hi, flux_lo = halves(flux)
        lifted = product(lift_ref[...], flux_hi)
        total = lifted[:ROWS] + lifted[ROWS:] + product(lift_ref[0:ROWS, :], flux_lo)
        geometry = geometry_ref[...] * (1.0 / 3.0)
        for axis_id in range(3):
            weighted = jnp.zeros((NODES, width), f32)
            for direction in range(3):
                at = 3 * axis_id + direction
                velocity = one_field(stacked, 1 + direction)
                weighted = weighted + geometry[at : at + 1, :] * velocity
            combined[PAD * axis_id : PAD * axis_id + NODES, :] = weighted
        total = total + product(into_ref[...], jnp.concatenate(halves(combined[...]), axis=0))
        slow[0:NODES, :] = one_field(stacked, 0)
        slopes = product(from_ref[...], jnp.concatenate(halves(slow[...]), axis=0))
        place = lax.broadcasted_iota(jnp.int32, (8, width), 0) & 3
        for axis_id in range(3):
            pattern = jnp.zeros((8, width), f32)
            for direction in range(3):
                at = 3 * axis_id + direction
                pattern = jnp.where(place == direction + 1, geometry[at : at + 1, :], pattern)
            slope = slopes[ROWS * axis_id : ROWS * axis_id + ROWS].reshape(ROWS // 8, 8, width)
            total = total - (slope * pattern[None]).reshape(ROWS, width)
        rates[...] = total
        keep = lax.broadcasted_iota(jnp.int32, (1, width), 1) + first < live_ref[0]
        for node in range(NODES):
            rate = rates[4 * node : 4 * node + 4, :]
            residue_next = section_decay * residue_ref[node] + time_step * rate
            fields_next = fields_ref[node] + section_gain * residue_next
            fields_next = jnp.where(keep, fields_next, 0.0)
            fields_out[node] = fields_next
            residue_out[node] = jnp.where(keep, residue_next, 0.0)
            pressure[node : node + 1, :] = fields_next[0:1]
        parts = jnp.concatenate(thirds(pressure[...]), axis=0)
        slots = lax.broadcasted_iota(jnp.int32, (width, elems_ref.shape[1]), 0) + first
        picks = jnp.where(slots == elems_ref[...], 1.0, 0.0).astype(bf16)
        sampled[...] += product(parts, picks)

    @pl.when(step == 0)
    def _():
        stacked[...] = jnp.zeros_like(stacked)
        combined[...] = jnp.zeros_like(combined)
        slow[...] = jnp.zeros_like(slow)
        pressure[...] = jnp.zeros_like(pressure)
        sampled[...] = jnp.zeros_like(sampled)
        monomials[...] = jnp.zeros_like(monomials)
        remote[...] = jnp.zeros_like(remote)
        count = right_ref.shape[2]
        sources = [
            left_ref[2],
            above_ref[1],
            right_ref[2],
            left_ref[0],
            right_ref[0],
            left_ref[1],
            below_ref[1],
            right_ref[1],
        ]
        for heading in range(8):
            remote[:, count * heading : count * heading + count] = sources[heading]
        gather()

    @pl.when((step > 0) & ((step - 1) * width < 8 * right_ref.shape[2]))
    def _():
        lanes = pl.ds(pl.multiple_of((step - 1) * width, width), width)
        for face in range(4):
            rows = slice(FACE_ROWS * face, FACE_ROWS * face + FACE_ROWS)
            total = -remote[0:16, lanes]
            for axis_id in range(3):
                facing = normals_ref[axis_id, face : face + 1, :]
                total = total + facing * remote[16 + 16 * axis_id : 32 + 16 * axis_id, lanes]
            is_remote = codes_ref[face : face + 1, :] >= slot_faces
            outer[rows, :] = jnp.where(is_remote, total, outer[rows, :])

    @pl.when((step > 0) & (step < last))
    def _():
        update(gather)

    @pl.when(step == last)
    def _():
        update(lambda: None)
        ladders = []
        for axis_id in range(3):
            base = coords_ref[axis_id : axis_id + 1, :]
            square = base * base
            ladders.append([jnp.ones_like(base), base, square, square * base, square * square])
        for node in range(NODES):
            exps = [int(entry) for entry in powers[node]]
            monomials[node : node + 1, :] = (
                ladders[0][exps[0]] * ladders[1][exps[1]] * ladders[2][exps[2]]
            )
        basis = jnp.dot(
            inverse_ref[...], monomials[...], precision=highest, preferred_element_type=f32
        )
        gathered = sampled[0:PAD, :] + sampled[48 : 48 + PAD, :] + sampled[96 : 96 + PAD, :]
        values = jnp.sum(basis * gathered, axis=0, keepdims=True)
        ids = ids_ref[...]
        owner = lax.shift_right_logical(ids * 5243, 20)
        place = ids - group * owner
        owners = lax.broadcasted_iota(jnp.int32, (spread_ref.shape[0], ids.shape[1]), 0)
        held = jnp.where(owners == owner, values, 0.0)
        places = lax.broadcasted_iota(jnp.int32, (spread_ref.shape[2], ids.shape[1]), 0)
        chosen = jnp.where(places == place, 1.0, 0.0).astype(bf16)
        spread = jnp.zeros((spread_ref.shape[0], spread_ref.shape[2]), f32)
        for part in thirds(held):
            spread = spread + product(part, chosen, ((1,), (1,)))
        spread_ref[:, 0, :] = spread


def harmonic_kernel(received_ref, table_ref, groups_ref, out_ref):
    mine = jnp.sum(received_ref[...], axis=0)
    weighted = groups_ref[...] * mine
    out_ref[...] = lax.dot_general(
        weighted,
        table_ref[...],
        (((1,), (1,)), ((), ())),
        precision=highest,
        preferred_element_type=f32,
    )


def fixed(shape):
    return pl.BlockSpec(shape, lambda *_: (0,) * len(shape))


def local(
    fields,
    residue,
    geometry,
    normals,
    face_scale,
    neighbours,
    send_faces,
    live_counts,
    sample_ids,
    sample_elems,
    sample_coords,
):
    const = constant_tables()
    fields = jnp.transpose(fields, (1, 0, 2))
    residue = jnp.transpose(residue, (1, 0, 2))
    slot_count = fields.shape[2]
    slot_faces = 4 * slot_count
    bound_count = send_faces.shape[1]
    reach = 8 * bound_count
    samples = sample_ids.shape[0]
    devices = lax.axis_size(("px", "py"))
    shape = jax.ShapeDtypeStruct

    up, down, left, right = pl.pallas_call(
        functools.partial(pack_kernel, slot_faces),
        grid=(1,),
        in_specs=[
            pl.BlockSpec((NODES, 4, reach), lambda t: (0, 0, 0)),
            pl.BlockSpec((4, reach), lambda t: (0, 0)),
            fixed((256, ROWS)),
        ],
        out_specs=[
            fixed((3, 64, bound_count)),
            fixed((3, 64, bound_count)),
            fixed((64, bound_count)),
            fixed((64, bound_count)),
        ],
        out_shape=[
            shape((3, 64, bound_count), f32),
            shape((3, 64, bound_count), f32),
            shape((64, bound_count), f32),
            shape((64, bound_count), f32),
        ],
        scratch_shapes=[pltpu.VMEM((reach // LANES, ROWS, LANES), f32)],
        compiler_params=pltpu.CompilerParams(vmem_limit_bytes=16 << 20),
        name="pack",
    )(fields, neighbours, const["trace_select"])

    def steps_along(axis):
        count = lax.axis_size(axis)
        forward = [(i, i + 1) for i in range(count - 1)]
        return forward, [(target, source) for source, target in forward]

    forward, backward = steps_along("px")
    below = lax.ppermute(up, "px", backward)
    above = lax.ppermute(down, "px", forward)

    width = 768
    table, packed = pl.pallas_call(
        functools.partial(table_kernel, slot_faces),
        grid=(slot_count // width,),
        in_specs=[
            pl.BlockSpec((NODES, 4, width), lambda t: (0, 0, t)),
            pl.BlockSpec((4, width), lambda t: (0, t)),
            fixed((ROWS, 4 * LANES)),
        ],
        out_specs=[
            pl.BlockSpec((4, width, LANES), lambda t: (0, t, 0)),
            pl.BlockSpec((2, width), lambda t: (0, t)),
        ],
        out_shape=[
            shape((4, slot_count, LANES), f32),
            shape((2, slot_count), jnp.int32),
        ],
        scratch_shapes=[pltpu.VMEM((width // LANES, ROWS, LANES), f32)],
        compiler_params=pltpu.CompilerParams(vmem_limit_bytes=24 << 20),
        name="table",
    )(fields, neighbours, const["table_select"])
    table = table.reshape(slot_faces, LANES)

    forward, backward = steps_along("py")
    to_left = jnp.concatenate([left[None], below[0:1], above[0:1]])
    to_right = jnp.concatenate([right[None], below[2:3], above[2:3]])
    from_right = lax.ppermute(to_left, "py", backward)
    from_left = lax.ppermute(to_right, "py", forward)

    width = 512
    steps = slot_count // width

    def behind(rank):
        return lambda t, *_: (0,) * rank + (jnp.maximum(t - 1, 0),)

    def ahead(rank):
        return lambda t, *_: (0,) * rank + (jnp.minimum(t, steps - 1),)

    fields_next, residue_next, spread = pl.pallas_call(
        functools.partial(section_kernel, slot_count, const["powers"], samples),
        grid_spec=pltpu.PrefetchScalarGridSpec(
            num_scalar_prefetch=2,
            grid=(steps + 1,),
            in_specs=[
                pl.BlockSpec(memory_space=pltpu.VMEM),
                pl.BlockSpec((3, 4, width), ahead(2)),
                pl.BlockSpec((NODES, 4, width), behind(2)),
                pl.BlockSpec((NODES, 4, width), behind(2)),
                pl.BlockSpec((9, width), behind(1)),
                pl.BlockSpec((3, 4, width), behind(2)),
                pl.BlockSpec((4, width), behind(1)),
                pl.BlockSpec((4, width), behind(1)),
                fixed((3, 64, bound_count)),
                fixed((3, 64, bound_count)),
                fixed((3, 64, bound_count)),
                fixed((3, 64, bound_count)),
                fixed((1, samples)),
                fixed((1, samples)),
                fixed((3, samples)),
                fixed((256, ROWS)),
                fixed((ROWS, 256)),
                fixed((3 * ROWS, 96)),
                fixed((2 * ROWS, 256)),
                fixed((PAD, PAD)),
            ],
            out_specs=[
                pl.BlockSpec((NODES, 4, width), behind(2)),
                pl.BlockSpec((NODES, 4, width), behind(2)),
                fixed((devices, 1, samples)),
            ],
            scratch_shapes=[
                pltpu.VMEM((width // LANES, ROWS, LANES), f32),
                pltpu.VMEM((128, width), f32),
                pltpu.VMEM((48, width), f32),
                pltpu.VMEM((ROWS, width), f32),
                pltpu.VMEM((64, pl.cdiv(reach, width) * width), f32),
                pltpu.VMEM((64, width), f32),
                pltpu.VMEM((144, samples), f32),
                pltpu.VMEM((48, width), f32),
                pltpu.VMEM((PAD, samples), f32),
                pltpu.VMEM((LANES, LANES), f32),
                pltpu.VMEM((LANES, LANES), f32),
            ],
        ),
        out_shape=[
            shape(fields.shape, f32),
            shape(residue.shape, f32),
            shape((devices, 1, samples), f32),
        ],
        compiler_params=pltpu.CompilerParams(vmem_limit_bytes=32 << 20),
        name="section",
    )(
        packed.reshape(-1),
        live_counts,
        table,
        normals,
        fields,
        residue,
        geometry,
        normals,
        face_scale,
        neighbours,
        from_right,
        from_left,
        below,
        above,
        sample_elems.reshape(1, samples),
        sample_ids.reshape(1, samples),
        sample_coords,
        const["trace_select"],
        const["into_p"],
        const["from_p"],
        const["lift"],
        const["inverse"],
    )
    received = lax.all_to_all(spread, ("px", "py"), 0, 0, tiled=True)

    receivers = samples // QPTS
    harmonic = np.tile(harmonic_table(), (1, receivers)).astype(np.float32)
    groups = (np.arange(samples)[None] // QPTS == np.arange(receivers)[:, None]).astype(np.float32)
    coefficients = pl.pallas_call(
        harmonic_kernel,
        out_shape=shape((receivers, harmonic.shape[0]), f32),
        name="harmonic",
    )(received, jnp.asarray(harmonic), jnp.asarray(groups))
    return (
        jnp.transpose(fields_next, (1, 0, 2)),
        jnp.transpose(residue_next, (1, 0, 2)),
        coefficients.T,
    )


def solution(mesh):
    placed = (
        P(None, None, ("px", "py")),
        P(None, None, ("px", "py")),
        P(None, ("px", "py")),
        P(None, None, ("px", "py")),
        P(None, ("px", "py")),
        P(None, ("px", "py")),
        P(None, ("px", "py")),
        P(("px", "py")),
        P(("px", "py")),
        P(("px", "py")),
        P(None, ("px", "py")),
    )
    return jax.shard_map(
        local,
        mesh=mesh,
        in_specs=placed,
        out_specs=(P(None, None, ("px", "py")), P(None, None, ("px", "py")), P(None, ("px", "py"))),
        check_vma=False,
    )
```

time: 92.6 us -> 96.9 us (1.046)
  blocking collectives: 0 us -> 23.4 us
  starting transfers between devices: 25.2 us -> 12.5 us
  Pallas kernels: 44.8 us -> 36.4 us
  local copies, waits for them, and re-layouts: 17.8 us -> 19.6 us
    all_to_all x0 -> x1, blocking collectives: none -> 23.4 us  [local(): received = lax.all_to_all(spread, ('px', 'py'), 0, 0, tiled=True)]
    all_to_all x1 -> x0, starting transfers between devices: 12.9 us -> none  [local(): received = lax.all_to_all(spread, ('px', 'py'), 0, 0, tiled=True)]
    pallas_call x5 -> x3, Pallas kernels: 43.2 us -> 35.8 us  [the longest x1 29.2 us: local(): pl.pallas_call(functools.partial(section_kernel, slot_count, const['power...]
    unnamed x39 -> x42, local copies, waits for them, and re-layouts: 15.5 us -> 18.8 us
    all_to_all x2 -> x0, local copies, waits for them, and re-layouts: 1.45 us -> none  [local(): received = lax.all_to_all(spread, ('px', 'py'), 0, 0, tiled=True)]
    pallas_call x1, Pallas kernels: 1.58 us -> 0.59 us  [local(): pl.pallas_call(functools.partial(pack_kernel, slot_faces), grid=(1,), in_...]
  transfers between devices with their start and end apart: 5 -> 4, of which waited for: 1 -> 2; matrix products, arithmetic and copies ran while one was open for 14% -> 2% of each run, Pallas kernels for 36% -> 5%
where the time goes in v1:
time: 96.9 us; the launch traced here: 96.2 us
  Pallas kernels  36.4 us (38%)
  blocking collectives  23.4 us (24%)
  local copies, waits for them, and re-layouts  19.6 us (20%)
  starting transfers between devices  12.5 us (13%)
  waiting for transfers between devices  1.62 us (2%)
  between operations  1.46 us (2%)
  other arithmetic  1.3 us (1%)
    pallas_call x1, Pallas kernels, local(): pl.pallas_call(functools.partial(section_kernel, slot_count, const['power...  29.2 us
    all_to_all x1, blocking collectives, local(): received = lax.all_to_all(spread, ('px', 'py'), 0, 0, tiled=True)  23.4 us
    unnamed x42, local copies, waits for them, and re-layouts  18.8 us
    pallas_call x1, Pallas kernels, local(): pl.pallas_call(functools.partial(table_kernel, slot_faces), grid=(slot_co...  4.82 us
    ppermute x1, starting transfers between devices, local(): from_left = lax.ppermute(to_right, 'py', forward)  4.62 us
    ppermute x1, starting transfers between devices, local(): below = lax.ppermute(up, 'px', backward)  3.46 us
    ppermute x1, starting transfers between devices, local(): above = lax.ppermute(down, 'px', forward)  3.1 us
  transfers between devices with their start and end apart: 4, of which 2 were waited for; matrix products, arithmetic and copies ran while one was open for 2% of the time, Pallas kernels for 5%

profile of v1, /device:TPU:1, one launch (start us, length us, event | category | flops | bytes accessed | tf_op | source)
XLA Modules:
  0.0 96.2 jit_solution(7185633173926588790)
XLA Ops:
  0.6 0.0 copy-start
  0.6 1.7 %copy-done = f32[4,35,4608]{2,0,1:T(4,128)S(1)} copy-done((f32[4,35,4608]{2,0,1:T(4,128)S(1)}, f32[4,35,4608]{2,0,1:T(4,128)}, u32[]{:S(2)}) %copy-start) | copy-done | bytes 2580504
  2.4 0.0 copy-start.6
  2.4 0.9 copy-done.6
  3.2 0.0 copy-start.8
  3.2 0.9 copy-done.8
  4.2 0.0 copy-start.1
  4.2 0.0 copy-start.7
  4.2 0.0 copy-start.11
  4.2 0.0 copy-start.9
  4.2 0.0 copy-start.10
  4.2 0.0 copy-start.17
  4.2 0.6 pack.1
  4.8 3.5 %collective-permute-start = (f32[3,64,96]{2,1,0:T(8,128)S(1)}, f32[3,64,96]{2,1,0:T(8,128)S(1)}, u32[]{:S(2)}, u32[]{:S(2)}) collective-permute-start(f32[3,64,96]{2,1,0:T(8,128)S(1)} %get-tuple-element.15), channel_id=1, source_target_pairs={{16,0},{32,16},{48,32},{64,48},{80,64},{96,80},{112,96},{17,1},{33... | collective-permute-start | bytes 221192 | tf_op jit(solution)/shard_map/ppermute | solution.py:544
  8.3 3.1 %collective-permute-start.1 = (f32[3,64,96]{2,1,0:T(8,128)S(1)}, f32[3,64,96]{2,1,0:T(8,128)S(1)}, u32[]{:S(2)}, u32[]{:S(2)}) collective-permute-start(f32[3,64,96]{2,1,0:T(8,128)S(1)} %get-tuple-element.16), channel_id=1, source_target_pairs={{0,16},{16,32},{32,48},{48,64},{64,80},{80,96},{96,112},{1,17},{17... | collective-permute-start | bytes 221192 | tf_op jit(solution)/shard_map/ppermute | solution.py:545
  11.4 0.4 collective-permute-done.below_ref
  11.7 1.3 %collective-permute-done.1.above_ref = f32[3,64,96]{2,1,0:T(8,128)S(1)} collective-permute-done((f32[3,64,96]{2,1,0:T(8,128)S(1)}, f32[3,64,96]{2,1,0:T(8,128)S(1)}, u32[]{:S(2)}, u32[]{:S(2)}) %collective-permute-start.1) | collective-permute-done | bytes 73760 | tf_op jit(solution)/shard_map/ppermute | solution.py:545
  13.0 0.6 pad_maximum_fusion
  13.6 1.3 %collective-permute-start.2 = (f32[3,64,96]{2,1,0:T(8,128)}, f32[3,64,96]{2,1,0:T(8,128)}, u32[]{:S(2)}, u32[]{:S(2)}) collective-permute-start(f32[3,64,96]{2,1,0:T(8,128)} %pad_maximum_fusion), channel_id=1, source_target_pairs={{1,0},{2,1},{3,2},{4,3},{5,4},{6,5},{7,6},{8,7},{9,8},{10,9},{11,1... | collective-permute-start | bytes 221192 | tf_op jit(solution)/shard_map/ppermute | solution.py:573
  14.9 0.7 pad_maximum_fusion.1
  15.6 4.6 %collective-permute-start.3 = (f32[3,64,96]{2,1,0:T(8,128)}, f32[3,64,96]{2,1,0:T(8,128)}, u32[]{:S(2)}, u32[]{:S(2)}) collective-permute-start(f32[3,64,96]{2,1,0:T(8,128)} %pad_maximum_fusion.1), channel_id=1, source_target_pairs={{0,1},{1,2},{2,3},{3,4},{4,5},{5,6},{6,7},{7,8},{8,9},{9,10},{10,1... | collective-permute-start | bytes 221192 | tf_op jit(solution)/shard_map/ppermute | solution.py:574
  20.9 0.0 copy-done.1
  20.9 0.0 copy-done.7
  20.9 0.0 copy-done.11
  20.9 4.8 %table.1 = (f32[4,4608,128]{2,1,0:T(8,128)S(1)}, s32[2,4608]{1,0:T(2,128)S(1)}) custom-call(f32[35,4,4608]{2,1,0:T(4,128)S(1)} %bitcast.11, s32[4,4608]{1,0:T(4,128)S(1)} %copy-done.7, bf16[144,512]{1,0:T(8,128)(2,1)S(1)} %copy-done.11), custom_call_target="tpu_custom_call" | custom-call | tf_op jit(solution)/shard_map/table/pallas_call | solution.py:548
  25.7 0.0 copy-start.2
  25.7 3.7 %copy-done.2 = f32[4,4608,128]{2,1,0:T(8,128)} copy-done((f32[4,4608,128]{2,1,0:T(8,128)}, f32[4,4608,128]{2,1,0:T(8,128)S(1)}, u32[]{:S(2)}) %copy-start.2) | copy-done | bytes 9437208
  29.4 0.6 copy-done.16
  30.0 0.8 reshape.18.packed_ref
  30.8 0.0 collective-permute-done.2.right_ref
  30.8 0.0 collective-permute-done.3.left_ref
  30.8 0.0 copy-done.5
  30.8 0.0 copy-done.9
  30.8 0.0 copy-done.10
  30.8 0.0 copy-done.17
  30.9 0.0 copy-start.3
  30.9 3.7 %copy-done.3 = f32[4,4608,128]{2,1,0:T(8,128)S(1)} copy-done((f32[4,4608,128]{2,1,0:T(8,128)S(1)}, f32[4,4608,128]{2,1,0:T(8,128)}, u32[]{:S(2)}) %copy-start.3) | copy-done | bytes 9437208
  34.5 1.7 %copy-done.4 = f32[4,35,4608]{2,0,1:T(4,128)S(1)} copy-done((f32[4,35,4608]{2,0,1:T(4,128)S(1)}, f32[4,35,4608]{2,0,1:T(4,128)}, u32[]{:S(2)}) %copy-start.4) | copy-done | bytes 2580504
  36.3 0.9 copy-done.12
  37.2 0.9 copy-done.13
  38.1 0.9 copy-done.14
  39.0 0.9 copy-done.15
  39.8 0.7 copy-done.18
  40.5 0.7 copy-done.19
  41.2 0.7 copy-done.20
  41.9 29.2 %section.1 = (f32[35,4,4608]{2,1,0:T(4,128)}, f32[35,4,4608]{2,1,0:T(4,128)}, f32[128,1,200]{2,1,0:T(1,128)S(1)}) custom-call(s32[9216]{0:T(1024)S(1)} %reshape.18.packed_ref, s32[1]{0:T(128)S(6)} %copy.21.live_ref, f32[18432,128]{1,0:T(8,128)S(1)} %bitcast.13, f32[3,4,4608]{2,1,0:T(4,128)S(1)} %copy-done.5, f32[35,4,4608]{2,1,0:T(4,128)S(1)} %bitcast.12, ...), custom_call_target="tpu_custom_call" | custom-call | tf_op jit(solution)/shard_map/section/pallas_call | solution.py:585
  71.0 23.4 %all_to_all.5.received_ref = f32[128,1,200]{2,1,0:T(1,128)} all-to-all(f32[128,1,200]{2,1,0:T(1,128)S(1)} %get-tuple-element.20), channel_id=1, replica_groups=mesh['px'=8,'py'=16] {'px','py'}, dimensions={0} | all-to-all | bytes 204800 | tf_op jit(solution)/shard_map/all_to_all | solution.py:662
  94.4 1.8 %harmonic.1 = f32[4,25]{1,0:T(4,128)} custom-call(f32[128,1,200]{2,1,0:T(1,128)} %all_to_all.5.received_ref, f32[25,200]{1,0:T(8,128)} %constant.22.clone.table_ref, f32[4,200]{1,0:T(4,128)} %constant.23.clone.groups_ref), custom_call_target="tpu_custom_call" | custom-call | tf_op jit(solution)/shard_map/harmonic/pallas_call | solution.py:667
  (12 shorter events, 0.0 us)
Async XLA Ops:
  0.6 1.7 %copy-start = (f32[4,35,4608]{2,0,1:T(4,128)S(1)}, f32[4,35,4608]{2,0,1:T(4,128)}, u32[]{:S(2)}) copy-start(f32[4,35,4608]{2,0,1:T(4,128)} %param.19) | copy-start | bytes 7741444
  2.4 0.9 copy-start.6
  3.2 0.9 copy-start.8
  4.2 16.7 %copy-start.1 = (f32[4,35,4608]{2,0,1:T(4,128)S(1)}, f32[4,35,4608]{2,0,1:T(4,128)}, u32[]{:S(2)}) copy-start(f32[4,35,4608]{2,0,1:T(4,128)} %param.19) | copy-start | bytes 7741444
  4.2 16.7 %copy-start.7 = (s32[4,4608]{1,0:T(4,128)S(1)}, s32[4,4608]{1,0:T(4,128)}, u32[]{:S(2)}) copy-start(s32[4,4608]{1,0:T(4,128)} %codes_ref.5) | copy-start | bytes 221188
  4.2 16.7 %copy-start.11 = (bf16[144,512]{1,0:T(8,128)(2,1)S(1)}, bf16[144,512]{1,0:T(8,128)(2,1)}, u32[]{:S(2)}) copy-start(bf16[144,512]{1,0:T(8,128)(2,1)} %constant.16.clone.select_ref) | copy-start | bytes 442372
  4.2 26.7 %copy-start.5 = (f32[3,4,4608]{2,1,0:T(4,128)S(1)}, f32[3,4,4608]{2,1,0:T(4,128)}, u32[]{:S(2)}) copy-start(f32[3,4,4608]{2,1,0:T(4,128)} %normals_ref.1) | copy-start | bytes 663556
  4.2 26.7 %copy-start.9 = (bf16[256,144]{1,0:T(8,128)(2,1)S(1)}, bf16[256,144]{1,0:T(8,128)(2,1)}, u32[]{:S(2)}) copy-start(bf16[256,144]{1,0:T(8,128)(2,1)} %constant.17.clone.select_ref) | copy-start | bytes 221188
  4.2 26.7 %copy-start.10 = (f32[9,4608]{1,0:T(8,128)S(1)}, f32[9,4608]{1,0:T(8,128)}, u32[]{:S(2)}) copy-start(f32[9,4608]{1,0:T(8,128)} %geometry_ref.1) | copy-start | bytes 497668
  4.2 26.7 %copy-start.17 = (f32[40,40]{1,0:T(8,128)S(1)}, f32[40,40]{1,0:T(8,128)}, u32[]{:S(2)}) copy-start(f32[40,40]{1,0:T(8,128)} %constant.21.clone.inverse_ref) | copy-start | bytes 19204
  4.8 6.9 %collective-permute-start = (f32[3,64,96]{2,1,0:T(8,128)S(1)}, f32[3,64,96]{2,1,0:T(8,128)S(1)}, u32[]{:S(2)}, u32[]{:S(2)}) collective-permute-start(f32[3,64,96]{2,1,0:T(8,128)S(1)} %get-tuple-element.15), channel_id=1, source_target_pairs={{16,0},{32,16},{48,32},{64,48},{80,64},{96,80},{112,96},{17,1},{33... | collective-permute-start | bytes 221192 | tf_op jit(solution)/shard_map/ppermute | solution.py:544
  8.3 4.7 %collective-permute-start.1 = (f32[3,64,96]{2,1,0:T(8,128)S(1)}, f32[3,64,96]{2,1,0:T(8,128)S(1)}, u32[]{:S(2)}, u32[]{:S(2)}) collective-permute-start(f32[3,64,96]{2,1,0:T(8,128)S(1)} %get-tuple-element.16), channel_id=1, source_target_pairs={{0,16},{16,32},{32,48},{48,64},{64,80},{80,96},{96,112},{1,17},{17... | collective-permute-start | bytes 221192 | tf_op jit(solution)/shard_map/ppermute | solution.py:545
  13.6 17.1 %collective-permute-start.2 = (f32[3,64,96]{2,1,0:T(8,128)}, f32[3,64,96]{2,1,0:T(8,128)}, u32[]{:S(2)}, u32[]{:S(2)}) collective-permute-start(f32[3,64,96]{2,1,0:T(8,128)} %pad_maximum_fusion), channel_id=1, source_target_pairs={{1,0},{2,1},{3,2},{4,3},{5,4},{6,5},{7,6},{8,7},{9,8},{10,9},{11,1... | collective-permute-start | bytes 221192 | tf_op jit(solution)/shard_map/ppermute | solution.py:573
  15.6 15.2 %collective-permute-start.3 = (f32[3,64,96]{2,1,0:T(8,128)}, f32[3,64,96]{2,1,0:T(8,128)}, u32[]{:S(2)}, u32[]{:S(2)}) collective-permute-start(f32[3,64,96]{2,1,0:T(8,128)} %pad_maximum_fusion.1), channel_id=1, source_target_pairs={{0,1},{1,2},{2,3},{3,4},{4,5},{5,6},{6,7},{7,8},{8,9},{9,10},{10,1... | collective-permute-start | bytes 221192 | tf_op jit(solution)/shard_map/ppermute | solution.py:574
  25.7 3.7 %copy-start.2 = (f32[4,4608,128]{2,1,0:T(8,128)}, f32[4,4608,128]{2,1,0:T(8,128)S(1)}, u32[]{:S(2)}) copy-start(f32[4,4608,128]{2,1,0:T(8,128)S(1)} %get-tuple-element.13) | copy-start | bytes 28311556
  29.4 0.6 copy-start.16
  30.9 3.7 %copy-start.3 = (f32[4,4608,128]{2,1,0:T(8,128)S(1)}, f32[4,4608,128]{2,1,0:T(8,128)}, u32[]{:S(2)}) copy-start(f32[4,4608,128]{2,1,0:T(8,128)} %copy-done.2) | copy-start | bytes 28311556
  34.5 1.7 %copy-start.4 = (f32[4,35,4608]{2,0,1:T(4,128)S(1)}, f32[4,35,4608]{2,0,1:T(4,128)}, u32[]{:S(2)}) copy-start(f32[4,35,4608]{2,0,1:T(4,128)} %param.20) | copy-start | bytes 7741444
  36.3 0.9 copy-start.12
  37.2 0.9 copy-start.13
  38.1 0.9 copy-start.14
  39.0 0.9 copy-start.15
  39.8 0.7 copy-start.18
  40.5 0.7 copy-start.19
  41.2 0.7 copy-start.20

commit v2 on v1

--- a/solution.py
+++ b/solution.py
@@ -230,81 +230,93 @@
     return jnp.concatenate([stacked[tile, rows, :] for tile in tiles], axis=1)
 
 
-def pack_kernel(slot_faces, fields_ref, codes_ref, select_ref, up_ref, down_ref, left_ref, right_ref, stacked):
+def pack_kernel(
+    slot_faces,
+    fields_ref,
+    codes_ref,
+    select_ref,
+    up_ref,
+    down_ref,
+    left_ref,
+    right_ref,
+    packed_ref,
+    stacked,
+):
     stacked[...] = jnp.zeros_like(stacked)
     high, low = stack_nodes(fields_ref, stacked)
     traces = product(select_ref[...], high) + product(select_ref[...], low)
-    chosen = jnp.zeros((64, traces.shape[1]), f32)
+    width = left_ref.shape[1]
+    reach = 8 * width
+    chosen = jnp.zeros((64, reach), f32)
     for face in range(4):
-        remote = codes_ref[face : face + 1, :] >= slot_faces
+        remote = codes_ref[face : face + 1, 0:reach] >= slot_faces
         chosen = jnp.where(remote, traces[64 * face : 64 * face + 64, :], chosen)
-    width = left_ref.shape[1]
     pieces = [chosen[:, width * heading : width * heading + width] for heading in range(8)]
     for place in range(3):
         up_ref[place] = pieces[place]
         down_ref[place] = pieces[5 + place]
     left_ref[...] = pieces[3]
     right_ref[...] = pieces[4]
-
-
-def table_kernel(slot_faces, fields_ref, codes_ref, select_ref, table_ref, packed_ref, stacked):
-    @pl.when(pl.program_id(0) == 0)
-    def _():
-        stacked[...] = jnp.zeros_like(stacked)
-
+    tiles = codes_ref.shape[1] // LANES
+    for half in range(2):
+        codes = codes_ref[2 * half : 2 * half + 2, :]
+        codes = jnp.where((codes >= 0) & (codes < slot_faces), codes, 0)
+        codes = codes[0:1] + (codes[1:2] << 16)
+        for tile in range(tiles):
+            row = half * tiles + tile
+            packed_ref[row : row + 1, :] = codes[:, LANES * tile : LANES * tile + LANES]
+
+
+def relay_kernel(left_ref, right_ref, below_ref, above_ref, to_left_ref, to_right_ref):
+    to_left_ref[0] = left_ref[...]
+    to_left_ref[1] = below_ref[0]
+    to_left_ref[2] = above_ref[0]
+    to_right_ref[0] = right_ref[...]
+    to_right_ref[1] = below_ref[2]
+    to_right_ref[2] = above_ref[2]
+
+
+def build_rows(first, fields_ref, select_ref, table_ref, stacked):
+    slot_count = table_ref.shape[0] // 4
+    width = fields_ref.shape[2]
     high, low = stack_nodes(fields_ref, stacked)
     for half in range(2):
         select = select_ref[:, 256 * half : 256 * half + 256]
         rows = product(high, select, ((0,), (0,))) + product(low, select, ((0,), (0,)))
-        table_ref[2 * half] = rows[:, :LANES]
-        table_ref[2 * half + 1] = rows[:, LANES:]
-        codes = codes_ref[2 * half : 2 * half + 2, :]
-        codes = jnp.where((codes >= 0) & (codes < slot_faces), codes, 0)
-        packed_ref[half : half + 1, :] = codes[0:1] + (codes[1:2] << 16)
-
-
-def gather_rows(slot_count, first, codes_ref, table_ref, normals_ref, outer_ref, rows_refs):
+        for side in range(2):
+            start = pl.multiple_of((2 * half + side) * slot_count + first, width)
+            table_ref[pl.ds(start, width), :] = rows[:, LANES * side : LANES * side + LANES]
+
+
+def gather_pieces(slot_count, first, codes_ref, table_ref, normals_ref, outer_ref, rows_refs):
     width = outer_ref.shape[1]
     left_half = lax.broadcasted_iota(jnp.int32, (1, LANES), 1) < 64
+
+    def load(tile, half, rows):
+        base = half * slot_count + first + tile * LANES
+        for row in rows:
+            code = codes_ref[base + row]
+            one = table_ref[pl.ds(code & 0xFFFF, 1), :]
+            two = table_ref[pl.ds(lax.shift_right_logical(code, 16), 1), :]
+            rows_refs[half][row : row + 1, :] = jnp.where(left_half, one, two)
+
+    def combine(tile, half):
+        turned = rows_refs[half][...].T
+        lanes = slice(tile * LANES, tile * LANES + LANES)
+        for side in range(2):
+            face = 2 * half + side
+            part = turned[64 * side : 64 * side + 64, :]
+            total = -part[0:16]
+            for axis_id in range(3):
+                facing = normals_ref[axis_id, face : face + 1, lanes]
+                total = total + facing * part[16 + 16 * axis_id : 32 + 16 * axis_id]
+            outer_ref[FACE_ROWS * face : FACE_ROWS * face + FACE_ROWS, lanes] = total
+
     for tile in range(width // LANES):
         for half in range(2):
-            rows_ref = rows_refs[half]
-            base = half * slot_count + first + tile * LANES
-            for row in range(LANES):
-                code = codes_ref[base + row]
-                one = table_ref[pl.ds(code & 0xFFFF, 1), :]
-                two = table_ref[pl.ds(lax.shift_right_logical(code, 16), 1), :]
-                rows_ref[row : row + 1, :] = jnp.where(left_half, one, two)
-            turned = rows_ref[...].T
-            lanes = slice(tile * LANES, tile * LANES + LANES)
-            for side in range(2):
-                face = 2 * half + side
-                part = turned[64 * side : 64 * side + 64, :]
-                total = -part[0:16]
-                for axis_id in range(3):
-                    facing = normals_ref[axis_id, face : face + 1, lanes]
-                    total = total + facing * part[16 + 16 * axis_id : 32 + 16 * axis_id]
-                outer_ref[FACE_ROWS * face : FACE_ROWS * face + FACE_ROWS, lanes] = total
-
-
-def outer_flux(traces, normals_ref, scale_ref, codes_ref, outer_ref):
-    fluxes = []
-    for face in range(4):
-        inner_p = traces[64 * face : 64 * face + 16]
-        along = jnp.zeros_like(inner_p)
-        for axis_id in range(3):
-            facing = normals_ref[axis_id, face : face + 1, :]
-            start = 64 * face + 16 + 16 * axis_id
-            along = along + facing * traces[start : start + 16]
-        wall = codes_ref[face : face + 1, :] < 0
-        beyond = outer_ref[FACE_ROWS * face : FACE_ROWS * face + FACE_ROWS, :]
-        beyond = jnp.where(wall, -along - inner_p, beyond)
-        fluxes.append((0.5 * scale_ref[face : face + 1, :]) * (along - inner_p - beyond))
-    columns = list(fluxes)
-    for axis_id in range(3):
-        for face in range(4):
-            columns.append(normals_ref[axis_id, face : face + 1, :] * fluxes[face])
-    return jnp.concatenate(columns, axis=0)
+            for part in range(2):
+                yield functools.partial(load, tile, half, range(64 * part, 64 * part + 64))
+            yield functools.partial(combine, tile, half)
 
 
 def section_kernel(
@@ -313,7 +325,6 @@
     group,
     packed_ref,
     live_ref,
-    table_ref,
     next_normals_ref,
     fields_ref,
     residue_ref,
@@ -328,6 +339,7 @@
     elems_ref,
     ids_ref,
     coords_ref,
+    table_select_ref,
     select_ref,
     into_ref,
     from_ref,
@@ -336,70 +348,143 @@
     fields_out,
     residue_out,
     spread_ref,
+    table_ref,
     stacked,
     combined,
     slow,
     rates,
     remote,
     outer,
+    beyond_ref,
     sampled,
     pressure,
     monomials,
     *rows_refs,
 ):
-    step = pl.program_id(0)
-    last = pl.num_programs(0) - 1
     width = fields_ref.shape[2]
+    tiles = slot_count // width
+    step = pl.program_id(0) - tiles
     slot_faces = 4 * slot_count
+    half_width = 256
 
     def gather():
         first = step * width
-        gather_rows(slot_count, first, packed_ref, table_ref, next_normals_ref, outer, rows_refs)
-
-    def update(beside):
+        return gather_pieces(
+            slot_count, first, packed_ref, table_ref, next_normals_ref, outer, rows_refs
+        )
+
+    def update_pieces():
         first = (step - 1) * width
-        high, low = stack_nodes(fields_ref, stacked)
-        traces = product(select_ref[...], high) + product(select_ref[...], low)
-        flux = outer_flux(traces, normals_ref, scale_ref, codes_ref, outer)
-        beside()
-        flux_hi, flux_lo = halves(flux)
-        lifted = product(lift_ref[...], flux_hi)
-        total = lifted[:ROWS] + lifted[ROWS:] + product(lift_ref[0:ROWS, :], flux_lo)
-        geometry = geometry_ref[...] * (1.0 / 3.0)
-        for axis_id in range(3):
-            weighted = jnp.zeros((NODES, width), f32)
-            for direction in range(3):
-                at = 3 * axis_id + direction
-                velocity = one_field(stacked, 1 + direction)
-                weighted = weighted + geometry[at : at + 1, :] * velocity
-            combined[PAD * axis_id : PAD * axis_id + NODES, :] = weighted
-        total = total + product(into_ref[...], jnp.concatenate(halves(combined[...]), axis=0))
-        slow[0:NODES, :] = one_field(stacked, 0)
-        slopes = product(from_ref[...], jnp.concatenate(halves(slow[...]), axis=0))
-        place = lax.broadcasted_iota(jnp.int32, (8, width), 0) & 3
-        for axis_id in range(3):
-            pattern = jnp.zeros((8, width), f32)
-            for direction in range(3):
-                at = 3 * axis_id + direction
-                pattern = jnp.where(place == direction + 1, geometry[at : at + 1, :], pattern)
-            slope = slopes[ROWS * axis_id : ROWS * axis_id + ROWS].reshape(ROWS // 8, 8, width)
-            total = total - (slope * pattern[None]).reshape(ROWS, width)
-        rates[...] = total
-        keep = lax.broadcasted_iota(jnp.int32, (1, width), 1) + first < live_ref[0]
-        for node in range(NODES):
-            rate = rates[4 * node : 4 * node + 4, :]
-            residue_next = section_decay * residue_ref[node] + time_step * rate
-            fields_next = fields_ref[node] + section_gain * residue_next
-            fields_next = jnp.where(keep, fields_next, 0.0)
-            fields_out[node] = fields_next
-            residue_out[node] = jnp.where(keep, residue_next, 0.0)
-            pressure[node : node + 1, :] = fields_next[0:1]
-        parts = jnp.concatenate(thirds(pressure[...]), axis=0)
-        slots = lax.broadcasted_iota(jnp.int32, (width, elems_ref.shape[1]), 0) + first
-        picks = jnp.where(slots == elems_ref[...], 1.0, 0.0).astype(bf16)
-        sampled[...] += product(parts, picks)
-
-    @pl.when(step == 0)
+        kept = {}
+
+        def inside(at):
+            return slice(half_width * at, half_width * at + half_width)
+
+        def traces(at):
+            lanes = inside(at)
+            for tile in range(2 * at, 2 * at + 2):
+                for node in range(NODES):
+                    stacked[tile, 4 * node : 4 * node + 4, :] = fields_ref[
+                        node, :, LANES * tile : LANES * tile + LANES
+                    ]
+            high, low = halves(jnp.concatenate([stacked[2 * at], stacked[2 * at + 1]], axis=1))
+            inner = product(select_ref[...], high) + product(select_ref[...], low)
+            fluxes = []
+            for face in range(4):
+                inner_p = inner[64 * face : 64 * face + 16]
+                along = jnp.zeros_like(inner_p)
+                for axis_id in range(3):
+                    facing = normals_ref[axis_id, face : face + 1, lanes]
+                    start = 64 * face + 16 + 16 * axis_id
+                    along = along + facing * inner[start : start + 16]
+                wall = codes_ref[face : face + 1, lanes] < 0
+                beyond = beyond_ref[FACE_ROWS * face : FACE_ROWS * face + FACE_ROWS, lanes]
+                beyond = jnp.where(wall, -along - inner_p, beyond)
+                scale = 0.5 * scale_ref[face : face + 1, lanes]
+                fluxes.append(scale * (along - inner_p - beyond))
+            kept[at] = fluxes
+
+        def lift(at):
+            lanes = inside(at)
+            fluxes = kept.pop(at)
+            columns = list(fluxes)
+            for axis_id in range(3):
+                for face in range(4):
+                    columns.append(normals_ref[axis_id, face : face + 1, lanes] * fluxes[face])
+            flux_hi, flux_lo = halves(jnp.concatenate(columns, axis=0))
+            lifted = product(lift_ref[...], flux_hi)
+            total = lifted[:ROWS] + lifted[ROWS:] + product(lift_ref[0:ROWS, :], flux_lo)
+            rates[:, lanes] = total
+
+        def field_rows(at, field):
+            rows = pl.ds(field, NODES, stride=4)
+            return jnp.concatenate([stacked[tile, rows, :] for tile in (2 * at, 2 * at + 1)], axis=1)
+
+        def into(at):
+            lanes = inside(at)
+            geometry = geometry_ref[:, lanes] * (1.0 / 3.0)
+            for axis_id in range(3):
+                weighted = jnp.zeros((NODES, half_width), f32)
+                for direction in range(3):
+                    row = 3 * axis_id + direction
+                    weighted = weighted + geometry[row : row + 1, :] * field_rows(at, 1 + direction)
+                combined[PAD * axis_id : PAD * axis_id + NODES, lanes] = weighted
+            parts = jnp.concatenate(halves(combined[:, lanes]), axis=0)
+            rates[:, lanes] += product(into_ref[...], parts)
+
+        def slopes(at):
+            lanes = inside(at)
+            geometry = geometry_ref[:, lanes] * (1.0 / 3.0)
+            slow[0:NODES, lanes] = field_rows(at, 0)
+            parts = jnp.concatenate(halves(slow[:, lanes]), axis=0)
+            place = lax.broadcasted_iota(jnp.int32, (8, half_width), 0) & 3
+            total = rates[:, lanes]
+            for axis_id in range(3):
+                slope = product(from_ref[ROWS * axis_id : ROWS * axis_id + ROWS, :], parts)
+                pattern = jnp.zeros((8, half_width), f32)
+                for direction in range(3):
+                    row = 3 * axis_id + direction
+                    pattern = jnp.where(place == direction + 1, geometry[row : row + 1, :], pattern)
+                slope = slope.reshape(ROWS // 8, 8, half_width) * pattern[None]
+                total = total - slope.reshape(ROWS, half_width)
+            rates[:, lanes] = total
+
+        def advance(at):
+            lanes = inside(at)
+            slots = lax.broadcasted_iota(jnp.int32, (1, half_width), 1) + (first + half_width * at)
+            keep = slots < live_ref[0]
+            for node in range(NODES):
+                rate = rates[4 * node : 4 * node + 4, lanes]
+                residue_next = section_decay * residue_ref[node, :, lanes] + time_step * rate
+                fields_next = fields_ref[node, :, lanes] + section_gain * residue_next
+                fields_next = jnp.where(keep, fields_next, 0.0)
+                fields_out[node, :, lanes] = fields_next
+                residue_out[node, :, lanes] = jnp.where(keep, residue_next, 0.0)
+                pressure[node : node + 1, lanes] = fields_next[0:1]
+
+        def sample(at):
+            lanes = inside(at)
+            parts = jnp.concatenate(thirds(pressure[:, lanes]), axis=0)
+            start = first + half_width * at
+            slots = lax.broadcasted_iota(jnp.int32, (half_width, elems_ref.shape[1]), 0) + start
+            picks = jnp.where(slots == elems_ref[...], 1.0, 0.0).astype(bf16)
+            sampled[...] += product(parts, picks)
+
+        for at in range(width // half_width):
+            for piece in (traces, lift, into, slopes, advance, sample):
+                yield functools.partial(piece, at)
+
+    def interleave(gathers, updates):
+        gathers, updates = list(gathers), list(updates)
+        done = 0
+        for at, piece in enumerate(gathers):
+            piece()
+            upto = (at + 1) * len(updates) // len(gathers)
+            for other in updates[done:upto]:
+                other()
+            done = upto
+
+    @pl.when(step == -tiles)
     def _():
         stacked[...] = jnp.zeros_like(stacked)
         combined[...] = jnp.zeros_like(combined)
@@ -421,7 +506,15 @@
         ]
         for heading in range(8):
             remote[:, count * heading : count * heading + count] = sources[heading]
-        gather()
+
+    @pl.when(step < 0)
+    def _():
+        build_rows((step + tiles) * width, fields_ref, table_select_ref, table_ref, stacked)
+
+    @pl.when(step == 0)
+    def _():
+        for piece in gather():
+            piece()
 
     @pl.when((step > 0) & ((step - 1) * width < 8 * right_ref.shape[2]))
     def _():
@@ -435,13 +528,16 @@
             is_remote = codes_ref[face : face + 1, :] >= slot_faces
             outer[rows, :] = jnp.where(is_remote, total, outer[rows, :])
 
-    @pl.when((step > 0) & (step < last))
+    @pl.when((step > 0) & (step < tiles))
     def _():
-        update(gather)
-
-    @pl.when(step == last)
+        beyond_ref[...] = outer[...]
+        interleave(gather(), update_pieces())
+
+    @pl.when(step == tiles)
     def _():
-        update(lambda: None)
+        beyond_ref[...] = outer[...]
+        for piece in update_pieces():
+            piece()
         ladders = []
         for axis_id in range(3):
             base = coords_ref[axis_id : axis_id + 1, :]
@@ -482,6 +578,10 @@
     )
 
 
+def in_hbm(array):
+    return pltpu.with_memory_space_constraint(array, pltpu.HBM)
+
+
 def fixed(shape):
     return pl.BlockSpec(shape, lambda *_: (0,) * len(shape))
 
@@ -499,9 +599,14 @@
     sample_elems,
     sample_coords,
 ):
-    const = constant_tables()
-    fields = jnp.transpose(fields, (1, 0, 2))
-    residue = jnp.transpose(residue, (1, 0, 2))
+    const = {
+        name: in_hbm(table) if isinstance(table, jax.Array) else table
+        for name, table in constant_tables().items()
+    }
+    fields = in_hbm(jnp.transpose(fields, (1, 0, 2)))
+    residue = in_hbm(jnp.transpose(residue, (1, 0, 2)))
+    geometry, normals, face_scale = in_hbm(geometry), in_hbm(normals), in_hbm(face_scale)
+    neighbours, sample_coords = in_hbm(neighbours), in_hbm(sample_coords)
     slot_count = fields.shape[2]
     slot_faces = 4 * slot_count
     bound_count = send_faces.shape[1]
@@ -510,25 +615,31 @@
     devices = lax.axis_size(("px", "py"))
     shape = jax.ShapeDtypeStruct
 
-    up, down, left, right = pl.pallas_call(
+    width = 512
+    tiles = slot_count // width
+    piece = (3, 64, bound_count)
+
+    up, down, left, right, packed = pl.pallas_call(
         functools.partial(pack_kernel, slot_faces),
         grid=(1,),
         in_specs=[
             pl.BlockSpec((NODES, 4, reach), lambda t: (0, 0, 0)),
-            pl.BlockSpec((4, reach), lambda t: (0, 0)),
+            fixed((4, slot_count)),
             fixed((256, ROWS)),
         ],
         out_specs=[
-            fixed((3, 64, bound_count)),
-            fixed((3, 64, bound_count)),
-            fixed((64, bound_count)),
-            fixed((64, bound_count)),
+            fixed(piece),
+            fixed(piece),
+            fixed(piece[1:]),
+            fixed(piece[1:]),
+            fixed((2 * slot_count // LANES, LANES)),
         ],
         out_shape=[
-            shape((3, 64, bound_count), f32),
-            shape((3, 64, bound_count), f32),
-            shape((64, bound_count), f32),
-            shape((64, bound_count), f32),
+            shape(piece, f32),
+            shape(piece, f32),
+            shape(piece[1:], f32),
+            shape(piece[1:], f32),
+            shape((2 * slot_count // LANES, LANES), jnp.int32),
         ],
         scratch_shapes=[pltpu.VMEM((reach // LANES, ROWS, LANES), f32)],
         compiler_params=pltpu.CompilerParams(vmem_limit_bytes=16 << 20),
@@ -541,68 +652,47 @@
         return forward, [(target, source) for source, target in forward]
 
     forward, backward = steps_along("px")
-    below = lax.ppermute(up, "px", backward)
-    above = lax.ppermute(down, "px", forward)
-
-    width = 768
-    table, packed = pl.pallas_call(
-        functools.partial(table_kernel, slot_faces),
-        grid=(slot_count // width,),
-        in_specs=[
-            pl.BlockSpec((NODES, 4, width), lambda t: (0, 0, t)),
-            pl.BlockSpec((4, width), lambda t: (0, t)),
-            fixed((ROWS, 4 * LANES)),
-        ],
-        out_specs=[
-            pl.BlockSpec((4, width, LANES), lambda t: (0, t, 0)),
-            pl.BlockSpec((2, width), lambda t: (0, t)),
-        ],
-        out_shape=[
-            shape((4, slot_count, LANES), f32),
-            shape((2, slot_count), jnp.int32),
-        ],
-        scratch_shapes=[pltpu.VMEM((width // LANES, ROWS, LANES), f32)],
-        compiler_params=pltpu.CompilerParams(vmem_limit_bytes=24 << 20),
-        name="table",
-    )(fields, neighbours, const["table_select"])
-    table = table.reshape(slot_faces, LANES)
-
+    below = in_hbm(lax.ppermute(up, "px", backward))
+    above = in_hbm(lax.ppermute(down, "px", forward))
+    to_left, to_right = pl.pallas_call(
+        relay_kernel,
+        out_shape=[shape(piece, f32), shape(piece, f32)],
+        name="relay",
+    )(in_hbm(left), in_hbm(right), below, above)
     forward, backward = steps_along("py")
-    to_left = jnp.concatenate([left[None], below[0:1], above[0:1]])
-    to_right = jnp.concatenate([right[None], below[2:3], above[2:3]])
-    from_right = lax.ppermute(to_left, "py", backward)
-    from_left = lax.ppermute(to_right, "py", forward)
-
-    width = 512
-    steps = slot_count // width
+    from_right = in_hbm(lax.ppermute(to_left, "py", backward))
+    from_left = in_hbm(lax.ppermute(to_right, "py", forward))
 
     def behind(rank):
-        return lambda t, *_: (0,) * rank + (jnp.maximum(t - 1, 0),)
+        return lambda t, *_: (0,) * rank + (jnp.maximum(t - tiles - 1, 0),)
 
     def ahead(rank):
-        return lambda t, *_: (0,) * rank + (jnp.minimum(t, steps - 1),)
+        return lambda t, *_: (0,) * rank + (jnp.clip(t - tiles, 0, tiles - 1),)
+
+    def twice(t, *_):
+        return (0, 0, jnp.where(t < tiles, t, jnp.maximum(t - tiles - 1, 0)))
 
     fields_next, residue_next, spread = pl.pallas_call(
         functools.partial(section_kernel, slot_count, const["powers"], samples),
         grid_spec=pltpu.PrefetchScalarGridSpec(
             num_scalar_prefetch=2,
-            grid=(steps + 1,),
+            grid=(2 * tiles + 1,),
             in_specs=[
-                pl.BlockSpec(memory_space=pltpu.VMEM),
                 pl.BlockSpec((3, 4, width), ahead(2)),
-                pl.BlockSpec((NODES, 4, width), behind(2)),
+                pl.BlockSpec((NODES, 4, width), twice),
                 pl.BlockSpec((NODES, 4, width), behind(2)),
                 pl.BlockSpec((9, width), behind(1)),
                 pl.BlockSpec((3, 4, width), behind(2)),
                 pl.BlockSpec((4, width), behind(1)),
                 pl.BlockSpec((4, width), behind(1)),
-                fixed((3, 64, bound_count)),
-                fixed((3, 64, bound_count)),
-                fixed((3, 64, bound_count)),
-                fixed((3, 64, bound_count)),
+                fixed(piece),
+                fixed(piece),
+                fixed(piece),
+                fixed(piece),
                 fixed((1, samples)),
                 fixed((1, samples)),
                 fixed((3, samples)),
+                fixed((ROWS, 4 * LANES)),
                 fixed((256, ROWS)),
                 fixed((ROWS, 256)),
                 fixed((3 * ROWS, 96)),
@@ -615,11 +705,13 @@
                 fixed((devices, 1, samples)),
             ],
             scratch_shapes=[
+                pltpu.VMEM((slot_faces, LANES), f32),
                 pltpu.VMEM((width // LANES, ROWS, LANES), f32),
                 pltpu.VMEM((128, width), f32),
                 pltpu.VMEM((48, width), f32),
                 pltpu.VMEM((ROWS, width), f32),
                 pltpu.VMEM((64, pl.cdiv(reach, width) * width), f32),
+                pltpu.VMEM((64, width), f32),
                 pltpu.VMEM((64, width), f32),
                 pltpu.VMEM((144, samples), f32),
                 pltpu.VMEM((48, width), f32),
@@ -633,12 +725,11 @@
             shape(residue.shape, f32),
             shape((devices, 1, samples), f32),
         ],
-        compiler_params=pltpu.CompilerParams(vmem_limit_bytes=32 << 20),
+        compiler_params=pltpu.CompilerParams(vmem_limit_bytes=48 << 20),
         name="section",
     )(
         packed.reshape(-1),
         live_counts,
-        table,
         normals,
         fields,
         residue,
@@ -650,9 +741,10 @@
         from_left,
         below,
         above,
-        sample_elems.reshape(1, samples),
-        sample_ids.reshape(1, samples),
+        in_hbm(sample_elems.reshape(1, samples)),
+        in_hbm(sample_ids.reshape(1, samples)),
         sample_coords,
+        const["table_select"],
         const["trace_select"],
         const["into_p"],
         const["from_p"],

time: 96.9 us -> 87.1 us (0.90)
  local copies, waits for them, and re-layouts: 19.6 us -> 2.52 us
  Pallas kernels: 36.4 us -> 42.8 us
  blocking collectives: 23.4 us -> 25.1 us
  waiting for transfers between devices: 1.62 us -> 3.22 us
  other arithmetic: 1.3 us -> 0 us
    unnamed x42 -> x12, local copies, waits for them, and re-layouts: 18.8 us -> 2.52 us
    pallas_call x1, Pallas kernels: 29.2 us -> 37.7 us  [local(): pl.pallas_call(functools.partial(section_kernel, slot_count, const['power...]
    pallas_call x1, Pallas kernels: 4.82 us -> 1.66 us  [local(): pl.pallas_call(relay_kernel, out_shape=[shape(piece, f32), shape(piece, f...]
    all_to_all x1, blocking collectives: 23.4 us -> 25.1 us  [local(): received = lax.all_to_all(spread, ('px', 'py'), 0, 0, tiled=True)]
    ppermute x4, waiting for transfers between devices: 1.62 us -> 3.22 us  [the longest x1 1.6 us: local(): from_left = in_hbm(lax.ppermute(to_right, 'py', forward))]
    concatenate x2 -> x0, other arithmetic: 1.3 us -> none  [the longest x1 0.65 us: local(): to_right = jnp.concatenate([right[None], below[2:3], above[2:3]])]
    pallas_call x1, Pallas kernels: 0.59 us -> 1.66 us  [local(): pl.pallas_call(functools.partial(pack_kernel, slot_faces), grid=(1,), in_...]
  transfers between devices with their start and end apart: 4 -> 4, of which waited for: 2 -> 3; matrix products, arithmetic and copies ran while one was open for 2% -> 0% of each run, Pallas kernels for 5% -> 0%
where the time goes in v2:
time: 87.1 us; the launch traced here: 86.7 us
  Pallas kernels  42.8 us (49%)
  blocking collectives  25.1 us (29%)
  starting transfers between devices  11.7 us (13%)
  waiting for transfers between devices  3.22 us (4%)
  local copies, waits for them, and re-layouts  2.52 us (3%)
  between operations  1.35 us (2%)
    pallas_call x1, Pallas kernels, local(): pl.pallas_call(functools.partial(section_kernel, slot_count, const['power...  37.7 us
    all_to_all x1, blocking collectives, local(): received = lax.all_to_all(spread, ('px', 'py'), 0, 0, tiled=True)  25.1 us
    ppermute x1, starting transfers between devices, local(): from_left = in_hbm(lax.ppermute(to_right, 'py', forward))  3.99 us
    ppermute x1, starting transfers between devices, local(): below = in_hbm(lax.ppermute(up, 'px', backward))  3.32 us
    ppermute x1, starting transfers between devices, local(): above = in_hbm(lax.ppermute(down, 'px', forward))  3.1 us
    unnamed x12, local copies, waits for them, and re-layouts  2.52 us
    pallas_call x1, Pallas kernels, local(): pl.pallas_call(harmonic_kernel, out_shape=shape((receivers, harmonic.shap...  1.79 us
  transfers between devices with their start and end apart: 4, of which 3 were waited for; matrix products, arithmetic and copies ran while one was open for 0% of the time, Pallas kernels for 0%

profile of v2, /device:TPU:1, one launch (start us, length us, event | category | flops | bytes accessed | tf_op | source)
XLA Modules:
  0.0 86.7 jit_solution(9640452560107113171)
XLA Ops:
  0.6 1.7 %pack.1 = (f32[3,64,96]{2,1,0:T(8,128)S(1)}, f32[3,64,96]{2,1,0:T(8,128)S(1)}, f32[64,96]{1,0:T(8,128)S(1)}, f32[64,96]{1,0:T(8,128)S(1)}, s32[72,128]{1,0:T(8,128)S(1)}) custom-call(f32[35,4,4608]{2,1,0:T(4,128)} %bitcast.9, s32[4,4608]{1,0:T(4,128)} %codes_ref.3, bf16[256,144]{1,0:T(8,128)(2,1)} %constant.17.clone.select_ref), custom_call_target="tpu_custom_call" | custom-call | tf_op jit(solution)/shard_map/pack/pallas_call | solution.py:622
  2.3 0.0 copy-start
  2.3 0.6 copy-done
  2.9 0.0 copy-start.1
  2.9 0.6 copy-done.1
  3.5 3.3 %collective-permute-start = (f32[3,64,96]{2,1,0:T(8,128)S(1)}, f32[3,64,96]{2,1,0:T(8,128)S(1)}, u32[]{:S(2)}, u32[]{:S(2)}) collective-permute-start(f32[3,64,96]{2,1,0:T(8,128)S(1)} %get-tuple-element.16), channel_id=1, source_target_pairs={{16,0},{32,16},{48,32},{64,48},{80,64},{96,80},{112,96},{17,1},{33... | collective-permute-start | bytes 221192 | tf_op jit(solution)/shard_map/ppermute | solution.py:655
  6.9 3.1 %collective-permute-start.1 = (f32[3,64,96]{2,1,0:T(8,128)S(1)}, f32[3,64,96]{2,1,0:T(8,128)S(1)}, u32[]{:S(2)}, u32[]{:S(2)}) collective-permute-start(f32[3,64,96]{2,1,0:T(8,128)S(1)} %get-tuple-element.17), channel_id=1, source_target_pairs={{0,16},{16,32},{32,48},{48,64},{64,80},{80,96},{96,112},{1,17},{17... | collective-permute-start | bytes 221192 | tf_op jit(solution)/shard_map/ppermute | solution.py:656
  10.0 0.4 collective-permute-done.below_ref
  10.3 0.0 copy-start.2
  10.3 1.3 %collective-permute-done.1.above_ref = f32[3,64,96]{2,1,0:T(8,128)S(1)} collective-permute-done((f32[3,64,96]{2,1,0:T(8,128)S(1)}, f32[3,64,96]{2,1,0:T(8,128)S(1)}, u32[]{:S(2)}, u32[]{:S(2)}) %collective-permute-start.1) | collective-permute-done | bytes 73760 | tf_op jit(solution)/shard_map/ppermute | solution.py:656
  11.6 0.0 copy-start.3
  11.6 0.0 copy-done.2
  11.6 0.6 copy-done.3
  12.2 1.7 %relay.1 = (f32[3,64,96]{2,1,0:T(8,128)}, f32[3,64,96]{2,1,0:T(8,128)}) custom-call(f32[64,96]{1,0:T(8,128)} %copy-done, f32[64,96]{1,0:T(8,128)} %copy-done.1, f32[3,64,96]{2,1,0:T(8,128)} %copy-done.2, f32[3,64,96]{2,1,0:T(8,128)} %copy-done.3), custom_call_target="tpu_custom_call" | custom-call | tf_op jit(solution)/shard_map/relay/pallas_call | solution.py:657
  13.9 1.3 %collective-permute-start.2 = (f32[3,64,96]{2,1,0:T(8,128)}, f32[3,64,96]{2,1,0:T(8,128)S(1)}, u32[]{:S(2)}, u32[]{:S(2)}) collective-permute-start(f32[3,64,96]{2,1,0:T(8,128)} %get-tuple-element.18), channel_id=1, source_target_pairs={{1,0},{2,1},{3,2},{4,3},{5,4},{6,5},{7,6},{8,7},{9,8},{10,9},{11,1... | collective-permute-start | bytes 221192 | tf_op jit(solution)/shard_map/ppermute | solution.py:663
  15.2 4.0 %collective-permute-start.3 = (f32[3,64,96]{2,1,0:T(8,128)}, f32[3,64,96]{2,1,0:T(8,128)S(1)}, u32[]{:S(2)}, u32[]{:S(2)}) collective-permute-start(f32[3,64,96]{2,1,0:T(8,128)} %get-tuple-element.19), channel_id=1, source_target_pairs={{0,1},{1,2},{2,3},{3,4},{4,5},{5,6},{6,7},{7,8},{8,9},{9,10},{10,1... | collective-permute-start | bytes 221192 | tf_op jit(solution)/shard_map/ppermute | solution.py:664
  19.8 0.0 collective-permute-done.2.right_ref
  19.8 0.0 copy-start.4
  19.8 1.6 %collective-permute-done.3.left_ref = f32[3,64,96]{2,1,0:T(8,128)S(1)} collective-permute-done((f32[3,64,96]{2,1,0:T(8,128)}, f32[3,64,96]{2,1,0:T(8,128)S(1)}, u32[]{:S(2)}, u32[]{:S(2)}) %collective-permute-start.3) | collective-permute-done | bytes 73760 | tf_op jit(solution)/shard_map/ppermute | solution.py:664
  21.4 0.0 copy-start.5
  21.4 0.0 copy-done.4
  21.4 0.6 copy-done.5
  22.1 37.7 %section.1 = (f32[35,4,4608]{2,1,0:T(4,128)}, f32[35,4,4608]{2,1,0:T(4,128)}, f32[128,1,200]{2,1,0:T(1,128)S(1)}) custom-call(s32[9216]{0:T(1024)S(1)} %bitcast.8, s32[1]{0:T(128)S(6)} %copy.21.live_ref, f32[3,4,4608]{2,1,0:T(4,128)} %normals_ref.1, f32[35,4,4608]{2,1,0:T(4,128)} %bitcast.10, f32[35,4,4608]{2,1,0:T(4,128)} %bitcast.11, ...), custom_call_target="tpu_custom_call" | custom-call | tf_op jit(solution)/shard_map/section/pallas_call | solution.py:675
  59.8 25.1 %all_to_all.5.received_ref = f32[128,1,200]{2,1,0:T(1,128)} all-to-all(f32[128,1,200]{2,1,0:T(1,128)S(1)} %get-tuple-element.22), channel_id=1, replica_groups=mesh['px'=8,'py'=16] {'px','py'}, dimensions={0} | all-to-all | bytes 204800 | tf_op jit(solution)/shard_map/all_to_all | solution.py:754
  84.9 1.8 %harmonic.1 = f32[4,25]{1,0:T(4,128)} custom-call(f32[128,1,200]{2,1,0:T(1,128)} %all_to_all.5.received_ref, f32[25,200]{1,0:T(8,128)} %constant.22.clone.table_ref, f32[4,200]{1,0:T(4,128)} %constant.23.clone.groups_ref), custom_call_target="tpu_custom_call" | custom-call | tf_op jit(solution)/shard_map/harmonic/pallas_call | solution.py:759
Async XLA Ops:
  2.3 0.6 copy-start
  2.9 0.6 copy-start.1
  3.5 6.8 %collective-permute-start = (f32[3,64,96]{2,1,0:T(8,128)S(1)}, f32[3,64,96]{2,1,0:T(8,128)S(1)}, u32[]{:S(2)}, u32[]{:S(2)}) collective-permute-start(f32[3,64,96]{2,1,0:T(8,128)S(1)} %get-tuple-element.16), channel_id=1, source_target_pairs={{16,0},{32,16},{48,32},{64,48},{80,64},{96,80},{112,96},{17,1},{33... | collective-permute-start | bytes 221192 | tf_op jit(solution)/shard_map/ppermute | solution.py:655
  6.9 4.7 %collective-permute-start.1 = (f32[3,64,96]{2,1,0:T(8,128)S(1)}, f32[3,64,96]{2,1,0:T(8,128)S(1)}, u32[]{:S(2)}, u32[]{:S(2)}) collective-permute-start(f32[3,64,96]{2,1,0:T(8,128)S(1)} %get-tuple-element.17), channel_id=1, source_target_pairs={{0,16},{16,32},{32,48},{48,64},{64,80},{80,96},{96,112},{1,17},{17... | collective-permute-start | bytes 221192 | tf_op jit(solution)/shard_map/ppermute | solution.py:656
  10.3 1.3 %copy-start.2 = (f32[3,64,96]{2,1,0:T(8,128)}, f32[3,64,96]{2,1,0:T(8,128)S(1)}, u32[]{:S(2)}) copy-start(f32[3,64,96]{2,1,0:T(8,128)S(1)} %collective-permute-done.below_ref) | copy-start | bytes 221188
  11.6 0.6 copy-start.3
  13.9 5.9 %collective-permute-start.2 = (f32[3,64,96]{2,1,0:T(8,128)}, f32[3,64,96]{2,1,0:T(8,128)S(1)}, u32[]{:S(2)}, u32[]{:S(2)}) collective-permute-start(f32[3,64,96]{2,1,0:T(8,128)} %get-tuple-element.18), channel_id=1, source_target_pairs={{1,0},{2,1},{3,2},{4,3},{5,4},{6,5},{7,6},{8,7},{9,8},{10,9},{11,1... | collective-permute-start | bytes 221192 | tf_op jit(solution)/shard_map/ppermute | solution.py:663
  15.2 6.3 %collective-permute-start.3 = (f32[3,64,96]{2,1,0:T(8,128)}, f32[3,64,96]{2,1,0:T(8,128)S(1)}, u32[]{:S(2)}, u32[]{:S(2)}) collective-permute-start(f32[3,64,96]{2,1,0:T(8,128)} %get-tuple-element.19), channel_id=1, source_target_pairs={{0,1},{1,2},{2,3},{3,4},{4,5},{5,6},{6,7},{7,8},{8,9},{9,10},{10,1... | collective-permute-start | bytes 221192 | tf_op jit(solution)/shard_map/ppermute | solution.py:664
  19.8 1.6 %copy-start.4 = (f32[3,64,96]{2,1,0:T(8,128)}, f32[3,64,96]{2,1,0:T(8,128)S(1)}, u32[]{:S(2)}) copy-start(f32[3,64,96]{2,1,0:T(8,128)S(1)} %collective-permute-done.2.right_ref) | copy-start | bytes 221188
  21.4 0.6 copy-start.5

commit v3 on v2

--- a/solution.py
+++ b/solution.py
@@ -190,9 +190,13 @@
     return {
         "table_select": jnp.asarray(table_select, bf16),
         "trace_select": jnp.asarray(trace_select, bf16),
-        "into_p": jnp.asarray(np.concatenate([into_p, into_p], axis=1), bf16),
+        "twice_select": jnp.asarray(np.concatenate([trace_select] * 2, axis=1), bf16),
         "from_p": jnp.asarray(np.concatenate([from_p, from_p], axis=1), bf16),
-        "lift": jnp.asarray(np.concatenate([lift_hi, lift_lo], axis=0)),
+        "lift": jnp.asarray(
+            np.concatenate(
+                [lift_hi, lift_lo, lift_hi] + [into_p.astype(jnp.bfloat16)] * 2, axis=1
+            )
+        ),
         "inverse": jnp.asarray(np.pad(inverse.T, ((0, 5), (0, 5))), f32),
         "powers": powers,
     }
@@ -239,69 +243,73 @@
     down_ref,
     left_ref,
     right_ref,
-    packed_ref,
+    faces_ref,
     stacked,
 ):
     stacked[...] = jnp.zeros_like(stacked)
     high, low = stack_nodes(fields_ref, stacked)
     traces = product(select_ref[...], high) + product(select_ref[...], low)
-    width = left_ref.shape[1]
-    reach = 8 * width
+    reach = fields_ref.shape[2]
+    count = reach // 8
     chosen = jnp.zeros((64, reach), f32)
     for face in range(4):
         remote = codes_ref[face : face + 1, 0:reach] >= slot_faces
         chosen = jnp.where(remote, traces[64 * face : 64 * face + 64, :], chosen)
-    pieces = [chosen[:, width * heading : width * heading + width] for heading in range(8)]
-    for place in range(3):
-        up_ref[place] = pieces[place]
-        down_ref[place] = pieces[5 + place]
-    left_ref[...] = pieces[3]
-    right_ref[...] = pieces[4]
+    homes = [up_ref.at[0], up_ref.at[1], up_ref.at[2], left_ref, right_ref]
+    homes += [down_ref.at[0], down_ref.at[1], down_ref.at[2]]
+    for heading, home in enumerate(homes):
+        part = chosen[:, count * heading : count * heading + count]
+        home[:, 0:96] = part[0:48]
+        for third in range(3):
+            home[16 * third : 16 * third + 16, 96:128] = part[48:64, 32 * third : 32 * third + 32]
     tiles = codes_ref.shape[1] // LANES
-    for half in range(2):
-        codes = codes_ref[2 * half : 2 * half + 2, :]
-        codes = jnp.where((codes >= 0) & (codes < slot_faces), codes, 0)
-        codes = codes[0:1] + (codes[1:2] << 16)
+    codes = codes_ref[...]
+    codes = jnp.where((codes >= 0) & (codes < slot_faces), codes, 0)
+    for face in range(4):
         for tile in range(tiles):
-            row = half * tiles + tile
-            packed_ref[row : row + 1, :] = codes[:, LANES * tile : LANES * tile + LANES]
-
-
-def relay_kernel(left_ref, right_ref, below_ref, above_ref, to_left_ref, to_right_ref):
+            row = face * tiles + tile
+            faces_ref[row : row + 1, :] = codes[
+                face : face + 1, LANES * tile : LANES * tile + LANES
+            ]
+
+
+def relay_kernel(left_ref, right_ref, below_ref, above_ref, to_left_ref, to_right_ref, middle_ref):
     to_left_ref[0] = left_ref[...]
     to_left_ref[1] = below_ref[0]
     to_left_ref[2] = above_ref[0]
     to_right_ref[0] = right_ref[...]
     to_right_ref[1] = below_ref[2]
     to_right_ref[2] = above_ref[2]
-
-
-def build_rows(first, fields_ref, select_ref, table_ref, stacked):
+    middle_ref[0] = below_ref[1]
+    middle_ref[1] = above_ref[1]
+
+
+def build_rows(first, part, fields_ref, select_ref, table_ref, stacked):
     slot_count = table_ref.shape[0] // 4
-    width = fields_ref.shape[2]
-    high, low = stack_nodes(fields_ref, stacked)
+    width = LANES * stacked.shape[0]
+    high, low = stack_nodes(fields_ref.at[:, :, width * part : width * part + width], stacked)
     for half in range(2):
         select = select_ref[:, 256 * half : 256 * half + 256]
         rows = product(high, select, ((0,), (0,))) + product(low, select, ((0,), (0,)))
         for side in range(2):
-            start = pl.multiple_of((2 * half + side) * slot_count + first, width)
+            start = pl.multiple_of((2 * half + side) * slot_count + first + width * part, width)
             table_ref[pl.ds(start, width), :] = rows[:, LANES * side : LANES * side + LANES]
 
 
-def gather_pieces(slot_count, first, codes_ref, table_ref, normals_ref, outer_ref, rows_refs):
+def gather_pieces(slot_count, first, faces_ref, table_ref, normals_ref, outer_ref, rows_refs):
     width = outer_ref.shape[1]
     left_half = lax.broadcasted_iota(jnp.int32, (1, LANES), 1) < 64
 
-    def load(tile, half, rows):
-        base = half * slot_count + first + tile * LANES
+    def load(lists, tile, rows):
         for row in rows:
-            code = codes_ref[base + row]
-            one = table_ref[pl.ds(code & 0xFFFF, 1), :]
-            two = table_ref[pl.ds(lax.shift_right_logical(code, 16), 1), :]
-            rows_refs[half][row : row + 1, :] = jnp.where(left_half, one, two)
+            for half in range(2):
+                one = table_ref[pl.ds(lists[2 * half][row], 1), :]
+                two = table_ref[pl.ds(lists[2 * half + 1][row], 1), :]
+                rows_ref = rows_refs[2 * (tile % 2) + half]
+                rows_ref[row : row + 1, :] = jnp.where(left_half, one, two)
 
     def combine(tile, half):
-        turned = rows_refs[half][...].T
+        turned = rows_refs[2 * (tile % 2) + half][...].T
         lanes = slice(tile * LANES, tile * LANES + LANES)
         for side in range(2):
             face = 2 * half + side
@@ -313,19 +321,26 @@
             outer_ref[FACE_ROWS * face : FACE_ROWS * face + FACE_ROWS, lanes] = total
 
     for tile in range(width // LANES):
-        for half in range(2):
-            for part in range(2):
-                yield functools.partial(load, tile, half, range(64 * part, 64 * part + 64))
-            yield functools.partial(combine, tile, half)
+        base = first + tile * LANES
+        lists = [faces_ref.at[pl.ds(base + face * slot_count, LANES)] for face in range(4)]
+        for part in range(8):
+            rows = range(16 * part, 16 * part + 16)
+            yield functools.partial(load, lists, tile, rows)
+            if tile > 0 and part < 2:
+                yield functools.partial(combine, tile - 1, part)
+    for half in range(2):
+        yield functools.partial(combine, tile, half)
 
 
 def section_kernel(
     slot_count,
+    bound_count,
     powers,
     group,
-    packed_ref,
+    faces_ref,
     live_ref,
     next_normals_ref,
+    bulk_ref,
     fields_ref,
     residue_ref,
     geometry_ref,
@@ -334,14 +349,12 @@
     codes_ref,
     right_ref,
     left_ref,
-    below_ref,
-    above_ref,
+    middle_ref,
     elems_ref,
     ids_ref,
     coords_ref,
     table_select_ref,
     select_ref,
-    into_ref,
     from_ref,
     lift_ref,
     inverse_ref,
@@ -359,101 +372,120 @@
     sampled,
     pressure,
     monomials,
+    fields_split,
+    slow_split,
+    inner,
+    sources,
     *rows_refs,
 ):
     width = fields_ref.shape[2]
     tiles = slot_count // width
-    step = pl.program_id(0) - tiles
+    bulks = slot_count // bulk_ref.shape[2]
+    step = pl.program_id(0) - bulks
     slot_faces = 4 * slot_count
     half_width = 256
 
     def gather():
         first = step * width
         return gather_pieces(
-            slot_count, first, packed_ref, table_ref, next_normals_ref, outer, rows_refs
+            slot_count, first, faces_ref, table_ref, next_normals_ref, outer, rows_refs
         )
 
     def update_pieces():
         first = (step - 1) * width
-        kept = {}
-
-        def inside(at):
-            return slice(half_width * at, half_width * at + half_width)
-
-        def traces(at):
-            lanes = inside(at)
+
+        def stack(at, low, high):
             for tile in range(2 * at, 2 * at + 2):
-                for node in range(NODES):
+                for node in range(low, high):
                     stacked[tile, 4 * node : 4 * node + 4, :] = fields_ref[
                         node, :, LANES * tile : LANES * tile + LANES
                     ]
-            high, low = halves(jnp.concatenate([stacked[2 * at], stacked[2 * at + 1]], axis=1))
-            inner = product(select_ref[...], high) + product(select_ref[...], low)
-            fluxes = []
-            for face in range(4):
-                inner_p = inner[64 * face : 64 * face + 16]
-                along = jnp.zeros_like(inner_p)
-                for axis_id in range(3):
-                    facing = normals_ref[axis_id, face : face + 1, lanes]
-                    start = 64 * face + 16 + 16 * axis_id
-                    along = along + facing * inner[start : start + 16]
-                wall = codes_ref[face : face + 1, lanes] < 0
-                beyond = beyond_ref[FACE_ROWS * face : FACE_ROWS * face + FACE_ROWS, lanes]
-                beyond = jnp.where(wall, -along - inner_p, beyond)
-                scale = 0.5 * scale_ref[face : face + 1, lanes]
-                fluxes.append(scale * (along - inner_p - beyond))
-            kept[at] = fluxes
-
-        def lift(at):
-            lanes = inside(at)
-            fluxes = kept.pop(at)
-            columns = list(fluxes)
-            for axis_id in range(3):
-                for face in range(4):
-                    columns.append(normals_ref[axis_id, face : face + 1, lanes] * fluxes[face])
-            flux_hi, flux_lo = halves(jnp.concatenate(columns, axis=0))
-            lifted = product(lift_ref[...], flux_hi)
-            total = lifted[:ROWS] + lifted[ROWS:] + product(lift_ref[0:ROWS, :], flux_lo)
-            rates[:, lanes] = total
+
+        def split(at):
+            for side in range(2):
+                lanes = slice(LANES * side, LANES * side + LANES)
+                high, low = halves(stacked[2 * at + side])
+                fields_split[at, 0:ROWS, lanes] = high
+                fields_split[at, ROWS : 2 * ROWS, lanes] = low
+
+        def inside(at):
+            return slice(half_width * at, half_width * at + half_width)
 
         def field_rows(at, field):
             rows = pl.ds(field, NODES, stride=4)
             return jnp.concatenate([stacked[tile, rows, :] for tile in (2 * at, 2 * at + 1)], axis=1)
 
-        def into(at):
+        def copy_slow(at):
             lanes = inside(at)
-            geometry = geometry_ref[:, lanes] * (1.0 / 3.0)
+            slow[0:NODES, lanes] = field_rows(at, 0)
+            slow_split[at, 0:48, :], slow_split[at, 48:96, :] = halves(slow[:, lanes])
+
+        def weigh(at, axis_id):
+            lanes = inside(at)
+            weighted = jnp.zeros((NODES, half_width), f32)
+            for direction in range(3):
+                row = 3 * axis_id + direction
+                factor = geometry_ref[row : row + 1, lanes] * (1.0 / 3.0)
+                weighted = weighted + factor * field_rows(at, 1 + direction)
+            combined[PAD * axis_id : PAD * axis_id + NODES, lanes] = weighted
+
+        def split_weighted(at):
+            high, low = halves(combined[:, inside(at)])
+            sources[at, 768:896, :], sources[at, 896:1024, :] = high, low
+
+        def traces(at):
+            inner[at] = product(select_ref[...], fields_split[at])
+
+        def slope(at, axis_id):
+            lanes = inside(at)
+            place = lax.broadcasted_iota(jnp.int32, (8, half_width), 0) & 3
+            value = product(from_ref[ROWS * axis_id : ROWS * axis_id + ROWS, :], slow_split[at])
+            pattern = jnp.zeros((8, half_width), f32)
+            for direction in range(3):
+                row = 3 * axis_id + direction
+                factor = geometry_ref[row : row + 1, lanes] * (1.0 / 3.0)
+                pattern = jnp.where(place == direction + 1, factor, pattern)
+            value = value.reshape(ROWS // 8, 8, half_width) * pattern[None]
+            value = value.reshape(ROWS, half_width)
+            if axis_id == 0:
+                rates[:, lanes] = value
+            else:
+                rates[:, lanes] += value
+
+        def keep_split(at, start, value):
+            high, low = halves(value)
+            rows = value.shape[0]
+            sources[at, start : start + rows, :] = high
+            sources[at, 256 + start : 256 + start + rows, :] = high
+            sources[at, 512 + start : 512 + start + rows, :] = low
+
+        def jump(at, face):
+            lanes = inside(at)
+            inner_p = inner[at, 64 * face : 64 * face + 16, :]
+            along = jnp.zeros_like(inner_p)
             for axis_id in range(3):
-                weighted = jnp.zeros((NODES, half_width), f32)
-                for direction in range(3):
-                    row = 3 * axis_id + direction
-                    weighted = weighted + geometry[row : row + 1, :] * field_rows(at, 1 + direction)
-                combined[PAD * axis_id : PAD * axis_id + NODES, lanes] = weighted
-            parts = jnp.concatenate(halves(combined[:, lanes]), axis=0)
-            rates[:, lanes] += product(into_ref[...], parts)
-
-        def slopes(at):
+                facing = normals_ref[axis_id, face : face + 1, lanes]
+                start = 64 * face + 16 + 16 * axis_id
+                along = along + facing * inner[at, start : start + 16, :]
+            wall = codes_ref[face : face + 1, lanes] < 0
+            beyond = beyond_ref[FACE_ROWS * face : FACE_ROWS * face + FACE_ROWS, lanes]
+            beyond = jnp.where(wall, -along - inner_p, beyond)
+            scale = 0.5 * scale_ref[face : face + 1, lanes]
+            value = scale * (along - inner_p - beyond)
+            keep_split(at, FACE_ROWS * face, value)
+            for axis_id in range(3):
+                start = 64 + 64 * axis_id + FACE_ROWS * face
+                keep_split(at, start, normals_ref[axis_id, face : face + 1, lanes] * value)
+
+        def lift(at):
             lanes = inside(at)
-            geometry = geometry_ref[:, lanes] * (1.0 / 3.0)
-            slow[0:NODES, lanes] = field_rows(at, 0)
-            parts = jnp.concatenate(halves(slow[:, lanes]), axis=0)
-            place = lax.broadcasted_iota(jnp.int32, (8, half_width), 0) & 3
-            total = rates[:, lanes]
-            for axis_id in range(3):
-                slope = product(from_ref[ROWS * axis_id : ROWS * axis_id + ROWS, :], parts)
-                pattern = jnp.zeros((8, half_width), f32)
-                for direction in range(3):
-                    row = 3 * axis_id + direction
-                    pattern = jnp.where(place == direction + 1, geometry[row : row + 1, :], pattern)
-                slope = slope.reshape(ROWS // 8, 8, half_width) * pattern[None]
-                total = total - slope.reshape(ROWS, half_width)
-            rates[:, lanes] = total
-
-        def advance(at):
+            rates[:, lanes] = product(lift_ref[...], sources[at]) - rates[:, lanes]
+
+        def advance(at, low, high):
             lanes = inside(at)
             slots = lax.broadcasted_iota(jnp.int32, (1, half_width), 1) + (first + half_width * at)
             keep = slots < live_ref[0]
-            for node in range(NODES):
+            for node in range(low, high):
                 rate = rates[4 * node : 4 * node + 4, lanes]
                 residue_next = section_decay * residue_ref[node, :, lanes] + time_step * rate
                 fields_next = fields_ref[node, :, lanes] + section_gain * residue_next
@@ -470,21 +502,45 @@
             picks = jnp.where(slots == elems_ref[...], 1.0, 0.0).astype(bf16)
             sampled[...] += product(parts, picks)
 
-        for at in range(width // half_width):
-            for piece in (traces, lift, into, slopes, advance, sample):
-                yield functools.partial(piece, at)
-
-    def interleave(gathers, updates):
-        gathers, updates = list(gathers), list(updates)
-        done = 0
-        for at, piece in enumerate(gathers):
-            piece()
-            upto = (at + 1) * len(updates) // len(gathers)
-            for other in updates[done:upto]:
-                other()
-            done = upto
-
-    @pl.when(step == -tiles)
+        call = functools.partial
+
+        def stages(at):
+            sevens = range(0, NODES, 7)
+            return [
+                [call(stack, at, low, low + 7) for low in sevens] + [call(split, at)],
+                [call(copy_slow, at)]
+                + [call(weigh, at, axis_id) for axis_id in range(3)]
+                + [call(split_weighted, at), call(traces, at)],
+                [call(slope, at, axis_id) for axis_id in range(3)],
+                [call(jump, at, face) for face in range(4)],
+                [call(lift, at)],
+                [call(advance, at, low, low + 7) for low in sevens],
+                [call(sample, at)],
+            ]
+
+        both = [stages(at) for at in range(width // half_width)]
+        depth = len(both[0])
+        return [
+            [piece for lag, chain in enumerate(both) if 0 <= at - lag < depth for piece in chain[at - lag]]
+            for at in range(depth + len(both) - 1)
+        ]
+
+    def interleave(gathers, groups):
+        gathers = list(gathers)
+
+        def run(at, updates):
+            @pl.when(live_ref[0] > at)
+            def _():
+                low = at * len(gathers) // len(groups)
+                loads = gathers[low : (at + 1) * len(gathers) // len(groups)]
+                for place in range(max(len(loads), len(updates))):
+                    for piece in loads[place : place + 1] + updates[place : place + 1]:
+                        piece()
+
+        for at, updates in enumerate(groups):
+            run(at, updates)
+
+    @pl.when(step == -bulks)
     def _():
         stacked[...] = jnp.zeros_like(stacked)
         combined[...] = jnp.zeros_like(combined)
@@ -493,30 +549,35 @@
         sampled[...] = jnp.zeros_like(sampled)
         monomials[...] = jnp.zeros_like(monomials)
         remote[...] = jnp.zeros_like(remote)
-        count = right_ref.shape[2]
-        sources = [
+        arrivals = [
             left_ref[2],
-            above_ref[1],
+            middle_ref[1],
             right_ref[2],
             left_ref[0],
             right_ref[0],
             left_ref[1],
-            below_ref[1],
+            middle_ref[0],
             right_ref[1],
         ]
-        for heading in range(8):
-            remote[:, count * heading : count * heading + count] = sources[heading]
+        for heading, source in enumerate(arrivals):
+            start = bound_count * heading
+            remote[0:48, start : start + 96] = source[:, 0:96]
+            for third in range(3):
+                place = start + 32 * third
+                remote[48:64, place : place + 32] = source[16 * third : 16 * third + 16, 96:128]
 
     @pl.when(step < 0)
     def _():
-        build_rows((step + tiles) * width, fields_ref, table_select_ref, table_ref, stacked)
+        first = (step + bulks) * bulk_ref.shape[2]
+        for part in range(bulk_ref.shape[2] // width):
+            build_rows(first, part, bulk_ref, table_select_ref, table_ref, stacked)
 
     @pl.when(step == 0)
     def _():
         for piece in gather():
             piece()
 
-    @pl.when((step > 0) & ((step - 1) * width < 8 * right_ref.shape[2]))
+    @pl.when((step > 0) & ((step - 1) * width < 8 * bound_count))
     def _():
         lanes = pl.ds(pl.multiple_of((step - 1) * width, width), width)
         for face in range(4):
@@ -536,8 +597,9 @@
     @pl.when(step == tiles)
     def _():
         beyond_ref[...] = outer[...]
-        for piece in update_pieces():
-            piece()
+        for stage in update_pieces():
+            for piece in stage:
+                piece()
         ladders = []
         for axis_id in range(3):
             base = coords_ref[axis_id : axis_id + 1, :]
@@ -617,9 +679,9 @@
 
     width = 512
     tiles = slot_count // width
-    piece = (3, 64, bound_count)
-
-    up, down, left, right, packed = pl.pallas_call(
+    piece = (3, 48, LANES)
+
+    up, down, left, right, faces = pl.pallas_call(
         functools.partial(pack_kernel, slot_faces),
         grid=(1,),
         in_specs=[
@@ -632,14 +694,14 @@
             fixed(piece),
             fixed(piece[1:]),
             fixed(piece[1:]),
-            fixed((2 * slot_count // LANES, LANES)),
+            fixed((slot_faces // LANES, LANES)),
         ],
         out_shape=[
             shape(piece, f32),
             shape(piece, f32),
             shape(piece[1:], f32),
             shape(piece[1:], f32),
-            shape((2 * slot_count // LANES, LANES), jnp.int32),
+            shape((slot_faces // LANES, LANES), jnp.int32),
         ],
         scratch_shapes=[pltpu.VMEM((reach // LANES, ROWS, LANES), f32)],
         compiler_params=pltpu.CompilerParams(vmem_limit_bytes=16 << 20),
@@ -652,34 +714,35 @@
         return forward, [(target, source) for source, target in forward]
 
     forward, backward = steps_along("px")
-    below = in_hbm(lax.ppermute(up, "px", backward))
-    above = in_hbm(lax.ppermute(down, "px", forward))
-    to_left, to_right = pl.pallas_call(
+    below = lax.ppermute(up, "px", backward)
+    above = lax.ppermute(down, "px", forward)
+    to_left, to_right, middle = pl.pallas_call(
         relay_kernel,
-        out_shape=[shape(piece, f32), shape(piece, f32)],
+        out_shape=[shape(piece, f32), shape(piece, f32), shape((2,) + piece[1:], f32)],
         name="relay",
-    )(in_hbm(left), in_hbm(right), below, above)
+    )(left, right, below, above)
     forward, backward = steps_along("py")
-    from_right = in_hbm(lax.ppermute(to_left, "py", backward))
-    from_left = in_hbm(lax.ppermute(to_right, "py", forward))
+    from_right = lax.ppermute(to_left, "py", backward)
+    from_left = lax.ppermute(to_right, "py", forward)
+
+    bulk = 3 * width
+    bulks = slot_count // bulk
 
     def behind(rank):
-        return lambda t, *_: (0,) * rank + (jnp.maximum(t - tiles - 1, 0),)
+        return lambda t, *_: (0,) * rank + (jnp.maximum(t - bulks - 1, 0),)
 
     def ahead(rank):
-        return lambda t, *_: (0,) * rank + (jnp.clip(t - tiles, 0, tiles - 1),)
-
-    def twice(t, *_):
-        return (0, 0, jnp.where(t < tiles, t, jnp.maximum(t - tiles - 1, 0)))
+        return lambda t, *_: (0,) * rank + (jnp.clip(t - bulks, 0, tiles - 1),)
 
     fields_next, residue_next, spread = pl.pallas_call(
-        functools.partial(section_kernel, slot_count, const["powers"], samples),
+        functools.partial(section_kernel, slot_count, bound_count, const["powers"], samples),
         grid_spec=pltpu.PrefetchScalarGridSpec(
             num_scalar_prefetch=2,
-            grid=(2 * tiles + 1,),
+            grid=(bulks + tiles + 1,),
             in_specs=[
                 pl.BlockSpec((3, 4, width), ahead(2)),
-                pl.BlockSpec((NODES, 4, width), twice),
+                pl.BlockSpec((NODES, 4, bulk), lambda t, *_: (0, 0, jnp.minimum(t, bulks - 1))),
+                pl.BlockSpec((NODES, 4, width), behind(2)),
                 pl.BlockSpec((NODES, 4, width), behind(2)),
                 pl.BlockSpec((9, width), behind(1)),
                 pl.BlockSpec((3, 4, width), behind(2)),
@@ -687,16 +750,14 @@
                 pl.BlockSpec((4, width), behind(1)),
                 fixed(piece),
                 fixed(piece),
-                fixed(piece),
-                fixed(piece),
+                fixed((2,) + piece[1:]),
                 fixed((1, samples)),
                 fixed((1, samples)),
                 fixed((3, samples)),
                 fixed((ROWS, 4 * LANES)),
-                fixed((256, ROWS)),
-                fixed((ROWS, 256)),
+                fixed((256, 2 * ROWS)),
                 fixed((3 * ROWS, 96)),
-                fixed((2 * ROWS, 256)),
+                fixed((ROWS, 1024)),
                 fixed((PAD, PAD)),
             ],
             out_specs=[
@@ -716,8 +777,11 @@
                 pltpu.VMEM((144, samples), f32),
                 pltpu.VMEM((48, width), f32),
                 pltpu.VMEM((PAD, samples), f32),
-                pltpu.VMEM((LANES, LANES), f32),
-                pltpu.VMEM((LANES, LANES), f32),
+                pltpu.VMEM((width // 256, 2 * ROWS, 256), bf16),
+                pltpu.VMEM((width // 256, 96, 256), bf16),
+                pltpu.VMEM((width // 256, 256, 256), f32),
+                pltpu.VMEM((width // 256, 1024, 256), bf16),
+                *[pltpu.VMEM((LANES, LANES), f32)] * 4,
             ],
         ),
         out_shape=[
@@ -728,9 +792,10 @@
         compiler_params=pltpu.CompilerParams(vmem_limit_bytes=48 << 20),
         name="section",
     )(
-        packed.reshape(-1),
+        faces.reshape(-1),
         live_counts,
         normals,
+        fields,
         fields,
         residue,
         geometry,
@@ -739,14 +804,12 @@
         neighbours,
         from_right,
         from_left,
-        below,
-        above,
+        middle,
         in_hbm(sample_elems.reshape(1, samples)),
         in_hbm(sample_ids.reshape(1, samples)),
         sample_coords,
         const["table_select"],
-        const["trace_select"],
-        const["into_p"],
+        const["twice_select"],
         const["from_p"],
         const["lift"],
         const["inverse"],

time: 87.1 us -> 81 us (0.930)
  Pallas kernels: 42.8 us -> 37.2 us
    pallas_call x1, Pallas kernels: 37.7 us -> 32 us  [local(): pl.pallas_call(functools.partial(section_kernel, slot_count, bound_count,...]
    unnamed x12 -> x10, local copies, waits for them, and re-layouts: 2.52 us -> 2.66 us
where the time goes in v3:
time: 81 us; the launch traced here: 80.6 us
  Pallas kernels  37.2 us (46%)
  blocking collectives  25.1 us (31%)
  starting transfers between devices  11.7 us (14%)
  local copies, waits for them, and re-layouts  2.66 us (3%)
  waiting for transfers between devices  2.66 us (3%)
  between operations  1.33 us (2%)
    pallas_call x1, Pallas kernels, local(): pl.pallas_call(functools.partial(section_kernel, slot_count, bound_count,...  32 us
    all_to_all x1, blocking collectives, local(): received = lax.all_to_all(spread, ('px', 'py'), 0, 0, tiled=True)  25.1 us
    ppermute x1, starting transfers between devices, local(): from_left = lax.ppermute(to_right, 'py', forward)  3.99 us
    ppermute x1, starting transfers between devices, local(): below = lax.ppermute(up, 'px', backward)  3.31 us
    ppermute x1, starting transfers between devices, local(): above = lax.ppermute(down, 'px', forward)  3.11 us
    unnamed x10, local copies, waits for them, and re-layouts  2.66 us
    pallas_call x1, Pallas kernels, local(): pl.pallas_call(harmonic_kernel, out_shape=shape((receivers, harmonic.shap...  1.79 us
    pallas_call x1, Pallas kernels, local(): pl.pallas_call(functools.partial(pack_kernel, slot_faces), grid=(1,), in_...  1.7 us
  transfers between devices with their start and end apart: 4, of which 3 were waited for; matrix products, arithmetic and copies ran while one was open for 0% of the time, Pallas kernels for 0%

profile of v3, /device:TPU:1, one launch (start us, length us, event | category | flops | bytes accessed | tf_op | source)
XLA Modules:
  0.0 80.6 jit_solution(12214389213122317047)
XLA Ops:
  0.6 1.7 %pack.1 = (f32[3,48,128]{2,1,0:T(8,128)S(1)}, f32[3,48,128]{2,1,0:T(8,128)S(1)}, f32[48,128]{1,0:T(8,128)S(1)}, f32[48,128]{1,0:T(8,128)S(1)}, s32[144,128]{1,0:T(8,128)S(1)}) custom-call(f32[35,4,4608]{2,1,0:T(4,128)} %bitcast.9, s32[4,4608]{1,0:T(4,128)} %codes_ref.3, bf16[256,144]{1,0:T(8,128)(2,1)} %constant.17.clone.select_ref), custom_call_target="tpu_custom_call" | custom-call | tf_op jit(solution)/shard_map/pack/pallas_call | solution.py:684
  2.3 0.0 copy-start.1
  2.3 0.6 copy-done.1
  3.0 0.0 copy-start.2
  3.0 0.6 copy-done.2
  3.6 3.3 %collective-permute-start = (f32[3,48,128]{2,1,0:T(8,128)S(1)}, f32[3,48,128]{2,1,0:T(8,128)S(1)}, u32[]{:S(2)}, u32[]{:S(2)}) collective-permute-start(f32[3,48,128]{2,1,0:T(8,128)S(1)} %get-tuple-element.17), channel_id=1, source_target_pairs={{16,0},{32,16},{48,32},{64,48},{80,64},{96,80},{112,96},{17,1},{33... | collective-permute-start | bytes 221192 | tf_op jit(solution)/shard_map/ppermute | solution.py:717
  6.9 3.1 %collective-permute-start.1 = (f32[3,48,128]{2,1,0:T(8,128)S(1)}, f32[3,48,128]{2,1,0:T(8,128)S(1)}, u32[]{:S(2)}, u32[]{:S(2)}) collective-permute-start(f32[3,48,128]{2,1,0:T(8,128)S(1)} %get-tuple-element.18), channel_id=1, source_target_pairs={{0,16},{16,32},{32,48},{48,64},{64,80},{80,96},{96,112},{1,17},{17... | collective-permute-start | bytes 221192 | tf_op jit(solution)/shard_map/ppermute | solution.py:718
  10.0 0.1 collective-permute-done.below_ref
  10.1 0.0 copy-start.3
  10.1 1.3 %collective-permute-done.1.above_ref = f32[3,48,128]{2,1,0:T(8,128)S(1)} collective-permute-done((f32[3,48,128]{2,1,0:T(8,128)S(1)}, f32[3,48,128]{2,1,0:T(8,128)S(1)}, u32[]{:S(2)}, u32[]{:S(2)}) %collective-permute-start.1) | collective-permute-done | bytes 73760 | tf_op jit(solution)/shard_map/ppermute | solution.py:718
  11.4 0.0 copy-start.4
  11.4 0.0 copy-done.3
  11.4 0.6 copy-done.4
  12.0 1.6 %relay.1 = (f32[3,48,128]{2,1,0:T(8,128)}, f32[3,48,128]{2,1,0:T(8,128)}, f32[2,48,128]{2,1,0:T(8,128)}) custom-call(f32[48,128]{1,0:T(8,128)} %copy-done.1, f32[48,128]{1,0:T(8,128)} %copy-done.2, f32[3,48,128]{2,1,0:T(8,128)} %copy-done.3, f32[3,48,128]{2,1,0:T(8,128)} %copy-done.4), custom_call_target="tpu_custom_call" | custom-call | tf_op jit(solution)/shard_map/relay/pallas_call | solution.py:719
  13.7 1.3 %collective-permute-start.2 = (f32[3,48,128]{2,1,0:T(8,128)}, f32[3,48,128]{2,1,0:T(8,128)S(1)}, u32[]{:S(2)}, u32[]{:S(2)}) collective-permute-start(f32[3,48,128]{2,1,0:T(8,128)} %get-tuple-element.19), channel_id=1, source_target_pairs={{1,0},{2,1},{3,2},{4,3},{5,4},{6,5},{7,6},{8,7},{9,8},{10,9},{11,1... | collective-permute-start | bytes 221192 | tf_op jit(solution)/shard_map/ppermute | solution.py:725
  14.9 4.0 %collective-permute-start.3 = (f32[3,48,128]{2,1,0:T(8,128)}, f32[3,48,128]{2,1,0:T(8,128)S(1)}, u32[]{:S(2)}, u32[]{:S(2)}) collective-permute-start(f32[3,48,128]{2,1,0:T(8,128)} %get-tuple-element.20), channel_id=1, source_target_pairs={{0,1},{1,2},{2,3},{3,4},{4,5},{5,6},{6,7},{7,8},{8,9},{9,10},{10,1... | collective-permute-start | bytes 221192 | tf_op jit(solution)/shard_map/ppermute | solution.py:726
  19.6 0.0 collective-permute-done.2.right_ref
  19.6 1.3 %collective-permute-done.3.left_ref = f32[3,48,128]{2,1,0:T(8,128)S(1)} collective-permute-done((f32[3,48,128]{2,1,0:T(8,128)}, f32[3,48,128]{2,1,0:T(8,128)S(1)}, u32[]{:S(2)}, u32[]{:S(2)}) %collective-permute-start.3) | collective-permute-done | bytes 73760 | tf_op jit(solution)/shard_map/ppermute | solution.py:726
  20.9 0.0 copy-start
  20.9 0.8 copy-done
  21.7 32.0 %section.1 = (f32[35,4,4608]{2,1,0:T(4,128)}, f32[35,4,4608]{2,1,0:T(4,128)}, f32[128,1,200]{2,1,0:T(1,128)S(1)}) custom-call(s32[18432]{0:T(1024)S(1)} %bitcast.8, s32[1]{0:T(128)S(6)} %copy.21.live_ref, f32[3,4,4608]{2,1,0:T(4,128)} %normals_ref.1, f32[35,4,4608]{2,1,0:T(4,128)} %bitcast.10, f32[35,4,4608]{2,1,0:T(4,128)} %bitcast.11, ...), custom_call_target="tpu_custom_call" | custom-call | tf_op jit(solution)/shard_map/section/pallas_call | solution.py:737
  53.7 25.1 %all_to_all.5.received_ref = f32[128,1,200]{2,1,0:T(1,128)} all-to-all(f32[128,1,200]{2,1,0:T(1,128)S(1)} %get-tuple-element.24), channel_id=1, replica_groups=mesh['px'=8,'py'=16] {'px','py'}, dimensions={0} | all-to-all | bytes 204800 | tf_op jit(solution)/shard_map/all_to_all | solution.py:817
  78.8 1.8 %harmonic.1 = f32[4,25]{1,0:T(4,128)} custom-call(f32[128,1,200]{2,1,0:T(1,128)} %all_to_all.5.received_ref, f32[25,200]{1,0:T(8,128)} %constant.22.clone.table_ref, f32[4,200]{1,0:T(4,128)} %constant.23.clone.groups_ref), custom_call_target="tpu_custom_call" | custom-call | tf_op jit(solution)/shard_map/harmonic/pallas_call | solution.py:822
Async XLA Ops:
  2.3 0.6 copy-start.1
  3.0 0.6 copy-start.2
  3.6 6.5 %collective-permute-start = (f32[3,48,128]{2,1,0:T(8,128)S(1)}, f32[3,48,128]{2,1,0:T(8,128)S(1)}, u32[]{:S(2)}, u32[]{:S(2)}) collective-permute-start(f32[3,48,128]{2,1,0:T(8,128)S(1)} %get-tuple-element.17), channel_id=1, source_target_pairs={{16,0},{32,16},{48,32},{64,48},{80,64},{96,80},{112,96},{17,1},{33... | collective-permute-start | bytes 221192 | tf_op jit(solution)/shard_map/ppermute | solution.py:717
  6.9 4.5 %collective-permute-start.1 = (f32[3,48,128]{2,1,0:T(8,128)S(1)}, f32[3,48,128]{2,1,0:T(8,128)S(1)}, u32[]{:S(2)}, u32[]{:S(2)}) collective-permute-start(f32[3,48,128]{2,1,0:T(8,128)S(1)} %get-tuple-element.18), channel_id=1, source_target_pairs={{0,16},{16,32},{32,48},{48,64},{64,80},{80,96},{96,112},{1,17},{17... | collective-permute-start | bytes 221192 | tf_op jit(solution)/shard_map/ppermute | solution.py:718
  10.1 1.3 %copy-start.3 = (f32[3,48,128]{2,1,0:T(8,128)}, f32[3,48,128]{2,1,0:T(8,128)S(1)}, u32[]{:S(2)}) copy-start(f32[3,48,128]{2,1,0:T(8,128)S(1)} %collective-permute-done.below_ref) | copy-start | bytes 221188
  11.4 0.6 copy-start.4
  13.7 5.9 %collective-permute-start.2 = (f32[3,48,128]{2,1,0:T(8,128)}, f32[3,48,128]{2,1,0:T(8,128)S(1)}, u32[]{:S(2)}, u32[]{:S(2)}) collective-permute-start(f32[3,48,128]{2,1,0:T(8,128)} %get-tuple-element.19), channel_id=1, source_target_pairs={{1,0},{2,1},{3,2},{4,3},{5,4},{6,5},{7,6},{8,7},{9,8},{10,9},{11,1... | collective-permute-start | bytes 221192 | tf_op jit(solution)/shard_map/ppermute | solution.py:725
  14.9 5.9 %collective-permute-start.3 = (f32[3,48,128]{2,1,0:T(8,128)}, f32[3,48,128]{2,1,0:T(8,128)S(1)}, u32[]{:S(2)}, u32[]{:S(2)}) collective-permute-start(f32[3,48,128]{2,1,0:T(8,128)} %get-tuple-element.20), channel_id=1, source_target_pairs={{0,1},{1,2},{2,3},{3,4},{4,5},{5,6},{6,7},{7,8},{8,9},{9,10},{10,1... | collective-permute-start | bytes 221192 | tf_op jit(solution)/shard_map/ppermute | solution.py:726
  20.9 0.8 copy-start

commit v4 on v3

--- a/solution.py
+++ b/solution.py
@@ -273,15 +273,13 @@
             ]
 
 
-def relay_kernel(left_ref, right_ref, below_ref, above_ref, to_left_ref, to_right_ref, middle_ref):
+def relay_kernel(left_ref, right_ref, below_ref, above_ref, to_left_ref, to_right_ref):
     to_left_ref[0] = left_ref[...]
     to_left_ref[1] = below_ref[0]
     to_left_ref[2] = above_ref[0]
     to_right_ref[0] = right_ref[...]
     to_right_ref[1] = below_ref[2]
     to_right_ref[2] = above_ref[2]
-    middle_ref[0] = below_ref[1]
-    middle_ref[1] = above_ref[1]
 
 
 def build_rows(first, part, fields_ref, select_ref, table_ref, stacked):
@@ -334,9 +332,7 @@
 
 def section_kernel(
     slot_count,
-    bound_count,
-    powers,
-    group,
+    reach,
     faces_ref,
     live_ref,
     next_normals_ref,
@@ -347,31 +343,22 @@
     normals_ref,
     scale_ref,
     codes_ref,
-    right_ref,
-    left_ref,
-    middle_ref,
     elems_ref,
-    ids_ref,
-    coords_ref,
     table_select_ref,
     select_ref,
     from_ref,
     lift_ref,
-    inverse_ref,
     fields_out,
     residue_out,
-    spread_ref,
+    sampled,
     table_ref,
     stacked,
     combined,
     slow,
     rates,
-    remote,
     outer,
     beyond_ref,
-    sampled,
     pressure,
-    monomials,
     fields_split,
     slow_split,
     inner,
@@ -470,6 +457,7 @@
             wall = codes_ref[face : face + 1, lanes] < 0
             beyond = beyond_ref[FACE_ROWS * face : FACE_ROWS * face + FACE_ROWS, lanes]
             beyond = jnp.where(wall, -along - inner_p, beyond)
+            beyond = jnp.where(codes_ref[face : face + 1, lanes] >= slot_faces, 0.0, beyond)
             scale = 0.5 * scale_ref[face : face + 1, lanes]
             value = scale * (along - inner_p - beyond)
             keep_split(at, FACE_ROWS * face, value)
@@ -499,8 +487,9 @@
             parts = jnp.concatenate(thirds(pressure[:, lanes]), axis=0)
             start = first + half_width * at
             slots = lax.broadcasted_iota(jnp.int32, (half_width, elems_ref.shape[1]), 0) + start
-            picks = jnp.where(slots == elems_ref[...], 1.0, 0.0).astype(bf16)
-            sampled[...] += product(parts, picks)
+            elems = elems_ref[...]
+            picks = (slots == elems) & (elems >= reach)
+            sampled[...] += product(parts, jnp.where(picks, 1.0, 0.0).astype(bf16))
 
         call = functools.partial
 
@@ -547,24 +536,6 @@
         slow[...] = jnp.zeros_like(slow)
         pressure[...] = jnp.zeros_like(pressure)
         sampled[...] = jnp.zeros_like(sampled)
-        monomials[...] = jnp.zeros_like(monomials)
-        remote[...] = jnp.zeros_like(remote)
-        arrivals = [
-            left_ref[2],
-            middle_ref[1],
-            right_ref[2],
-            left_ref[0],
-            right_ref[0],
-            left_ref[1],
-            middle_ref[0],
-            right_ref[1],
-        ]
-        for heading, source in enumerate(arrivals):
-            start = bound_count * heading
-            remote[0:48, start : start + 96] = source[:, 0:96]
-            for third in range(3):
-                place = start + 32 * third
-                remote[48:64, place : place + 32] = source[16 * third : 16 * third + 16, 96:128]
 
     @pl.when(step < 0)
     def _():
@@ -576,18 +547,6 @@
     def _():
         for piece in gather():
             piece()
-
-    @pl.when((step > 0) & ((step - 1) * width < 8 * bound_count))
-    def _():
-        lanes = pl.ds(pl.multiple_of((step - 1) * width, width), width)
-        for face in range(4):
-            rows = slice(FACE_ROWS * face, FACE_ROWS * face + FACE_ROWS)
-            total = -remote[0:16, lanes]
-            for axis_id in range(3):
-                facing = normals_ref[axis_id, face : face + 1, :]
-                total = total + facing * remote[16 + 16 * axis_id : 32 + 16 * axis_id, lanes]
-            is_remote = codes_ref[face : face + 1, :] >= slot_faces
-            outer[rows, :] = jnp.where(is_remote, total, outer[rows, :])
 
     @pl.when((step > 0) & (step < tiles))
     def _():
@@ -600,32 +559,111 @@
         for stage in update_pieces():
             for piece in stage:
                 piece()
-        ladders = []
+
+
+def boundary_kernel(
+    slot_faces,
+    powers,
+    group,
+    fields_ref,
+    residue_ref,
+    normals_ref,
+    scale_ref,
+    codes_ref,
+    right_ref,
+    left_ref,
+    below_ref,
+    above_ref,
+    elems_ref,
+    ids_ref,
+    coords_ref,
+    partial_ref,
+    lift_ref,
+    inverse_ref,
+    fields_out,
+    residue_out,
+    spread_ref,
+    remote,
+    sources,
+    rates,
+    pressure,
+    monomials,
+):
+    reach = fields_ref.shape[2]
+    bound_count = reach // 8
+    pressure[...] = jnp.zeros_like(pressure)
+    monomials[...] = jnp.zeros_like(monomials)
+    arrivals = [
+        left_ref[2],
+        above_ref[1],
+        right_ref[2],
+        left_ref[0],
+        right_ref[0],
+        left_ref[1],
+        below_ref[1],
+        right_ref[1],
+    ]
+    for heading, source in enumerate(arrivals):
+        start = bound_count * heading
+        remote[0:48, start : start + 96] = source[:, 0:96]
+        for third in range(3):
+            place = start + 32 * third
+            remote[48:64, place : place + 32] = source[16 * third : 16 * third + 16, 96:128]
+
+    def keep_split(start, value):
+        high, low = halves(value)
+        sources[start : start + FACE_ROWS, :] = high
+        sources[256 + start : 256 + start + FACE_ROWS, :] = high
+        sources[512 + start : 512 + start + FACE_ROWS, :] = low
+
+    for face in range(4):
+        beyond = -remote[0:16, :]
         for axis_id in range(3):
-            base = coords_ref[axis_id : axis_id + 1, :]
-            square = base * base
-            ladders.append([jnp.ones_like(base), base, square, square * base, square * square])
-        for node in range(NODES):
-            exps = [int(entry) for entry in powers[node]]
-            monomials[node : node + 1, :] = (
-                ladders[0][exps[0]] * ladders[1][exps[1]] * ladders[2][exps[2]]
-            )
-        basis = jnp.dot(
-            inverse_ref[...], monomials[...], precision=highest, preferred_element_type=f32
+            facing = normals_ref[axis_id, face : face + 1, :]
+            beyond = beyond + facing * remote[16 + 16 * axis_id : 32 + 16 * axis_id, :]
+        is_remote = codes_ref[face : face + 1, :] >= slot_faces
+        flux = jnp.where(is_remote, -0.5 * scale_ref[face : face + 1, :] * beyond, 0.0)
+        keep_split(FACE_ROWS * face, flux)
+        for axis_id in range(3):
+            facing = normals_ref[axis_id, face : face + 1, :]
+            keep_split(64 + 64 * axis_id + FACE_ROWS * face, facing * flux)
+    rates[...] = time_step * product(lift_ref[:, 0:768], sources[...])
+    for node in range(NODES):
+        rate = rates[4 * node : 4 * node + 4, :]
+        residue_out[node] = residue_ref[node] + rate
+        fields_next = fields_ref[node] + section_gain * rate
+        fields_out[node] = fields_next
+        pressure[node : node + 1, :] = fields_next[0:1]
+    parts = jnp.concatenate(thirds(pressure[...]), axis=0)
+    slots = lax.broadcasted_iota(jnp.int32, (reach, elems_ref.shape[1]), 0)
+    picks = jnp.where(slots == elems_ref[...], 1.0, 0.0).astype(bf16)
+    sampled = partial_ref[...] + product(parts, picks)
+    ladders = []
+    for axis_id in range(3):
+        base = coords_ref[axis_id : axis_id + 1, :]
+        square = base * base
+        ladders.append([jnp.ones_like(base), base, square, square * base, square * square])
+    for node in range(NODES):
+        exps = [int(entry) for entry in powers[node]]
+        monomials[node : node + 1, :] = (
+            ladders[0][exps[0]] * ladders[1][exps[1]] * ladders[2][exps[2]]
         )
-        gathered = sampled[0:PAD, :] + sampled[48 : 48 + PAD, :] + sampled[96 : 96 + PAD, :]
-        values = jnp.sum(basis * gathered, axis=0, keepdims=True)
-        ids = ids_ref[...]
-        owner = lax.shift_right_logical(ids * 5243, 20)
-        place = ids - group * owner
-        owners = lax.broadcasted_iota(jnp.int32, (spread_ref.shape[0], ids.shape[1]), 0)
-        held = jnp.where(owners == owner, values, 0.0)
-        places = lax.broadcasted_iota(jnp.int32, (spread_ref.shape[2], ids.shape[1]), 0)
-        chosen = jnp.where(places == place, 1.0, 0.0).astype(bf16)
-        spread = jnp.zeros((spread_ref.shape[0], spread_ref.shape[2]), f32)
-        for part in thirds(held):
-            spread = spread + product(part, chosen, ((1,), (1,)))
-        spread_ref[:, 0, :] = spread
+    basis = jnp.dot(
+        inverse_ref[...], monomials[...], precision=highest, preferred_element_type=f32
+    )
+    gathered = sampled[0:PAD, :] + sampled[48 : 48 + PAD, :] + sampled[96 : 96 + PAD, :]
+    values = jnp.sum(basis * gathered, axis=0, keepdims=True)
+    ids = ids_ref[...]
+    owner = lax.shift_right_logical(ids * 5243, 20)
+    place = ids - group * owner
+    owners = lax.broadcasted_iota(jnp.int32, (spread_ref.shape[0], ids.shape[1]), 0)
+    held = jnp.where(owners == owner, values, 0.0)
+    places = lax.broadcasted_iota(jnp.int32, (spread_ref.shape[2], ids.shape[1]), 0)
+    chosen = jnp.where(places == place, 1.0, 0.0).astype(bf16)
+    spread = jnp.zeros((spread_ref.shape[0], spread_ref.shape[2]), f32)
+    for part in thirds(held):
+        spread = spread + product(part, chosen, ((1,), (1,)))
+    spread_ref[:, 0, :] = spread
 
 
 def harmonic_kernel(received_ref, table_ref, groups_ref, out_ref):
@@ -677,6 +715,7 @@
     devices = lax.axis_size(("px", "py"))
     shape = jax.ShapeDtypeStruct
 
+    elems = in_hbm(sample_elems.reshape(1, samples))
     width = 512
     tiles = slot_count // width
     piece = (3, 48, LANES)
@@ -697,10 +736,10 @@
             fixed((slot_faces // LANES, LANES)),
         ],
         out_shape=[
-            shape(piece, f32),
-            shape(piece, f32),
-            shape(piece[1:], f32),
-            shape(piece[1:], f32),
+            pltpu.HBM(piece, f32),
+            pltpu.HBM(piece, f32),
+            pltpu.HBM(piece[1:], f32),
+            pltpu.HBM(piece[1:], f32),
             shape((slot_faces // LANES, LANES), jnp.int32),
         ],
         scratch_shapes=[pltpu.VMEM((reach // LANES, ROWS, LANES), f32)],
@@ -716,9 +755,9 @@
     forward, backward = steps_along("px")
     below = lax.ppermute(up, "px", backward)
     above = lax.ppermute(down, "px", forward)
-    to_left, to_right, middle = pl.pallas_call(
+    to_left, to_right = pl.pallas_call(
         relay_kernel,
-        out_shape=[shape(piece, f32), shape(piece, f32), shape((2,) + piece[1:], f32)],
+        out_shape=[pltpu.HBM(piece, f32), pltpu.HBM(piece, f32)],
         name="relay",
     )(left, right, below, above)
     forward, backward = steps_along("py")
@@ -734,8 +773,8 @@
     def ahead(rank):
         return lambda t, *_: (0,) * rank + (jnp.clip(t - bulks, 0, tiles - 1),)
 
-    fields_next, residue_next, spread = pl.pallas_call(
-        functools.partial(section_kernel, slot_count, bound_count, const["powers"], samples),
+    fields_next, residue_next, partial = pl.pallas_call(
+        functools.partial(section_kernel, slot_count, reach),
         grid_spec=pltpu.PrefetchScalarGridSpec(
             num_scalar_prefetch=2,
             grid=(bulks + tiles + 1,),
@@ -748,22 +787,16 @@
                 pl.BlockSpec((3, 4, width), behind(2)),
                 pl.BlockSpec((4, width), behind(1)),
                 pl.BlockSpec((4, width), behind(1)),
-                fixed(piece),
-                fixed(piece),
-                fixed((2,) + piece[1:]),
                 fixed((1, samples)),
-                fixed((1, samples)),
-                fixed((3, samples)),
                 fixed((ROWS, 4 * LANES)),
                 fixed((256, 2 * ROWS)),
                 fixed((3 * ROWS, 96)),
                 fixed((ROWS, 1024)),
-                fixed((PAD, PAD)),
             ],
             out_specs=[
                 pl.BlockSpec((NODES, 4, width), behind(2)),
                 pl.BlockSpec((NODES, 4, width), behind(2)),
-                fixed((devices, 1, samples)),
+                fixed((144, samples)),
             ],
             scratch_shapes=[
                 pltpu.VMEM((slot_faces, LANES), f32),
@@ -771,12 +804,9 @@
                 pltpu.VMEM((128, width), f32),
                 pltpu.VMEM((48, width), f32),
                 pltpu.VMEM((ROWS, width), f32),
-                pltpu.VMEM((64, pl.cdiv(reach, width) * width), f32),
                 pltpu.VMEM((64, width), f32),
                 pltpu.VMEM((64, width), f32),
-                pltpu.VMEM((144, samples), f32),
                 pltpu.VMEM((48, width), f32),
-                pltpu.VMEM((PAD, samples), f32),
                 pltpu.VMEM((width // 256, 2 * ROWS, 256), bf16),
                 pltpu.VMEM((width // 256, 96, 256), bf16),
                 pltpu.VMEM((width // 256, 256, 256), f32),
@@ -787,7 +817,7 @@
         out_shape=[
             shape(fields.shape, f32),
             shape(residue.shape, f32),
-            shape((devices, 1, samples), f32),
+            shape((144, samples), f32),
         ],
         compiler_params=pltpu.CompilerParams(vmem_limit_bytes=48 << 20),
         name="section",
@@ -802,15 +832,70 @@
         normals,
         face_scale,
         neighbours,
-        from_right,
-        from_left,
-        middle,
-        in_hbm(sample_elems.reshape(1, samples)),
-        in_hbm(sample_ids.reshape(1, samples)),
-        sample_coords,
+        elems,
         const["table_select"],
         const["twice_select"],
         const["from_p"],
+        const["lift"],
+    )
+
+    def head(rank):
+        return lambda t: (0,) * rank
+
+    fields_next, residue_next, spread = pl.pallas_call(
+        functools.partial(boundary_kernel, slot_faces, const["powers"], samples),
+        grid=(1,),
+        in_specs=[
+            pl.BlockSpec((NODES, 4, reach), head(3)),
+            pl.BlockSpec((NODES, 4, reach), head(3)),
+            pl.BlockSpec((3, 4, reach), head(3)),
+            pl.BlockSpec((4, reach), head(2)),
+            pl.BlockSpec((4, reach), head(2)),
+            fixed(piece),
+            fixed(piece),
+            fixed(piece),
+            fixed(piece),
+            fixed((1, samples)),
+            fixed((1, samples)),
+            fixed((3, samples)),
+            fixed((144, samples)),
+            fixed((ROWS, 1024)),
+            fixed((PAD, PAD)),
+        ],
+        out_specs=[
+            pl.BlockSpec((NODES, 4, reach), head(3)),
+            pl.BlockSpec((NODES, 4, reach), head(3)),
+            fixed((devices, 1, samples)),
+        ],
+        out_shape=[
+            shape(fields.shape, f32),
+            shape(residue.shape, f32),
+            shape((devices, 1, samples), f32),
+        ],
+        scratch_shapes=[
+            pltpu.VMEM((64, reach), f32),
+            pltpu.VMEM((768, reach), bf16),
+            pltpu.VMEM((ROWS, reach), f32),
+            pltpu.VMEM((48, reach), f32),
+            pltpu.VMEM((PAD, samples), f32),
+        ],
+        input_output_aliases={0: 0, 1: 1},
+        compiler_params=pltpu.CompilerParams(vmem_limit_bytes=24 << 20),
+        name="boundary",
+    )(
+        in_hbm(fields_next),
+        in_hbm(residue_next),
+        normals,
+        face_scale,
+        neighbours,
+        from_right,
+        from_left,
+        below,
+        above,
+        elems,
+        in_hbm(sample_ids.reshape(1, samples)),
+        sample_coords,
+        partial,
         const["lift"],
         const["inverse"],
     )

time: 81 us -> 79.5 us (0.981)
  Pallas kernels: 37.2 us -> 39.9 us
  local copies, waits for them, and re-layouts: 2.66 us -> 0.65 us
  blocking collectives: 25.1 us -> 23.9 us
  waiting for transfers between devices: 2.66 us -> 1.71 us
    pallas_call x2 -> x3, Pallas kernels: 33.7 us -> 35.7 us  [the longest x1 31.1 us: local(): pl.pallas_call(functools.partial(section_kernel, slot_count, reach), grid...]
    unnamed x10 -> x8, local copies, waits for them, and re-layouts: 2.66 us -> 0.65 us
    ppermute x1, waiting for transfers between devices: 1.28 us -> 0.01 us  [local(): from_left = lax.ppermute(to_right, 'py', forward)]
    all_to_all x1, blocking collectives: 25.1 us -> 23.9 us  [local(): received = lax.all_to_all(spread, ('px', 'py'), 0, 0, tiled=True)]
  transfers between devices with their start and end apart: 4 -> 4, of which waited for: 3 -> 2; matrix products, arithmetic and copies ran while one was open for 0% -> 0% of each run, Pallas kernels for 0% -> 39%
where the time goes in v4:
time: 79.5 us; the launch traced here: 79.2 us
  Pallas kernels  39.9 us (50%)
  blocking collectives  23.9 us (30%)
  starting transfers between devices  11.7 us (15%)
  waiting for transfers between devices  1.71 us (2%)
  between operations  1.36 us (2%)
    pallas_call x1, Pallas kernels, local(): pl.pallas_call(functools.partial(section_kernel, slot_count, reach), grid...  31.1 us
    all_to_all x1, blocking collectives, local(): received = lax.all_to_all(spread, ('px', 'py'), 0, 0, tiled=True)  23.9 us
    ppermute x1, starting transfers between devices, local(): from_left = lax.ppermute(to_right, 'py', forward)  3.99 us
    ppermute x1, starting transfers between devices, local(): below = lax.ppermute(up, 'px', backward)  3.32 us
    ppermute x1, starting transfers between devices, local(): above = lax.ppermute(down, 'px', forward)  3.1 us
    pallas_call x1, Pallas kernels, local(): pl.pallas_call(functools.partial(boundary_kernel, slot_faces, const['powe...  2.98 us
    pallas_call x1, Pallas kernels, local(): pl.pallas_call(functools.partial(pack_kernel, slot_faces), grid=(1,), in_...  2.34 us
    pallas_call x1, Pallas kernels, local(): pl.pallas_call(harmonic_kernel, out_shape=shape((receivers, harmonic.shap...  1.79 us
  transfers between devices with their start and end apart: 4, of which 2 were waited for; matrix products, arithmetic and copies ran while one was open for 0% of the time, Pallas kernels for 39%

profile of v4, /device:TPU:1, one launch (start us, length us, event | category | flops | bytes accessed | tf_op | source)
XLA Modules:
  0.0 79.2 jit_solution(4828214280765229973)
XLA Ops:
  0.6 2.3 %pack.1 = (f32[3,48,128]{2,1,0:T(8,128)}, f32[3,48,128]{2,1,0:T(8,128)}, f32[48,128]{1,0:T(8,128)}, f32[48,128]{1,0:T(8,128)}, s32[144,128]{1,0:T(8,128)S(1)}) custom-call(f32[35,4,4608]{2,1,0:T(4,128)} %bitcast.9, s32[4,4608]{1,0:T(4,128)} %codes_ref.5, bf16[256,144]{1,0:T(8,128)(2,1)} %constant.17.clone.select_ref), custom_call_target="tpu_custom_call" | custom-call | tf_op jit(solution)/shard_map/pack/pallas_call | solution.py:723
  3.0 3.3 %collective-permute-start = (f32[3,48,128]{2,1,0:T(8,128)}, f32[3,48,128]{2,1,0:T(8,128)S(1)}, u32[]{:S(2)}, u32[]{:S(2)}) collective-permute-start(f32[3,48,128]{2,1,0:T(8,128)} %get-tuple-element.21), channel_id=1, source_target_pairs={{16,0},{32,16},{48,32},{64,48},{80,64},{96,80},{112,96},{17,1},{33... | collective-permute-start | bytes 221192 | tf_op jit(solution)/shard_map/ppermute | solution.py:756
  6.3 3.1 %collective-permute-start.1 = (f32[3,48,128]{2,1,0:T(8,128)}, f32[3,48,128]{2,1,0:T(8,128)S(1)}, u32[]{:S(2)}, u32[]{:S(2)}) collective-permute-start(f32[3,48,128]{2,1,0:T(8,128)} %get-tuple-element.22), channel_id=1, source_target_pairs={{0,16},{16,32},{32,48},{48,64},{64,80},{80,96},{96,112},{1,17},{17... | collective-permute-start | bytes 221192 | tf_op jit(solution)/shard_map/ppermute | solution.py:757
  9.4 0.3 collective-permute-done.below_ref
  9.7 0.0 copy-start
  9.7 1.4 %collective-permute-done.1.above_ref = f32[3,48,128]{2,1,0:T(8,128)S(1)} collective-permute-done((f32[3,48,128]{2,1,0:T(8,128)}, f32[3,48,128]{2,1,0:T(8,128)S(1)}, u32[]{:S(2)}, u32[]{:S(2)}) %collective-permute-start.1) | collective-permute-done | bytes 73760 | tf_op jit(solution)/shard_map/ppermute | solution.py:757
  11.1 0.0 copy-start.2
  11.1 0.0 copy-done
  11.1 0.6 copy-done.2
  11.8 1.6 %relay.1 = (f32[3,48,128]{2,1,0:T(8,128)}, f32[3,48,128]{2,1,0:T(8,128)}) custom-call(f32[48,128]{1,0:T(8,128)} %get-tuple-element.19.left_ref, f32[48,128]{1,0:T(8,128)} %get-tuple-element.20.right_ref, f32[3,48,128]{2,1,0:T(8,128)} %copy-done, f32[3,48,128]{2,1,0:T(8,128)} %copy-done.2), custom_call_target="tpu_custom_call" | custom-call | tf_op jit(solution)/shard_map/relay/pallas_call | solution.py:758
  13.4 1.3 %collective-permute-start.2 = (f32[3,48,128]{2,1,0:T(8,128)}, f32[3,48,128]{2,1,0:T(8,128)S(1)}, u32[]{:S(2)}, u32[]{:S(2)}) collective-permute-start(f32[3,48,128]{2,1,0:T(8,128)} %get-tuple-element.23), channel_id=1, source_target_pairs={{1,0},{2,1},{3,2},{4,3},{5,4},{6,5},{7,6},{8,7},{9,8},{10,9},{11,1... | collective-permute-start | bytes 221192 | tf_op jit(solution)/shard_map/ppermute | solution.py:764
  14.7 4.0 %collective-permute-start.3 = (f32[3,48,128]{2,1,0:T(8,128)}, f32[3,48,128]{2,1,0:T(8,128)S(1)}, u32[]{:S(2)}, u32[]{:S(2)}) collective-permute-start(f32[3,48,128]{2,1,0:T(8,128)} %get-tuple-element.24), channel_id=1, source_target_pairs={{0,1},{1,2},{2,3},{3,4},{4,5},{5,6},{6,7},{7,8},{8,9},{9,10},{10,1... | collective-permute-start | bytes 221192 | tf_op jit(solution)/shard_map/ppermute | solution.py:765
  19.3 0.0 copy-start.1
  19.3 0.0 copy-start.3
  19.3 31.1 %section.1 = (f32[35,4,4608]{2,1,0:T(4,128)}, f32[35,4,4608]{2,1,0:T(4,128)}, f32[144,200]{1,0:T(8,128)S(1)}) custom-call(s32[18432]{0:T(1024)S(1)} %bitcast.8, s32[1]{0:T(128)S(6)} %copy.25.live_ref, f32[3,4,4608]{2,1,0:T(4,128)} %normals_ref.3, f32[35,4,4608]{2,1,0:T(4,128)} %bitcast.10, f32[35,4,4608]{2,1,0:T(4,128)} %bitcast.11, ...), custom_call_target="tpu_custom_call" | custom-call | tf_op jit(solution)/shard_map/section/pallas_call | solution.py:776
  50.4 0.0 collective-permute-done.2.right_ref
  50.5 0.0 collective-permute-done.3.left_ref
  50.5 0.0 copy-done.1
  50.5 0.0 copy-done.3
  50.5 3.0 %boundary.1 = (f32[35,4,4608]{2,1,0:T(4,128)}, f32[35,4,4608]{2,1,0:T(4,128)}, f32[128,1,200]{2,1,0:T(1,128)S(1)}) custom-call(f32[35,4,4608]{2,1,0:T(4,128)} %get-tuple-element.17.fields_ref, f32[35,4,4608]{2,1,0:T(4,128)} %get-tuple-element.18.residue_ref, f32[3,4,4608]{2,1,0:T(4,128)} %normals_ref.3, ...), custom_call_target="tpu_custom_call", output_to_operand_aliasing={{0}: (0, {}), {1}: (1, {})} | custom-call | tf_op jit(solution)/shard_map/boundary/pallas_call | solution.py:845
  53.5 23.9 %all_to_all.5.received_ref = f32[128,1,200]{2,1,0:T(1,128)} all-to-all(f32[128,1,200]{2,1,0:T(1,128)S(1)} %get-tuple-element.28), channel_id=1, replica_groups=mesh['px'=8,'py'=16] {'px','py'}, dimensions={0} | all-to-all | bytes 204800 | tf_op jit(solution)/shard_map/all_to_all | solution.py:902
  77.4 1.8 %harmonic.1 = f32[4,25]{1,0:T(4,128)} custom-call(f32[128,1,200]{2,1,0:T(1,128)} %all_to_all.5.received_ref, f32[25,200]{1,0:T(8,128)} %constant.22.clone.table_ref, f32[4,200]{1,0:T(4,128)} %constant.23.clone.groups_ref), custom_call_target="tpu_custom_call" | custom-call | tf_op jit(solution)/shard_map/harmonic/pallas_call | solution.py:907
Async XLA Ops:
  3.0 6.7 %collective-permute-start = (f32[3,48,128]{2,1,0:T(8,128)}, f32[3,48,128]{2,1,0:T(8,128)S(1)}, u32[]{:S(2)}, u32[]{:S(2)}) collective-permute-start(f32[3,48,128]{2,1,0:T(8,128)} %get-tuple-element.21), channel_id=1, source_target_pairs={{16,0},{32,16},{48,32},{64,48},{80,64},{96,80},{112,96},{17,1},{33... | collective-permute-start | bytes 221192 | tf_op jit(solution)/shard_map/ppermute | solution.py:756
  6.3 4.8 %collective-permute-start.1 = (f32[3,48,128]{2,1,0:T(8,128)}, f32[3,48,128]{2,1,0:T(8,128)S(1)}, u32[]{:S(2)}, u32[]{:S(2)}) collective-permute-start(f32[3,48,128]{2,1,0:T(8,128)} %get-tuple-element.22), channel_id=1, source_target_pairs={{0,16},{16,32},{32,48},{48,64},{64,80},{80,96},{96,112},{1,17},{17... | collective-permute-start | bytes 221192 | tf_op jit(solution)/shard_map/ppermute | solution.py:757
  9.7 1.4 %copy-start = (f32[3,48,128]{2,1,0:T(8,128)}, f32[3,48,128]{2,1,0:T(8,128)S(1)}, u32[]{:S(2)}) copy-start(f32[3,48,128]{2,1,0:T(8,128)S(1)} %collective-permute-done.below_ref) | copy-start | bytes 221188
  11.1 0.6 copy-start.2
  13.4 37.1 %collective-permute-start.2 = (f32[3,48,128]{2,1,0:T(8,128)}, f32[3,48,128]{2,1,0:T(8,128)S(1)}, u32[]{:S(2)}, u32[]{:S(2)}) collective-permute-start(f32[3,48,128]{2,1,0:T(8,128)} %get-tuple-element.23), channel_id=1, source_target_pairs={{1,0},{2,1},{3,2},{4,3},{5,4},{6,5},{7,6},{8,7},{9,8},{10,9},{11,1... | collective-permute-start | bytes 221192 | tf_op jit(solution)/shard_map/ppermute | solution.py:764
  14.7 35.8 %collective-permute-start.3 = (f32[3,48,128]{2,1,0:T(8,128)}, f32[3,48,128]{2,1,0:T(8,128)S(1)}, u32[]{:S(2)}, u32[]{:S(2)}) collective-permute-start(f32[3,48,128]{2,1,0:T(8,128)} %get-tuple-element.24), channel_id=1, source_target_pairs={{0,1},{1,2},{2,3},{3,4},{4,5},{5,6},{6,7},{7,8},{8,9},{9,10},{10,1... | collective-permute-start | bytes 221192 | tf_op jit(solution)/shard_map/ppermute | solution.py:765
  19.3 31.2 %copy-start.1 = (f32[3,48,128]{2,1,0:T(8,128)S(1)}, f32[3,48,128]{2,1,0:T(8,128)}, u32[]{:S(2)}) copy-start(f32[3,48,128]{2,1,0:T(8,128)} %copy-done) | copy-start | bytes 221188
  19.3 31.2 %copy-start.3 = (f32[3,48,128]{2,1,0:T(8,128)S(1)}, f32[3,48,128]{2,1,0:T(8,128)}, u32[]{:S(2)}) copy-start(f32[3,48,128]{2,1,0:T(8,128)} %copy-done.2) | copy-start | bytes 221188

commit v5 on v4

--- a/solution.py
+++ b/solution.py
@@ -15,6 +15,7 @@
 FACE_ROWS = 16
 ROWS = 144
 LANES = 128
+FACE_TILES = 4
 
 
 highest = lax.Precision.HIGHEST
@@ -188,7 +189,7 @@
     lift_hi = lift.astype(jnp.bfloat16)
     lift_lo = (lift - lift_hi.astype(np.float32)).astype(jnp.bfloat16)
     return {
-        "table_select": jnp.asarray(table_select, bf16),
+        "table_select": jnp.asarray(np.concatenate([table_select] * 2, axis=0), bf16),
         "trace_select": jnp.asarray(trace_select, bf16),
         "twice_select": jnp.asarray(np.concatenate([trace_select] * 2, axis=1), bf16),
         "from_p": jnp.asarray(np.concatenate([from_p, from_p], axis=1), bf16),
@@ -267,7 +268,7 @@
     codes = jnp.where((codes >= 0) & (codes < slot_faces), codes, 0)
     for face in range(4):
         for tile in range(tiles):
-            row = face * tiles + tile
+            row = 4 * FACE_TILES * (tile // FACE_TILES) + FACE_TILES * face + tile % FACE_TILES
             faces_ref[row : row + 1, :] = codes[
                 face : face + 1, LANES * tile : LANES * tile + LANES
             ]
@@ -286,23 +287,25 @@
     slot_count = table_ref.shape[0] // 4
     width = LANES * stacked.shape[0]
     high, low = stack_nodes(fields_ref.at[:, :, width * part : width * part + width], stacked)
+    both = jnp.concatenate([high, low], axis=0)
     for half in range(2):
         select = select_ref[:, 256 * half : 256 * half + 256]
-        rows = product(high, select, ((0,), (0,))) + product(low, select, ((0,), (0,)))
+        rows = product(both, select, ((0,), (0,)))
         for side in range(2):
             start = pl.multiple_of((2 * half + side) * slot_count + first + width * part, width)
             table_ref[pl.ds(start, width), :] = rows[:, LANES * side : LANES * side + LANES]
 
 
-def gather_pieces(slot_count, first, faces_ref, table_ref, normals_ref, outer_ref, rows_refs):
+def gather_pieces(faces_ref, table_ref, normals_ref, outer_ref, rows_refs):
     width = outer_ref.shape[1]
     left_half = lax.broadcasted_iota(jnp.int32, (1, LANES), 1) < 64
 
-    def load(lists, tile, rows):
+    def load(tile, rows):
         for row in rows:
+            at = tile * LANES + row
             for half in range(2):
-                one = table_ref[pl.ds(lists[2 * half][row], 1), :]
-                two = table_ref[pl.ds(lists[2 * half + 1][row], 1), :]
+                one = table_ref[pl.ds(faces_ref[2 * half * width + at], 1), :]
+                two = table_ref[pl.ds(faces_ref[(2 * half + 1) * width + at], 1), :]
                 rows_ref = rows_refs[2 * (tile % 2) + half]
                 rows_ref[row : row + 1, :] = jnp.where(left_half, one, two)
 
@@ -319,11 +322,9 @@
             outer_ref[FACE_ROWS * face : FACE_ROWS * face + FACE_ROWS, lanes] = total
 
     for tile in range(width // LANES):
-        base = first + tile * LANES
-        lists = [faces_ref.at[pl.ds(base + face * slot_count, LANES)] for face in range(4)]
         for part in range(8):
             rows = range(16 * part, 16 * part + 16)
-            yield functools.partial(load, lists, tile, rows)
+            yield functools.partial(load, tile, rows)
             if tile > 0 and part < 2:
                 yield functools.partial(combine, tile - 1, part)
     for half in range(2):
@@ -333,8 +334,8 @@
 def section_kernel(
     slot_count,
     reach,
-    faces_ref,
     live_ref,
+    faces_hbm,
     next_normals_ref,
     bulk_ref,
     fields_ref,
@@ -363,8 +364,12 @@
     slow_split,
     inner,
     sources,
+    even_faces,
+    odd_faces,
+    arrived,
     *rows_refs,
 ):
+    faces_refs = (even_faces, odd_faces)
     width = fields_ref.shape[2]
     tiles = slot_count // width
     bulks = slot_count // bulk_ref.shape[2]
@@ -372,11 +377,21 @@
     slot_faces = 4 * slot_count
     half_width = 256
 
-    def gather():
-        first = step * width
+    def codes_copy(tile, parity):
+        source = faces_hbm.at[pl.ds(pl.multiple_of(tile * 4 * width, 4 * width), 4 * width)]
+        return pltpu.make_async_copy(source, faces_refs[parity], arrived.at[parity])
+
+    def gather(parity):
         return gather_pieces(
-            slot_count, first, faces_ref, table_ref, next_normals_ref, outer, rows_refs
+            faces_refs[parity], table_ref, next_normals_ref, outer, rows_refs
         )
+
+    def take_codes(parity):
+        codes_copy(step, parity).wait()
+
+        @pl.when(step < tiles - 1)
+        def _():
+            codes_copy(step + 1, 1 - parity).start()
 
     def update_pieces():
         first = (step - 1) * width
@@ -517,7 +532,7 @@
     def interleave(gathers, groups):
         gathers = list(gathers)
 
-        def run(at, updates):
+        def run(at, updates, groups):
             @pl.when(live_ref[0] > at)
             def _():
                 low = at * len(gathers) // len(groups)
@@ -526,8 +541,10 @@
                     for piece in loads[place : place + 1] + updates[place : place + 1]:
                         piece()
 
+        cuts = (0, 4, 8)
+        groups = [sum(groups[low:high], []) for low, high in zip(cuts, cuts[1:])]
         for at, updates in enumerate(groups):
-            run(at, updates)
+            run(at, updates, groups)
 
     @pl.when(step == -bulks)
     def _():
@@ -543,15 +560,23 @@
         for part in range(bulk_ref.shape[2] // width):
             build_rows(first, part, bulk_ref, table_select_ref, table_ref, stacked)
 
+    @pl.when(step == -1)
+    def _():
+        codes_copy(0, 0).start()
+
     @pl.when(step == 0)
     def _():
-        for piece in gather():
+        take_codes(0)
+        for piece in gather(0):
             piece()
 
-    @pl.when((step > 0) & (step < tiles))
-    def _():
-        beyond_ref[...] = outer[...]
-        interleave(gather(), update_pieces())
+    for parity in range(2):
+
+        @pl.when((step > 0) & (step < tiles) & (step % 2 == parity))
+        def _():
+            take_codes(parity)
+            beyond_ref[...] = outer[...]
+            interleave(gather(parity), update_pieces())
 
     @pl.when(step == tiles)
     def _():
@@ -716,7 +741,7 @@
     shape = jax.ShapeDtypeStruct
 
     elems = in_hbm(sample_elems.reshape(1, samples))
-    width = 512
+    width = LANES * FACE_TILES
     tiles = slot_count // width
     piece = (3, 48, LANES)
 
@@ -776,9 +801,10 @@
     fields_next, residue_next, partial = pl.pallas_call(
         functools.partial(section_kernel, slot_count, reach),
         grid_spec=pltpu.PrefetchScalarGridSpec(
-            num_scalar_prefetch=2,
+            num_scalar_prefetch=1,
             grid=(bulks + tiles + 1,),
             in_specs=[
+                pl.BlockSpec(memory_space=pltpu.HBM),
                 pl.BlockSpec((3, 4, width), ahead(2)),
                 pl.BlockSpec((NODES, 4, bulk), lambda t, *_: (0, 0, jnp.minimum(t, bulks - 1))),
                 pl.BlockSpec((NODES, 4, width), behind(2)),
@@ -788,7 +814,7 @@
                 pl.BlockSpec((4, width), behind(1)),
                 pl.BlockSpec((4, width), behind(1)),
                 fixed((1, samples)),
-                fixed((ROWS, 4 * LANES)),
+                fixed((2 * ROWS, 4 * LANES)),
                 fixed((256, 2 * ROWS)),
                 fixed((3 * ROWS, 96)),
                 fixed((ROWS, 1024)),
@@ -811,6 +837,9 @@
                 pltpu.VMEM((width // 256, 96, 256), bf16),
                 pltpu.VMEM((width // 256, 256, 256), f32),
                 pltpu.VMEM((width // 256, 1024, 256), bf16),
+                pltpu.SMEM((4 * width,), jnp.int32),
+                pltpu.SMEM((4 * width,), jnp.int32),
+                pltpu.SemaphoreType.DMA((2,)),
                 *[pltpu.VMEM((LANES, LANES), f32)] * 4,
             ],
         ),
@@ -822,8 +851,8 @@
         compiler_params=pltpu.CompilerParams(vmem_limit_bytes=48 << 20),
         name="section",
     )(
-        faces.reshape(-1),
         live_counts,
+        in_hbm(faces.reshape(-1)),
         normals,
         fields,
         fields,

time: 79.5 us -> 78.5 us (0.987)
  Pallas kernels: 39.9 us -> 38.2 us
    pallas_call x1, Pallas kernels: 31.1 us -> 29.4 us  [local(): pl.pallas_call(functools.partial(section_kernel, slot_count, reach), grid...]
  transfers between devices with their start and end apart: 4 -> 4, of which waited for: 2 -> 2; matrix products, arithmetic and copies ran while one was open for 0% -> 0% of each run, Pallas kernels for 39% -> 38%
where the time goes in v5:
time: 78.5 us; the launch traced here: 78.1 us
  Pallas kernels  38.2 us (49%)
  blocking collectives  23.9 us (30%)
  starting transfers between devices  11.7 us (15%)
  waiting for transfers between devices  1.71 us (2%)
  between operations  1.37 us (2%)
  local copies, waits for them, and re-layouts  1.26 us (2%)
    pallas_call x1, Pallas kernels, local(): pl.pallas_call(functools.partial(section_kernel, slot_count, reach), grid...  29.4 us
    all_to_all x1, blocking collectives, local(): received = lax.all_to_all(spread, ('px', 'py'), 0, 0, tiled=True)  23.9 us
    ppermute x1, starting transfers between devices, local(): from_left = lax.ppermute(to_right, 'py', forward)  3.99 us
    ppermute x1, starting transfers between devices, local(): below = lax.ppermute(up, 'px', backward)  3.32 us
    ppermute x1, starting transfers between devices, local(): above = lax.ppermute(down, 'px', forward)  3.1 us
    pallas_call x1, Pallas kernels, local(): pl.pallas_call(functools.partial(boundary_kernel, slot_faces, const['powe...  2.98 us
    pallas_call x1, Pallas kernels, local(): pl.pallas_call(functools.partial(pack_kernel, slot_faces), grid=(1,), in_...  2.34 us
    pallas_call x1, Pallas kernels, local(): pl.pallas_call(harmonic_kernel, out_shape=shape((receivers, harmonic.shap...  1.79 us
  transfers between devices with their start and end apart: 4, of which 2 were waited for; matrix products, arithmetic and copies ran while one was open for 0% of the time, Pallas kernels for 38%

profile of v5, /device:TPU:1, one launch (start us, length us, event | category | flops | bytes accessed | tf_op | source)
XLA Modules:
  0.0 78.1 jit_solution(2740326001276781488)
XLA Ops:
  0.6 2.3 %pack.1 = (f32[3,48,128]{2,1,0:T(8,128)}, f32[3,48,128]{2,1,0:T(8,128)}, f32[48,128]{1,0:T(8,128)}, f32[48,128]{1,0:T(8,128)}, s32[144,128]{1,0:T(8,128)S(1)}) custom-call(f32[35,4,4608]{2,1,0:T(4,128)} %bitcast.9, s32[4,4608]{1,0:T(4,128)} %codes_ref.5, bf16[256,144]{1,0:T(8,128)(2,1)} %constant.17.clone.select_ref), custom_call_target="tpu_custom_call" | custom-call | tf_op jit(solution)/shard_map/pack/pallas_call | solution.py:748
  3.0 0.0 copy-start.4
  3.0 0.6 copy-done.4
  3.6 3.3 %collective-permute-start = (f32[3,48,128]{2,1,0:T(8,128)}, f32[3,48,128]{2,1,0:T(8,128)S(1)}, u32[]{:S(2)}, u32[]{:S(2)}) collective-permute-start(f32[3,48,128]{2,1,0:T(8,128)} %get-tuple-element.21), channel_id=1, source_target_pairs={{16,0},{32,16},{48,32},{64,48},{80,64},{96,80},{112,96},{17,1},{33... | collective-permute-start | bytes 221192 | tf_op jit(solution)/shard_map/ppermute | solution.py:781
  6.9 3.1 %collective-permute-start.1 = (f32[3,48,128]{2,1,0:T(8,128)}, f32[3,48,128]{2,1,0:T(8,128)S(1)}, u32[]{:S(2)}, u32[]{:S(2)}) collective-permute-start(f32[3,48,128]{2,1,0:T(8,128)} %get-tuple-element.22), channel_id=1, source_target_pairs={{0,16},{16,32},{32,48},{48,64},{64,80},{80,96},{96,112},{1,17},{17... | collective-permute-start | bytes 221192 | tf_op jit(solution)/shard_map/ppermute | solution.py:782
  10.0 0.3 collective-permute-done.below_ref
  10.3 0.0 copy-start
  10.3 1.4 %collective-permute-done.1.above_ref = f32[3,48,128]{2,1,0:T(8,128)S(1)} collective-permute-done((f32[3,48,128]{2,1,0:T(8,128)}, f32[3,48,128]{2,1,0:T(8,128)S(1)}, u32[]{:S(2)}, u32[]{:S(2)}) %collective-permute-start.1) | collective-permute-done | bytes 73760 | tf_op jit(solution)/shard_map/ppermute | solution.py:782
  11.7 0.0 copy-start.2
  11.7 0.0 copy-done
  11.7 0.6 copy-done.2
  12.4 1.6 %relay.1 = (f32[3,48,128]{2,1,0:T(8,128)}, f32[3,48,128]{2,1,0:T(8,128)}) custom-call(f32[48,128]{1,0:T(8,128)} %get-tuple-element.19.left_ref, f32[48,128]{1,0:T(8,128)} %get-tuple-element.20.right_ref, f32[3,48,128]{2,1,0:T(8,128)} %copy-done, f32[3,48,128]{2,1,0:T(8,128)} %copy-done.2), custom_call_target="tpu_custom_call" | custom-call | tf_op jit(solution)/shard_map/relay/pallas_call | solution.py:783
  14.0 1.3 %collective-permute-start.2 = (f32[3,48,128]{2,1,0:T(8,128)}, f32[3,48,128]{2,1,0:T(8,128)S(1)}, u32[]{:S(2)}, u32[]{:S(2)}) collective-permute-start(f32[3,48,128]{2,1,0:T(8,128)} %get-tuple-element.23), channel_id=1, source_target_pairs={{1,0},{2,1},{3,2},{4,3},{5,4},{6,5},{7,6},{8,7},{9,8},{10,9},{11,1... | collective-permute-start | bytes 221192 | tf_op jit(solution)/shard_map/ppermute | solution.py:789
  15.3 4.0 %collective-permute-start.3 = (f32[3,48,128]{2,1,0:T(8,128)}, f32[3,48,128]{2,1,0:T(8,128)S(1)}, u32[]{:S(2)}, u32[]{:S(2)}) collective-permute-start(f32[3,48,128]{2,1,0:T(8,128)} %get-tuple-element.24), channel_id=1, source_target_pairs={{0,1},{1,2},{2,3},{3,4},{4,5},{5,6},{6,7},{7,8},{8,9},{9,10},{10,1... | collective-permute-start | bytes 221192 | tf_op jit(solution)/shard_map/ppermute | solution.py:790
  19.9 0.0 copy-start.1
  19.9 0.0 copy-start.3
  19.9 29.4 %section.1 = (f32[35,4,4608]{2,1,0:T(4,128)}, f32[35,4,4608]{2,1,0:T(4,128)}, f32[144,200]{1,0:T(8,128)S(1)}) custom-call(s32[1]{0:T(128)S(6)} %copy.25.live_ref, s32[18432]{0:T(1024)} %bitcast.8, f32[3,4,4608]{2,1,0:T(4,128)} %normals_ref.3, f32[35,4,4608]{2,1,0:T(4,128)} %bitcast.10, f32[35,4,4608]{2,1,0:T(4,128)} %bitcast.11, f32[35,4,4608]{2,1,0:T(4,128)} %bitcast.14, ...), custom_call_target="tpu_custom_call" | custom-call | tf_op jit(solution)/shard_map/section/pallas_call | solution.py:801
  49.4 0.0 collective-permute-done.2.right_ref
  49.4 0.0 collective-permute-done.3.left_ref
  49.4 0.0 copy-done.1
  49.4 0.0 copy-done.3
  49.4 3.0 %boundary.1 = (f32[35,4,4608]{2,1,0:T(4,128)}, f32[35,4,4608]{2,1,0:T(4,128)}, f32[128,1,200]{2,1,0:T(1,128)S(1)}) custom-call(f32[35,4,4608]{2,1,0:T(4,128)} %get-tuple-element.17.fields_ref, f32[35,4,4608]{2,1,0:T(4,128)} %get-tuple-element.18.residue_ref, f32[3,4,4608]{2,1,0:T(4,128)} %normals_ref.3, ...), custom_call_target="tpu_custom_call", output_to_operand_aliasing={{0}: (0, {}), {1}: (1, {})} | custom-call | tf_op jit(solution)/shard_map/boundary/pallas_call | solution.py:874
  52.4 23.9 %all_to_all.5.received_ref = f32[128,1,200]{2,1,0:T(1,128)} all-to-all(f32[128,1,200]{2,1,0:T(1,128)S(1)} %get-tuple-element.28), channel_id=1, replica_groups=mesh['px'=8,'py'=16] {'px','py'}, dimensions={0} | all-to-all | bytes 204800 | tf_op jit(solution)/shard_map/all_to_all | solution.py:931
  76.3 1.8 %harmonic.1 = f32[4,25]{1,0:T(4,128)} custom-call(f32[128,1,200]{2,1,0:T(1,128)} %all_to_all.5.received_ref, f32[25,200]{1,0:T(8,128)} %constant.22.clone.table_ref, f32[4,200]{1,0:T(4,128)} %constant.23.clone.groups_ref), custom_call_target="tpu_custom_call" | custom-call | tf_op jit(solution)/shard_map/harmonic/pallas_call | solution.py:936
Async XLA Ops:
  3.0 0.6 copy-start.4
  3.6 6.7 %collective-permute-start = (f32[3,48,128]{2,1,0:T(8,128)}, f32[3,48,128]{2,1,0:T(8,128)S(1)}, u32[]{:S(2)}, u32[]{:S(2)}) collective-permute-start(f32[3,48,128]{2,1,0:T(8,128)} %get-tuple-element.21), channel_id=1, source_target_pairs={{16,0},{32,16},{48,32},{64,48},{80,64},{96,80},{112,96},{17,1},{33... | collective-permute-start | bytes 221192 | tf_op jit(solution)/shard_map/ppermute | solution.py:781
  6.9 4.8 %collective-permute-start.1 = (f32[3,48,128]{2,1,0:T(8,128)}, f32[3,48,128]{2,1,0:T(8,128)S(1)}, u32[]{:S(2)}, u32[]{:S(2)}) collective-permute-start(f32[3,48,128]{2,1,0:T(8,128)} %get-tuple-element.22), channel_id=1, source_target_pairs={{0,16},{16,32},{32,48},{48,64},{64,80},{80,96},{96,112},{1,17},{17... | collective-permute-start | bytes 221192 | tf_op jit(solution)/shard_map/ppermute | solution.py:782
  10.3 1.4 %copy-start = (f32[3,48,128]{2,1,0:T(8,128)}, f32[3,48,128]{2,1,0:T(8,128)S(1)}, u32[]{:S(2)}) copy-start(f32[3,48,128]{2,1,0:T(8,128)S(1)} %collective-permute-done.below_ref) | copy-start | bytes 221188
  11.7 0.6 copy-start.2
  14.0 35.4 %collective-permute-start.2 = (f32[3,48,128]{2,1,0:T(8,128)}, f32[3,48,128]{2,1,0:T(8,128)S(1)}, u32[]{:S(2)}, u32[]{:S(2)}) collective-permute-start(f32[3,48,128]{2,1,0:T(8,128)} %get-tuple-element.23), channel_id=1, source_target_pairs={{1,0},{2,1},{3,2},{4,3},{5,4},{6,5},{7,6},{8,7},{9,8},{10,9},{11,1... | collective-permute-start | bytes 221192 | tf_op jit(solution)/shard_map/ppermute | solution.py:789
  15.3 34.1 %collective-permute-start.3 = (f32[3,48,128]{2,1,0:T(8,128)}, f32[3,48,128]{2,1,0:T(8,128)S(1)}, u32[]{:S(2)}, u32[]{:S(2)}) collective-permute-start(f32[3,48,128]{2,1,0:T(8,128)} %get-tuple-element.24), channel_id=1, source_target_pairs={{0,1},{1,2},{2,3},{3,4},{4,5},{5,6},{6,7},{7,8},{8,9},{9,10},{10,1... | collective-permute-start | bytes 221192 | tf_op jit(solution)/shard_map/ppermute | solution.py:790
  19.9 29.5 %copy-start.1 = (f32[3,48,128]{2,1,0:T(8,128)S(1)}, f32[3,48,128]{2,1,0:T(8,128)}, u32[]{:S(2)}) copy-start(f32[3,48,128]{2,1,0:T(8,128)} %copy-done) | copy-start | bytes 221188
  19.9 29.5 %copy-start.3 = (f32[3,48,128]{2,1,0:T(8,128)S(1)}, f32[3,48,128]{2,1,0:T(8,128)}, u32[]{:S(2)}) copy-start(f32[3,48,128]{2,1,0:T(8,128)} %copy-done.2) | copy-start | bytes 221188

commit v6 on v5

--- a/solution.py
+++ b/solution.py
@@ -389,7 +389,7 @@
     def take_codes(parity):
         codes_copy(step, parity).wait()
 
-        @pl.when(step < tiles - 1)
+        @pl.when((step + 1) * width < live_ref[0])
         def _():
             codes_copy(step + 1, 1 - parity).start()
 
@@ -558,7 +558,10 @@
     def _():
         first = (step + bulks) * bulk_ref.shape[2]
         for part in range(bulk_ref.shape[2] // width):
-            build_rows(first, part, bulk_ref, table_select_ref, table_ref, stacked)
+
+            @pl.when(first + width * part < live_ref[0])
+            def _():
+                build_rows(first, part, bulk_ref, table_select_ref, table_ref, stacked)
 
     @pl.when(step == -1)
     def _():
@@ -572,13 +575,18 @@
 
     for parity in range(2):
 
-        @pl.when((step > 0) & (step < tiles) & (step % 2 == parity))
+        @pl.when((step > 0) & (step * width < live_ref[0]) & (step % 2 == parity))
         def _():
             take_codes(parity)
             beyond_ref[...] = outer[...]
             interleave(gather(parity), update_pieces())
 
-    @pl.when(step == tiles)
+    @pl.when((step > 0) & ((step - 1) * width >= live_ref[0]))
+    def _():
+        fields_out[...] = jnp.zeros_like(fields_out)
+        residue_out[...] = jnp.zeros_like(residue_out)
+
+    @pl.when((step > 0) & ((step - 1) * width < live_ref[0]) & (step * width >= live_ref[0]))
     def _():
         beyond_ref[...] = outer[...]
         for stage in update_pieces():
@@ -707,6 +715,10 @@
     return pltpu.with_memory_space_constraint(array, pltpu.HBM)
 
 
+def in_vmem(array):
+    return pltpu.with_memory_space_constraint(array, pltpu.VMEM)
+
+
 def fixed(shape):
     return pl.BlockSpec(shape, lambda *_: (0,) * len(shape))
 
@@ -765,7 +777,7 @@
             pltpu.HBM(piece, f32),
             pltpu.HBM(piece[1:], f32),
             pltpu.HBM(piece[1:], f32),
-            shape((slot_faces // LANES, LANES), jnp.int32),
+            pltpu.HBM((slot_faces // LANES, LANES), jnp.int32),
         ],
         scratch_shapes=[pltpu.VMEM((reach // LANES, ROWS, LANES), f32)],
         compiler_params=pltpu.CompilerParams(vmem_limit_bytes=16 << 20),
@@ -784,7 +796,7 @@
         relay_kernel,
         out_shape=[pltpu.HBM(piece, f32), pltpu.HBM(piece, f32)],
         name="relay",
-    )(left, right, below, above)
+    )(left, right, in_vmem(below), in_vmem(above))
     forward, backward = steps_along("py")
     from_right = lax.ppermute(to_left, "py", backward)
     from_left = lax.ppermute(to_right, "py", forward)

time: 78.5 us -> 72.2 us (0.920)
  Pallas kernels: 38.2 us -> 24.9 us
  blocking collectives: 23.9 us -> 31.5 us
  local copies, waits for them, and re-layouts: 1.26 us -> 0 us
    pallas_call x1, Pallas kernels: 29.4 us -> 16.4 us  [local(): pl.pallas_call(functools.partial(section_kernel, slot_count, reach), grid...]
    all_to_all x1, blocking collectives: 23.9 us -> 31.5 us  [local(): received = lax.all_to_all(spread, ('px', 'py'), 0, 0, tiled=True)]
    unnamed x10 -> x0, local copies, waits for them, and re-layouts: 1.26 us -> none
  transfers between devices with their start and end apart: 4 -> 4, of which waited for: 2 -> 2; matrix products, arithmetic and copies ran while one was open for 0% -> 0% of each run, Pallas kernels for 38% -> 23%
where the time goes in v6:
time: 72.2 us; the launch traced here: 71.2 us
  blocking collectives  31.5 us (44%)
  Pallas kernels  24.9 us (34%)
  starting transfers between devices  11.7 us (16%)
  waiting for transfers between devices  1.71 us (2%)
  between operations  1.33 us (2%)
    all_to_all x1, blocking collectives, local(): received = lax.all_to_all(spread, ('px', 'py'), 0, 0, tiled=True)  31.5 us
    pallas_call x1, Pallas kernels, local(): pl.pallas_call(functools.partial(section_kernel, slot_count, reach), grid...  16.4 us
    ppermute x1, starting transfers between devices, local(): from_left = lax.ppermute(to_right, 'py', forward)  3.99 us
    ppermute x1, starting transfers between devices, local(): below = lax.ppermute(up, 'px', backward)  3.32 us
    ppermute x1, starting transfers between devices, local(): above = lax.ppermute(down, 'px', forward)  3.1 us
    pallas_call x1, Pallas kernels, local(): pl.pallas_call(functools.partial(boundary_kernel, slot_faces, const['powe...  2.98 us
    pallas_call x1, Pallas kernels, local(): pl.pallas_call(functools.partial(pack_kernel, slot_faces), grid=(1,), in_...  2.33 us
    pallas_call x1, Pallas kernels, local(): pl.pallas_call(harmonic_kernel, out_shape=shape((receivers, harmonic.shap...  1.79 us
  transfers between devices with their start and end apart: 4, of which 2 were waited for; matrix products, arithmetic and copies ran while one was open for 0% of the time, Pallas kernels for 23%

profile of v6, /device:TPU:1, one launch (start us, length us, event | category | flops | bytes accessed | tf_op | source)
XLA Modules:
  0.0 71.2 jit_solution(7309239902531656583)
XLA Ops:
  0.6 2.3 %pack.1 = (f32[3,48,128]{2,1,0:T(8,128)}, f32[3,48,128]{2,1,0:T(8,128)}, f32[48,128]{1,0:T(8,128)}, f32[48,128]{1,0:T(8,128)}, s32[144,128]{1,0:T(8,128)}) custom-call(f32[35,4,4608]{2,1,0:T(4,128)} %bitcast.8, s32[4,4608]{1,0:T(4,128)} %codes_ref.5, bf16[256,144]{1,0:T(8,128)(2,1)} %constant.17.clone.select_ref), custom_call_target="tpu_custom_call" | custom-call | tf_op jit(solution)/shard_map/pack/pallas_call | solution.py:760
  3.0 3.3 %collective-permute-start = (f32[3,48,128]{2,1,0:T(8,128)}, f32[3,48,128]{2,1,0:T(8,128)S(1)}, u32[]{:S(2)}, u32[]{:S(2)}) collective-permute-start(f32[3,48,128]{2,1,0:T(8,128)} %get-tuple-element.21), channel_id=1, source_target_pairs={{16,0},{32,16},{48,32},{64,48},{80,64},{96,80},{112,96},{17,1},{33... | collective-permute-start | bytes 221192 | tf_op jit(solution)/shard_map/ppermute | solution.py:793
  6.3 3.1 %collective-permute-start.1 = (f32[3,48,128]{2,1,0:T(8,128)}, f32[3,48,128]{2,1,0:T(8,128)S(1)}, u32[]{:S(2)}, u32[]{:S(2)}) collective-permute-start(f32[3,48,128]{2,1,0:T(8,128)} %get-tuple-element.22), channel_id=1, source_target_pairs={{0,16},{16,32},{32,48},{48,64},{64,80},{80,96},{96,112},{1,17},{17... | collective-permute-start | bytes 221192 | tf_op jit(solution)/shard_map/ppermute | solution.py:794
  9.4 0.3 collective-permute-done.below_ref
  9.7 1.4 %collective-permute-done.1.above_ref = f32[3,48,128]{2,1,0:T(8,128)S(1)} collective-permute-done((f32[3,48,128]{2,1,0:T(8,128)}, f32[3,48,128]{2,1,0:T(8,128)S(1)}, u32[]{:S(2)}, u32[]{:S(2)}) %collective-permute-start.1) | collective-permute-done | bytes 73760 | tf_op jit(solution)/shard_map/ppermute | solution.py:794
  11.1 1.4 %relay.1 = (f32[3,48,128]{2,1,0:T(8,128)}, f32[3,48,128]{2,1,0:T(8,128)}) custom-call(f32[48,128]{1,0:T(8,128)} %get-tuple-element.19.left_ref, f32[48,128]{1,0:T(8,128)} %get-tuple-element.20.right_ref, f32[3,48,128]{2,1,0:T(8,128)S(1)} %collective-permute-done.below_ref, f32[3,48,128]{2,1,0:T(8,128)S(1)} %collective-permute-done.1.above_ref), custom_call_target="tpu_custom_call" | custom-call | tf_op jit(solution)/shard_map/relay/pallas_call | solution.py:795
  12.5 1.3 %collective-permute-start.2 = (f32[3,48,128]{2,1,0:T(8,128)}, f32[3,48,128]{2,1,0:T(8,128)S(1)}, u32[]{:S(2)}, u32[]{:S(2)}) collective-permute-start(f32[3,48,128]{2,1,0:T(8,128)} %get-tuple-element.23), channel_id=1, source_target_pairs={{1,0},{2,1},{3,2},{4,3},{5,4},{6,5},{7,6},{8,7},{9,8},{10,9},{11,1... | collective-permute-start | bytes 221192 | tf_op jit(solution)/shard_map/ppermute | solution.py:801
  13.8 4.0 %collective-permute-start.3 = (f32[3,48,128]{2,1,0:T(8,128)}, f32[3,48,128]{2,1,0:T(8,128)S(1)}, u32[]{:S(2)}, u32[]{:S(2)}) collective-permute-start(f32[3,48,128]{2,1,0:T(8,128)} %get-tuple-element.24), channel_id=1, source_target_pairs={{0,1},{1,2},{2,3},{3,4},{4,5},{5,6},{6,7},{7,8},{8,9},{9,10},{10,1... | collective-permute-start | bytes 221192 | tf_op jit(solution)/shard_map/ppermute | solution.py:802
  18.4 16.4 %section.1 = (f32[35,4,4608]{2,1,0:T(4,128)}, f32[35,4,4608]{2,1,0:T(4,128)}, f32[144,200]{1,0:T(8,128)S(1)}) custom-call(s32[1]{0:T(128)S(6)} %copy.25.live_ref, s32[18432]{0:T(1024)} %bitcast.14, f32[3,4,4608]{2,1,0:T(4,128)} %normals_ref.3, f32[35,4,4608]{2,1,0:T(4,128)} %bitcast.9, f32[35,4,4608]{2,1,0:T(4,128)} %bitcast.10, f32[35,4,4608]{2,1,0:T(4,128)} %bitcast.13, ...), custom_call_target="tpu_custom_call" | custom-call | tf_op jit(solution)/shard_map/section/pallas_call | solution.py:813
  34.9 0.0 collective-permute-done.2.right_ref
  34.9 0.0 collective-permute-done.3.left_ref
  34.9 3.0 %boundary.1 = (f32[35,4,4608]{2,1,0:T(4,128)}, f32[35,4,4608]{2,1,0:T(4,128)}, f32[128,1,200]{2,1,0:T(1,128)S(1)}) custom-call(f32[35,4,4608]{2,1,0:T(4,128)} %get-tuple-element.17.fields_ref, f32[35,4,4608]{2,1,0:T(4,128)} %get-tuple-element.18.residue_ref, f32[3,4,4608]{2,1,0:T(4,128)} %normals_ref.3, ...), custom_call_target="tpu_custom_call", output_to_operand_aliasing={{0}: (0, {}), {1}: (1, {})} | custom-call | tf_op jit(solution)/shard_map/boundary/pallas_call | solution.py:886
  37.9 31.5 %all_to_all.5.received_ref = f32[128,1,200]{2,1,0:T(1,128)} all-to-all(f32[128,1,200]{2,1,0:T(1,128)S(1)} %get-tuple-element.28), channel_id=1, replica_groups=mesh['px'=8,'py'=16] {'px','py'}, dimensions={0} | all-to-all | bytes 204800 | tf_op jit(solution)/shard_map/all_to_all | solution.py:943
  69.4 1.8 %harmonic.1 = f32[4,25]{1,0:T(4,128)} custom-call(f32[128,1,200]{2,1,0:T(1,128)} %all_to_all.5.received_ref, f32[25,200]{1,0:T(8,128)} %constant.22.clone.table_ref, f32[4,200]{1,0:T(4,128)} %constant.23.clone.groups_ref), custom_call_target="tpu_custom_call" | custom-call | tf_op jit(solution)/shard_map/harmonic/pallas_call | solution.py:948
Async XLA Ops:
  3.0 6.7 %collective-permute-start = (f32[3,48,128]{2,1,0:T(8,128)}, f32[3,48,128]{2,1,0:T(8,128)S(1)}, u32[]{:S(2)}, u32[]{:S(2)}) collective-permute-start(f32[3,48,128]{2,1,0:T(8,128)} %get-tuple-element.21), channel_id=1, source_target_pairs={{16,0},{32,16},{48,32},{64,48},{80,64},{96,80},{112,96},{17,1},{33... | collective-permute-start | bytes 221192 | tf_op jit(solution)/shard_map/ppermute | solution.py:793
  6.3 4.8 %collective-permute-start.1 = (f32[3,48,128]{2,1,0:T(8,128)}, f32[3,48,128]{2,1,0:T(8,128)S(1)}, u32[]{:S(2)}, u32[]{:S(2)}) collective-permute-start(f32[3,48,128]{2,1,0:T(8,128)} %get-tuple-element.22), channel_id=1, source_target_pairs={{0,16},{16,32},{32,48},{48,64},{64,80},{80,96},{96,112},{1,17},{17... | collective-permute-start | bytes 221192 | tf_op jit(solution)/shard_map/ppermute | solution.py:794
  12.5 22.4 %collective-permute-start.2 = (f32[3,48,128]{2,1,0:T(8,128)}, f32[3,48,128]{2,1,0:T(8,128)S(1)}, u32[]{:S(2)}, u32[]{:S(2)}) collective-permute-start(f32[3,48,128]{2,1,0:T(8,128)} %get-tuple-element.23), channel_id=1, source_target_pairs={{1,0},{2,1},{3,2},{4,3},{5,4},{6,5},{7,6},{8,7},{9,8},{10,9},{11,1... | collective-permute-start | bytes 221192 | tf_op jit(solution)/shard_map/ppermute | solution.py:801
  13.8 21.1 %collective-permute-start.3 = (f32[3,48,128]{2,1,0:T(8,128)}, f32[3,48,128]{2,1,0:T(8,128)S(1)}, u32[]{:S(2)}, u32[]{:S(2)}) collective-permute-start(f32[3,48,128]{2,1,0:T(8,128)} %get-tuple-element.24), channel_id=1, source_target_pairs={{0,1},{1,2},{2,3},{3,4},{4,5},{5,6},{6,7},{7,8},{8,9},{9,10},{10,1... | collective-permute-start | bytes 221192 | tf_op jit(solution)/shard_map/ppermute | solution.py:802
